TPU v7x, 32 devices: a whole 2x2x4 slice. The times are simulated.
32 devices in a mesh: dp: 8 (over z, x), seq: 4 (over y, core).
Axes of the slice: x: 2, y: 2, z: 4, core: 2. Of those that a mesh axis runs over, the one named last changes fastest.
Arguments:
- hidden_states: bfloat16 [32, 512, 768], P('dp', 'seq'), may hold values from -6 to 6
- lengths: int32 [32], P('dp'), may hold values from 20 to 512, as said below
- query_weight: bfloat16 [768, 768], replicated, may hold values from -0.21875 to 0.21875
- query_bias: float32 [768], replicated, may hold values from -3 to 3
- key_weight: bfloat16 [768, 768], replicated, may hold values from -0.21875 to 0.21875
- value_weight: bfloat16 [768, 768], replicated, may hold values from -0.21875 to 0.21875
- value_bias: float32 [768], replicated, may hold values from -3 to 3
- out_weight: bfloat16 [768, 768], replicated, may hold values from -1.75 to 1.75
- out_bias: float32 [768], replicated, may hold values from -2 to 2
- attn_gain: float32 [768], replicated, may hold values from 0.5 to 1.5
- attn_shift: float32 [768], replicated, may hold values from -2 to 2
- inner_weight: bfloat16 [768, 3072], replicated, may hold values from -0.21875 to 0.21875
- inner_bias: float32 [3072], replicated, may hold values from -3 to 3
- outer_weight: bfloat16 [3072, 768], replicated, may hold values from -0.109375 to 0.109375
- outer_bias: float32 [768], replicated, may hold values from -2 to 2
- ffn_gain: float32 [768], replicated, may hold values from 0.5 to 1.5
- ffn_shift: float32 [768], replicated, may hold values from -2 to 2
- cotangent: bfloat16 [32, 512, 768], P('dp', 'seq'), may hold values from -6 to 6
Outputs:
- block_output: bfloat16 [32, 512, 768], P('dp', 'seq')
- input_grad: bfloat16 [32, 512, 768], P('dp', 'seq')
- query_grad: float32 [768, 768], P('dp')
- qbias_grad: float32 [768], P('dp')
- key_grad: float32 [768, 768], P('dp')
- value_grad: float32 [768, 768], P('dp')
- vbias_grad: float32 [768], P('dp')
- out_grad: float32 [768, 768], P('dp')
- obias_grad: float32 [768], P('dp')
- gain1_grad: float32 [768], P('dp')
- shift1_grad: float32 [768], P('dp')
- inner_grad: float32 [768, 3072], P('dp')
- ibias_grad: float32 [3072], P('dp')
- outer_grad: float32 [3072, 768], P('dp')
- fbias_grad: float32 [768], P('dp')
- gain2_grad: float32 [768], P('dp')
- shift2_grad: float32 [768], P('dp')
Inputs may be any that keep to these rules, and one draw needn't show every extreme that they name: lengths[p] of the 512 slots of passage p are tokens, the rest padding; every draw has a passage of 512 tokens and one of 20.
All inputs are finite; a program needn't handle non-finite values.
Results may differ from a plain program's by a relative error of at most 0.015.
Values may be sent and summed in bfloat16 or wider, within the bound.
No kernel may reach another device: no remote copies, remote signals or barrier semaphores. Data moves between devices by JAX's collectives and lax.ppermute only.
A program may use at most 192 MiB of HBM per device.

v0:
```python
import math

import jax
import jax.numpy as jnp
from jax import lax
from jax.experimental import pallas as pl
from jax.experimental.pallas import tpu as pltpu
from jax.sharding import PartitionSpec as P

HEAD_DIM = 64
EPSILON = 1e-12
MASKED = -1e30
BF16 = jnp.bfloat16
F32 = jnp.float32
BOTH = ("dp", "seq")


TAIL = (
    0.11283793300390244, 0.11283480376005173, 0.10392128676176071, 0.08427156507968903, 0.07071308046579361,
    -0.0027973579708486795, 0.08453421294689178, -0.0914449393749237, 0.025129476562142372,
)


def dot(left, right, contract=(1, 0)):
    return lax.dot_general(
        left, right, (((contract[0],), (contract[1],)), ((), ())), preferred_element_type=F32
    )


def gelu_and_slope(x):
    t = 1.0 / (1.0 + (0.4 / math.sqrt(2.0)) * jnp.abs(x))
    bell = jnp.exp(x * x * -0.5)
    poly = TAIL[-1]
    for c in TAIL[-2::-1]:
        poly = poly * t + c
    tail = poly * t * bell
    cdf = jnp.where(x < 0.0, tail, 1.0 - tail)
    return x * cdf, cdf + x * bell * (1.0 / math.sqrt(2.0 * math.pi))


def normalize(z):
    center = z - jnp.mean(z, -1, keepdims=True)
    r = lax.rsqrt(jnp.mean(center * center, -1, keepdims=True) + EPSILON)
    return center * r, r


def norm_back(c, n, r):
    return r * (c - jnp.mean(c, -1, keepdims=True) - n * jnp.mean(c * n, -1, keepdims=True))


def fold8(x):
    return jnp.sum(x.reshape(x.shape[0] // 8, 8, x.shape[1]), 0)


def put_units(keep, send, slots, base, full, which, cols=slice(None)):
    n_dp = keep.shape[0]
    h = keep.shape[2]
    odd = slots[0] == 1
    low = full.astype(BF16)
    for m in range(full.shape[0] // (2 * h)):
        first = low[2 * m * h : (2 * m + 1) * h]
        second = low[(2 * m + 1) * h : (2 * m + 2) * h]
        keep[slots[1 + base + m], which, :, cols] = jnp.where(odd, second, first)
        send[slots[1 + n_dp + base + m], which, :, cols] = jnp.where(odd, first, second)


def up_kernel(ROWS, slots, hat, gain1, shift1, wi, bi, wo, bo, gain2, shift2, cot,
              result, slope, gpre, vec, keep, send, act_s, low_s, acc_s, gb_s):
    f = pl.program_id(0)
    nf = act_s.shape[0]
    tokens = hat.shape[0]

    @pl.when(f == 0)
    def _():
        normed = hat[...] * gain1[...] + shift1[...]
        low_s[...] = normed.astype(BF16)
        acc_s[...] = normed + bo[...]

    @pl.when(f < nf)
    def _():
        for r in range(0, tokens, ROWS):
            rows = slice(r, r + ROWS)
            act, slow = gelu_and_slope(dot(low_s[rows], wi[...]) + bi[...])
            act = act.astype(BF16)
            act_s[f, rows] = act
            slope[rows] = slow.astype(BF16)
            acc_s[rows] += dot(act, wo[...])

    @pl.when(f == nf - 1)
    def _():
        step = 32

        def body(i, sums):
            rows = pl.ds(pl.multiple_of(i * step, step), step)
            n, r = normalize(acc_s[rows])
            result[rows] = (n * gain2[...] + shift2[...]).astype(BF16)
            g = cot[rows].astype(F32)
            gz = norm_back(g * gain2[...], n, r)
            gpre[rows] = gz
            low = gz.astype(BF16)
            gb_s[rows] = low
            return sums[0] + fold8(low.astype(F32)), sums[1] + fold8(g * n), sums[2] + fold8(g)

        zero = jnp.zeros((8, hat.shape[1]), F32)
        sums = lax.fori_loop(0, tokens // step, body, (zero, zero, zero))
        for k in range(3):
            vec[k : k + 1] = jnp.sum(sums[k], 0, keepdims=True)

    @pl.when(f >= nf)
    def _():
        blocks = keep.shape[0] // nf
        put_units(keep, send, slots, (f - nf) * blocks, dot(act_s[f - nf], gb_s[...], (0, 0)), 0)


def whole(shape):
    return pl.BlockSpec(shape, lambda *_: (0,) * len(shape))


def ffn_up(n_dp, slots, hat, gain1, shift1, wi, bi, wo, bo, gain2, shift2, cot, ROWS=128):
    tokens, width = hat.shape
    ff = wi.shape[1]
    nf = ff // width
    half = ff // (2 * n_dp)
    step = lambda f: jnp.minimum(f, nf - 1)
    vector = whole((1, width))
    return pl.pallas_call(
        lambda *refs: up_kernel(ROWS, *refs),
        out_shape=(
            jax.ShapeDtypeStruct((tokens, width), BF16),
            jax.ShapeDtypeStruct((tokens, ff), BF16),
            jax.ShapeDtypeStruct((tokens, width), F32),
            jax.ShapeDtypeStruct((8, width), F32),
            jax.ShapeDtypeStruct((n_dp, 1, half, width), BF16),
            jax.ShapeDtypeStruct((n_dp, 1, half, width), BF16),
        ),
        grid_spec=pltpu.PrefetchScalarGridSpec(
            num_scalar_prefetch=1,
            grid=(2 * nf,),
            in_specs=[
                whole((tokens, width)), vector, vector,
                pl.BlockSpec((width, width), lambda f, s: (0, step(f))),
                pl.BlockSpec((1, width), lambda f, s: (0, step(f))),
                pl.BlockSpec((width, width), lambda f, s: (step(f), 0)),
                vector, vector, vector, whole((tokens, width)),
            ],
            out_specs=[
                whole((tokens, width)),
                pl.BlockSpec((tokens, width), lambda f, s: (0, step(f))),
                whole((tokens, width)),
                whole((8, width)),
                whole((n_dp, 1, half, width)),
                whole((n_dp, 1, half, width)),
            ],
            scratch_shapes=[
                pltpu.VMEM((nf, tokens, width), BF16),
                pltpu.VMEM((tokens, width), BF16),
                pltpu.VMEM((tokens, width), F32),
                pltpu.VMEM((tokens, width), BF16),
            ],
        ),
        compiler_params=pltpu.CompilerParams(vmem_limit_bytes=58 << 20),
        name="ffn_up",
    )(slots, hat, gain1, shift1, wi, bi, wo, bo, gain2, shift2, cot)


def attn_kernel(ROWS, x, bias, wq, bq, wk, wv, bv, wo, bo, q_out, k_out, v_out, p_out, c_out, hat_out, r_out, acc_s):
    g = pl.program_id(0)
    tokens = x.shape[0]
    xs = x[...]
    qs = (dot(xs, wq[...]) + bq[...]).astype(BF16) * (1.0 / math.sqrt(HEAD_DIM))
    ks = dot(xs, wk[...]).astype(BF16)
    vs = (dot(xs, wv[...]) + bv[...]).astype(BF16)
    q_out[...] = qs
    k_out[...] = ks
    v_out[...] = vs
    lane = lax.broadcasted_iota(jnp.int32, (1, 2 * HEAD_DIM), 1) < HEAD_DIM
    nil = jnp.zeros((), BF16)
    for pair in range(qs.shape[1] // (2 * HEAD_DIM)):
        cols = slice(pair * 2 * HEAD_DIM, (pair + 1) * 2 * HEAD_DIM)
        q2, k2, v2 = qs[:, cols], ks[:, cols], vs[:, cols]
        mine = (lane, jnp.logical_not(lane))
        vm = [jnp.where(m, v2, nil) for m in mine]
        for r in range(0, tokens, ROWS):
            rows = slice(r, r + ROWS)
            total = None
            for h in range(2):
                s = dot(jnp.where(mine[h], q2[rows], nil), k2, (1, 1)) + bias[...]
                e = jnp.exp(s - jnp.max(s, -1, keepdims=True))
                p = (e * (1.0 / jnp.sum(e, -1, keepdims=True))).astype(BF16)
                p_out[pair * 2 + h, rows] = p
                part = dot(p, vm[h])
                total = part if total is None else total + part
            c_out[rows, cols] = total.astype(BF16)
    more = dot(c_out[...], wo[...])

    @pl.when(g == 0)
    def _():
        acc_s[...] = xs.astype(F32) + bo[...] + more

    @pl.when(g > 0)
    def _():
        acc_s[...] += more

    @pl.when(g == pl.num_programs(0) - 1)
    def _():
        step = 32

        def body(i, _):
            rows = pl.ds(pl.multiple_of(i * step, step), step)
            n, r = normalize(acc_s[rows])
            hat_out[rows] = n
            r_out[rows] = r
            return 0

        lax.fori_loop(0, tokens // step, body, 0)


def attention_forward(x, bias, wq, bq, wk, wv, bv, wo, bo, ROWS=128):
    tokens, width = x.shape
    group = 4 * HEAD_DIM
    n = width // group
    heads = width // HEAD_DIM
    col = lambda rows: pl.BlockSpec((rows, group), lambda g: (0, g))
    low = jax.ShapeDtypeStruct((tokens, width), BF16)
    return pl.pallas_call(
        lambda *refs: attn_kernel(ROWS, *refs),
        out_shape=(
            low, low, low,
            jax.ShapeDtypeStruct((heads, tokens, tokens), BF16),
            low,
            jax.ShapeDtypeStruct((tokens, width), F32),
            jax.ShapeDtypeStruct((tokens, 1), F32),
        ),
        grid=(n,),
        in_specs=[
            whole((tokens, width)), whole((1, tokens)),
            col(width), col(1), col(width), col(width), col(1),
            pl.BlockSpec((group, width), lambda g: (g, 0)), whole((1, width)),
        ],
        out_specs=[
            col(tokens), col(tokens), col(tokens),
            pl.BlockSpec((4, tokens, tokens), lambda g: (g, 0, 0)),
            col(tokens), whole((tokens, width)), whole((tokens, 1)),
        ],
        scratch_shapes=[pltpu.VMEM((tokens, width), F32)],
        compiler_params=pltpu.CompilerParams(vmem_limit_bytes=58 << 20),
        name="attention_forward",
    )(x, bias, wq, bq, wk, wv, bv, wo, bo)


def down_kernel(ROWS, slots, gpre, slope, hat, gain1, shift1, wo, gi, ibias, keep, send, gb_s, nt_s):
    f = pl.program_id(0)
    tokens, width = hat.shape

    @pl.when(f == 0)
    def _():
        gb_s[...] = gpre[...].astype(BF16)
        nt_s[...] = (hat[...] * gain1[...] + shift1[...]).astype(BF16).T

    sums = jnp.zeros((8, width), F32)
    for r in range(0, tokens, ROWS):
        rows = slice(r, r + ROWS)
        low = (dot(gb_s[rows], wo[...], (1, 1)) * slope[rows].astype(F32)).astype(BF16)
        gi[rows] = low
        sums = sums + fold8(low.astype(F32))
    ibias[...] = jnp.sum(sums, 0, keepdims=True)
    put_units(keep, send, slots, 0, dot(nt_s[...], gi[...]), f)


def ffn_down(n_dp, slots, gpre, slope, hat, gain1, shift1, wo, ROWS=128):
    tokens, width = hat.shape
    ff = wo.shape[0]
    nf = ff // width
    vector = whole((1, width))
    full = whole((tokens, width))
    piece = pl.BlockSpec((tokens, width), lambda f, s: (0, f))
    shape = (n_dp, nf, width // (2 * n_dp), width)
    units = jax.ShapeDtypeStruct(shape, BF16)
    return pl.pallas_call(
        lambda *refs: down_kernel(ROWS, *refs),
        out_shape=(
            jax.ShapeDtypeStruct((tokens, ff), BF16),
            jax.ShapeDtypeStruct((1, ff), F32),
            units, units,
        ),
        grid_spec=pltpu.PrefetchScalarGridSpec(
            num_scalar_prefetch=1,
            grid=(nf,),
            in_specs=[
                full, piece, full, vector, vector,
                pl.BlockSpec((width, width), lambda f, s: (f, 0)),
            ],
            out_specs=[
                piece,
                pl.BlockSpec((1, width), lambda f, s: (0, f)),
                whole(shape), whole(shape),
            ],
            scratch_shapes=[
                pltpu.VMEM((tokens, width), BF16),
                pltpu.VMEM((width, tokens), BF16),
            ],
        ),
        compiler_params=pltpu.CompilerParams(vmem_limit_bytes=58 << 20),
        name="ffn_down",
    )(slots, gpre, slope, hat, gain1, shift1, wo)


def mid_kernel(slots, gpre, gi, hat, r1, gain1, wi, wa, ctx, gmid, gctx, vec, keep, send, acc_s, gb_s):
    f = pl.program_id(0)
    tokens, width = hat.shape
    more = dot(gi[...], wi[...], (1, 1))

    @pl.when(f == 0)
    def _():
        acc_s[...] = gpre[...] + more

    @pl.when(f > 0)
    def _():
        acc_s[...] += more

    @pl.when(f == pl.num_programs(0) - 1)
    def _():
        step = 32

        def body(i, sums):
            rows = pl.ds(pl.multiple_of(i * step, step), step)
            n = hat[rows]
            g = acc_s[rows]
            gz = norm_back(g * gain1[...], n, r1[rows])
            gmid[rows] = gz
            low = gz.astype(BF16)
            gb_s[rows] = low
            return sums[0] + fold8(low.astype(F32)), sums[1] + fold8(g * n), sums[2] + fold8(g)

        zero = jnp.zeros((8, width), F32)
        sums = lax.fori_loop(0, tokens // step, body, (zero, zero, zero))
        for k in range(3):
            vec[k : k + 1] = jnp.sum(sums[k], 0, keepdims=True)
        gctx[...] = dot(gb_s[...], wa[...], (1, 1)).astype(BF16)
        put_units(keep, send, slots, 0, dot(ctx[...].T, gb_s[...]), 0)


def middle(n_dp, slots, gpre, gi, hat, r1, gain1, wi, wa, ctx):
    tokens, width = hat.shape
    nf = wi.shape[1] // width
    full = whole((tokens, width))
    shape = (n_dp, 1, width // (2 * n_dp), width)
    units = jax.ShapeDtypeStruct(shape, BF16)
    return pl.pallas_call(
        mid_kernel,
        out_shape=(
            jax.ShapeDtypeStruct((tokens, width), F32),
            jax.ShapeDtypeStruct((tokens, width), BF16),
            jax.ShapeDtypeStruct((8, width), F32),
            units, units,
        ),
        grid_spec=pltpu.PrefetchScalarGridSpec(
            num_scalar_prefetch=1,
            grid=(nf,),
            in_specs=[
                full,
                pl.BlockSpec((tokens, width), lambda f, s: (0, f)),
                full, whole((tokens, 1)), whole((1, width)),
                pl.BlockSpec((width, width), lambda f, s: (0, f)),
                whole((width, width)), full,
            ],
            out_specs=[full, full, whole((8, width)), whole(shape), whole(shape)],
            scratch_shapes=[pltpu.VMEM((tokens, width), F32), pltpu.VMEM((tokens, width), BF16)],
        ),
        compiler_params=pltpu.CompilerParams(vmem_limit_bytes=58 << 20),
        name="middle",
    )(slots, gpre, gi, hat, r1, gain1, wi, wa, ctx)


def back_kernel(
    ROWS, slots, x, q, k, v, c, gc, p, dq, dk, dv, qb, vb, keep, send, xt_s, ds_s
):
    g = pl.program_id(0)
    tokens = x.shape[0]
    scale = 1.0 / math.sqrt(HEAD_DIM)
    pair_width = 2 * HEAD_DIM

    @pl.when(g == 0)
    def _():
        xt_s[...] = x[...].T

    lane = lax.broadcasted_iota(jnp.int32, (1, pair_width), 1) < HEAD_DIM
    mine = (lane, jnp.logical_not(lane))
    nil = jnp.zeros((), BF16)
    for pair in range(q.shape[1] // pair_width):
        cols = slice(pair * pair_width, (pair + 1) * pair_width)
        q2, k2, v2, c2, g2 = q[:, cols], k[:, cols], v[:, cols], c[:, cols], gc[:, cols]
        qt, gt = q2.T, g2.T
        prod = g2.astype(F32) * c2.astype(F32)
        dkt, dvt = [], []
        for r in range(0, tokens, ROWS):
            rows = slice(r, r + ROWS)
            total = None
            for h in range(2):
                delta = jnp.sum(jnp.where(mine[h], prod[rows], 0.0), -1, keepdims=True)
                dp = dot(jnp.where(mine[h], g2[rows], nil), v2, (1, 1))
                ds = (p[pair * 2 + h, rows].astype(F32) * (dp - delta)).astype(BF16)
                ds_s[h, rows] = ds
                part = dot(ds, jnp.where(mine[h], k2, nil))
                total = part if total is None else total + part
            dq[rows, cols] = (total * scale).astype(BF16)
        for h in range(2):
            rows = slice(h * HEAD_DIM, (h + 1) * HEAD_DIM)
            dvt.append(dot(gt[rows], p[pair * 2 + h]))
            dkt.append(dot(qt[rows], ds_s[h]))
        dv[:, cols] = jnp.concatenate(dvt, 0).astype(BF16).T
        dk[:, cols] = jnp.concatenate(dkt, 0).astype(BF16).T
    qb[...] = jnp.sum(fold8(dq[...].astype(F32)), 0, keepdims=True)
    vb[...] = jnp.sum(fold8(dv[...].astype(F32)), 0, keepdims=True)
    width = q.shape[1]
    cols = pl.ds(pl.multiple_of(g * width, width), width)
    for n, grad in enumerate((dq, dk, dv)):
        put_units(keep, send, slots, 0, dot(xt_s[...], grad[...]), n, cols)


def attention_back(n_dp, slots, x, q, k, v, c, gc, p, ROWS=128):
    tokens, width = x.shape
    group = 4 * HEAD_DIM
    col = pl.BlockSpec((tokens, group), lambda g, s: (0, g))
    row = pl.BlockSpec((1, group), lambda g, s: (0, g))
    low = jax.ShapeDtypeStruct((tokens, width), BF16)
    vector = jax.ShapeDtypeStruct((1, width), F32)
    shape = (n_dp, 3, width // (2 * n_dp), width)
    units = jax.ShapeDtypeStruct(shape, BF16)
    return pl.pallas_call(
        lambda *refs: back_kernel(ROWS, *refs),
        out_shape=(low, low, low, vector, vector, units, units),
        grid_spec=pltpu.PrefetchScalarGridSpec(
            num_scalar_prefetch=1,
            grid=(width // group,),
            in_specs=[whole((tokens, width)), col, col, col, col, col,
                      pl.BlockSpec((4, tokens, tokens), lambda g, s: (g, 0, 0))],
            out_specs=[col, col, col, row, row, whole(shape), whole(shape)],
            scratch_shapes=[
                pltpu.VMEM((width, tokens), BF16),
                pltpu.VMEM((2, tokens, tokens), BF16),
            ],
        ),
        compiler_params=pltpu.CompilerParams(vmem_limit_bytes=58 << 20),
        name="attention_back",
    )(slots, x, q, k, v, c, gc, p)


def input_kernel(gmid, dq, dk, dv, wq, wk, wv, out):
    total = gmid[...] + dot(dq[...], wq[...], (1, 1))
    total = total + dot(dk[...], wk[...], (1, 1))
    out[...] = (total + dot(dv[...], wv[...], (1, 1))).astype(BF16)


def input_gradient(gmid, dq, dk, dv, wq, wk, wv):
    tokens, width = gmid.shape
    rows = tokens // 4
    act = pl.BlockSpec((rows, width), lambda i: (i, 0))
    weight = whole((width, width))
    return pl.pallas_call(
        input_kernel,
        out_shape=jax.ShapeDtypeStruct((tokens, width), BF16),
        grid=(4,),
        in_specs=[act, act, act, act, weight, weight, weight],
        out_specs=act,
        compiler_params=pltpu.CompilerParams(vmem_limit_bytes=58 << 20),
        name="input_gradient",
    )(gmid, dq, dk, dv, wq, wk, wv)


def pairs(n_dp, n_seq, partner):
    out = []
    for d in range(n_dp):
        for s in range(n_seq):
            e, t = partner(d, s)
            out.append((d * n_seq + s, e * n_seq + t))
    return out


def pick(blocks, index):
    return lax.dynamic_index_in_dim(blocks, index, 0, keepdims=False)


def after(values, *others):
    return lax.optimization_barrier((values, others))[0]


def exchange(blocks, n_seq):
    return [blocks[0]] + [
        lax.ppermute(blocks[k], "seq", [(s, s ^ k) for s in range(n_seq)]) for k in range(1, n_seq)
    ]


def bit_orders(n_dp):
    bits = list(range(n_dp.bit_length() - 1))
    return bits, bits[1:] + bits[:1]


def slot_table(n_dp, d, s):
    orders = bit_orders(n_dp)
    odd = (s & 1) == 1
    by_core = []
    for order in orders:
        entries = []
        for j in range(n_dp):
            slot = 0
            for bit in order:
                slot = slot * 2 + (((d ^ j) >> bit) & 1)
            entries.append(slot)
        by_core.append(jnp.stack(entries))
    kept = jnp.where(odd, by_core[1], by_core[0])
    sent = jnp.where(odd, by_core[0], by_core[1])
    return jnp.concatenate([(s & 1)[None], kept, sent]).astype(jnp.int32)


def added(pieces, cut):
    total = pieces[0][cut].astype(F32)
    for piece in pieces[1:]:
        total = total + piece[cut].astype(F32)
    return total.astype(BF16)


class Halving:
    def __init__(self, keep, send, n_dp, n_seq):
        self.n_dp = n_dp
        self.n_seq = n_seq
        self.flips = [
            lambda d, s, zero=zero, one=one: (d ^ (1 << (one if s & 1 else zero)), s)
            for zero, one in zip(*bit_orders(n_dp))
        ]
        self.families = [[keep, self.permute(send, lambda d, s: (d, s ^ 1))]]

    def permute(self, values, partner):
        return lax.ppermute(values, BOTH, pairs(self.n_dp, self.n_seq, partner))

    def join(self, other):
        self.families += other.families

    def sums(self, cut):
        return jnp.concatenate([added(pieces, cut) for pieces in self.families], 1)

    def step(self, *wait):
        half = self.families[0][0].shape[0] // 2
        send = self.sums(slice(half, None))
        got = self.permute(after(send, *wait) if wait else send, self.flips.pop(0))
        families, first = [], 0
        for pieces in self.families:
            n = pieces[0].shape[1]
            families.append([piece[:half] for piece in pieces] + [got[:, first : first + n]])
            first += n
        self.families = families
        return got

    def share_y(self):
        mine = self.sums(slice(None))[0]
        got = self.permute(mine, lambda d, s: (d, s ^ 2))
        self.mine = (mine.astype(F32) + got.astype(F32)).astype(BF16)
        return got

    def share_core(self):
        other = self.permute(self.mine, lambda d, s: (d, s ^ 1))
        odd = (lax.axis_index("seq") & 1) == 1
        first = jnp.where(odd, other, self.mine)
        second = jnp.where(odd, self.mine, other)
        return jnp.concatenate([first, second], 1).astype(F32)


def sum_all(values, n_dp, n_seq):
    flips = [lambda d, s, k=k: (d, s ^ k) for k in (1, 2)]
    for bit in range(n_dp.bit_length() - 1):
        flips.append(lambda d, s, bit=bit: (d ^ (1 << bit), s))
    for flip in flips:
        values = values + lax.ppermute(values, BOTH, pairs(n_dp, n_seq, flip))
    return values


def local(
    hidden_states,
    lengths,
    query_weight,
    query_bias,
    key_weight,
    value_weight,
    value_bias,
    out_weight,
    out_bias,
    attn_gain,
    attn_shift,
    inner_weight,
    inner_bias,
    outer_weight,
    outer_bias,
    ffn_gain,
    ffn_shift,
    cotangent,
):
    _, slice_rows, width = hidden_states.shape
    n_seq = lax.axis_size("seq")
    n_dp = lax.axis_size("dp")
    d = lax.axis_index("dp")
    s = lax.axis_index("seq")
    tokens = slice_rows * n_seq
    slots = slot_table(n_dp, d, s)

    def to_passage(values):
        blocks = exchange([pick(values, s ^ k) for k in range(n_seq)], n_seq)
        return jnp.concatenate(blocks, 0)

    def to_slots(values):
        values = values.reshape(n_seq, slice_rows, width)
        blocks = exchange([values[k] for k in range(n_seq)], n_seq)
        odd = (s & 1) == 1
        high = (s & 2) == 2
        low = [jnp.where(odd, blocks[k ^ 1], blocks[k]) for k in range(4)]
        return jnp.stack([jnp.where(high, low[k ^ 2], low[k]) for k in range(4)])

    def row(vector):
        return vector.reshape(1, -1)

    x = to_passage(hidden_states)
    cot = to_passage(after(cotangent, x))
    spots = lax.iota(jnp.int32, tokens)
    spots = ((spots // slice_rows) ^ s) * slice_rows + spots % slice_rows
    bias = row(jnp.where(spots < pick(lengths, s), 0.0, MASKED))

    query, key, value, probs, context, hat, r1 = attention_forward(
        x, bias, query_weight, row(query_bias), key_weight, value_weight, row(value_bias),
        out_weight, row(out_bias),
    )
    gain1, shift1 = row(attn_gain), row(attn_shift)
    result, slope, grad_pre, vec2, *outer_units = ffn_up(
        n_dp, slots, hat, gain1, shift1, inner_weight, row(inner_bias), outer_weight,
        row(outer_bias), row(ffn_gain), row(ffn_shift), cot,
    )
    outer = Halving(*outer_units, n_dp, n_seq)
    grad_inner, ibias, *inner_units = ffn_down(
        n_dp, slots, grad_pre, slope, hat, gain1, shift1, outer_weight
    )
    inner = Halving(*inner_units, n_dp, n_seq)
    a1 = outer.step()
    grad_mid, grad_context, vec1, *out_units = middle(
        n_dp, slots, grad_pre, grad_inner, hat, r1, gain1, inner_weight, out_weight, context,
    )
    inner.join(Halving(*out_units, n_dp, n_seq))
    a2 = outer.step()
    b1 = inner.step()
    grad_query, grad_key, grad_value, qbias, vbias, *attn_units = attention_back(
        n_dp, slots, x, query, key, value, context, grad_context, probs,
    )
    attn = Halving(*attn_units, n_dp, n_seq)
    input_low = input_gradient(
        grad_mid, grad_query, grad_key, grad_value, query_weight, key_weight, value_weight,
    )
    vectors = jnp.concatenate([vec2[:3], vec1[:3], qbias, vbias, ibias.reshape(4, width)], 0)
    c1 = attn.step()
    b2 = inner.step()
    a3 = outer.step()
    c2 = attn.step()
    b3 = inner.step()
    outer.share_y()
    c3 = attn.step()
    while attn.flips:
        attn.step()
        inner.step()
        outer.step()
    inner.share_y()
    attn.share_y()
    vectors = sum_all(vectors, n_dp, n_seq)
    block_output = to_slots(result)
    input_grad = to_slots(input_low)
    outer_sum = outer.share_core()
    inner_sum = inner.share_core()
    attn_sum = attn.share_core()
    part = width // n_dp
    mine = lax.dynamic_slice_in_dim(vectors[:8], d * part, part, 1)
    ibias_part = lax.dynamic_slice_in_dim(vectors[8:].reshape(4 * width), d * 4 * part, 4 * part, 0)
    return (
        block_output,
        input_grad,
        attn_sum[0],
        mine[6],
        attn_sum[1],
        attn_sum[2],
        mine[7],
        inner_sum[4],
        mine[3],
        mine[4],
        mine[5],
        jnp.concatenate([inner_sum[t] for t in range(4)], 1),
        ibias_part,
        outer_sum[0],
        mine[0],
        mine[1],
        mine[2],
    )


def solution(mesh):
    tokens = P("dp", "seq", None)
    in_specs = (tokens, P("dp")) + (P(),) * 15 + (tokens,)
    rows = P("dp", None)
    vector = P("dp")
    out_specs = (
        tokens, tokens, rows, vector, rows, rows, vector, rows, vector,
        vector, vector, rows, vector, rows, vector, vector, vector,
    )
    return jax.shard_map(local, mesh=mesh, in_specs=in_specs, out_specs=out_specs, check_vma=False)
```

profile of v0, /device:TPU:0, one launch (start us, length us, event | category | flops | bytes accessed | tf_op | source)
XLA Modules:
  0.0 271.7 jit_solution(9826408759352528996)
XLA Ops:
  0.8 1.3 dynamic-slice_bitcast_fusion.7
  2.7 2.6 collective-permute-start.1
  11.0 3.7 %collective-permute-done.2 = bf16[128,768]{1,0:T(8,128)(2,1)S(1)} collective-permute-done((bf16[128,768]{1,0:T(8,128)(2,1)S(1)}, bf16[128,768]{1,0:T(8,128)(2,1)S(1)}, u32[]{:S(2)}, u32[]{:S(2)}) %collective-permute-start.2) | collective-permute-done | bytes 196640 | tf_op jit(solution)/shard_map/ppermute | solution.py:490
  15.9 1.7 collective-permute-start.4
  19.4 22.3 %attention_forward.1 = (bf16[512,768]{1,0:T(8,128)(2,1)}, bf16[512,768]{1,0:T(8,128)(2,1)}, bf16[512,768]{1,0:T(8,128)(2,1)}, bf16[12,512,512]{2,1,0:T(8,128)(2,...) custom-call(bf16[512,768]{1,0:T(8,128)(2,1)} %pad_maximum_fusion.2.refs_0_.refs_1_, ...), custom_call_target="tpu_custom_call" | custom-call | tf_op jit(solution)/shard_map/attention_forward/pallas_call | solution.py:225
  42.7 27.6 %ffn_up.1 = (bf16[512,768]{1,0:T(8,128)(2,1)}, bf16[512,3072]{1,0:T(8,128)(2,1)}, f32[512,768]{1,0:T(8,128)}, f32[8,768]{1,0:T(8,128)}, bf16[8,1,192,768]{3,2,1,...) custom-call(s32[17]{0:T(128)} %pad_add_fusion.refs_0_.slots, f32[512,768]{1,0:T(8,128)} %get-tuple-element.47.refs_1_.refs_3_.hat, ...), custom_call_target="tpu_custom_call" | custom-call | tf_op jit(solution)/shard_map/ffn_up/pallas_call | solution.py:126
  70.7 15.2 %ffn_down.1 = (bf16[512,3072]{1,0:T(8,128)(2,1)}, f32[1,3072]{1,0:T(1,128)}, bf16[8,4,48,768]{3,2,1,0:T(8,128)(2,1)}, bf16[8,4,48,768]{3,2,1,0:T(8,128)(2,1)}) custom-call(s32[17]{0:T(128)} %pad_add_fusion.refs_0_.slots, f32[512,768]{1,0:T(8,128)} %get-tuple-element.50.refs_1_.gpre, bf16[512,3072]{1,0:T(8,128)(2,1)} %get-tuple-element.51.refs_2_, ...), custom_call_target="tpu_custom_call" | custom-call | tf_op jit(solution)/shard_map/ffn_down/pallas_call | solution.py:279
  85.9 13.9 %middle.1 = (f32[512,768]{1,0:T(8,128)}, bf16[512,768]{1,0:T(8,128)(2,1)}, f32[8,768]{1,0:T(8,128)}, bf16[8,1,48,768]{3,2,1,0:T(8,128)(2,1)}, bf16[8,1,48,768]{3,2,1,0:T(8,128)(2,1)}) custom-call(s32[17]{0:T(128)} %pad_add_fusion.refs_0_.slots, f32[512,768]{1,0:T(8,128)} %get-tuple-element.50.refs_1_.gpre, bf16[512,3072]{1,0:T(8,128)(2,1)} %get-tuple-element.52.gi, ...), custom_call_target="tpu_custom_call" | custom-call | tf_op jit(solution)/shard_map/middle/pallas_call | solution.py:349
  99.8 16.4 %attention_back.1 = (bf16[512,768]{1,0:T(8,128)(2,1)}, bf16[512,768]{1,0:T(8,128)(2,1)}, bf16[512,768]{1,0:T(8,128)(2,1)}, f32[1,768]{1,0:T(1,128)}, f32[1,768]{...) custom-call(s32[17]{0:T(128)} %pad_add_fusion.refs_0_.slots, ...), custom_call_target="tpu_custom_call" | custom-call | tf_op jit(solution)/shard_map/attention_back/pallas_call | solution.py:430
  119.0 4.7 %collective-permute-done.18 = f32[12,768]{1,0:T(8,128)S(1)} collective-permute-done((f32[12,768]{1,0:T(8,128)S(1)}, f32[12,768]{1,0:T(8,128)S(1)}, u32[]{:S(2)}, u32[]{:S(2)}) %collective-permute-start.18) | collective-permute-done | bytes 36896 | tf_op jit(solution)/shard_map/ppermute | solution.py:573
  123.8 1.8 collective-permute-start.19
  125.5 2.4 collective-permute-done.19
  127.9 1.7 collective-permute-start.20
  129.7 8.4 %input_gradient.1 = bf16[512,768]{1,0:T(8,128)(2,1)} custom-call(f32[512,768]{1,0:T(8,128)} %get-tuple-element.55.gmid, bf16[512,768]{1,0:T(8,128)(2,1)} %get-tuple-element.61.dq, bf16[512,768]{1,0:T(8,128)(2,1)} %get-tuple-element.62.dk, bf16[512,768]{1,0:T(8,128)(2,1)} %get-tuple-element.63.dv, bf16[768,768]{1,0:T(8,128)(2,1)} %wq.1, bf16[768,768]{1,0:T(8,128)(2,1)} %wk.1, ...), custom_call_target="tpu_custom_call" | custom-call | tf_op jit(solution)/shard_map/input_gradient/pallas_call | solution.py:460
  138.1 1.6 collective-permute-start.21
  139.8 1.9 fusion.5
  142.3 1.5 collective-permute-start.10
  143.8 2.7 collective-permute-start.22
  146.5 1.5 add_convert_fusion.2
  148.8 1.4 copy-done.3
  150.3 1.7 add_convert_fusion
  152.0 1.5 collective-permute-start.31
  153.4 1.6 add_convert_fusion.1
  155.0 1.2 pad_maximum_fusion
  156.9 4.3 %collective-permute-done.13 = bf16[4,3,48,768]{3,2,1,0:T(8,128)(2,1)S(1)} collective-permute-done((bf16[4,3,48,768]{3,2,1,0:T(8,128)(2,1)S(1)}, bf16[4,3,48,768]{3,2,1,0:T(8,128)(2,1)S(1)}, u32[]{:S(2)}, u32[]{:S(2)}) %collective-permute-start.13) | collective-permute-done | bytes 884768 | tf_op jit(solution)/shard_map/ppermute | solution.py:534
  161.1 2.2 add_convert_fusion.5
  163.4 1.6 collective-permute-start.14
  167.0 1.3 dynamic_slice.45
  170.3 1.2 collective-permute-start.6
  171.5 4.4 %collective-permute-done.9 = bf16[128,768]{1,0:T(8,128)(2,1)S(1)} collective-permute-done((bf16[128,768]{1,0:T(8,128)(2,1)}, bf16[128,768]{1,0:T(8,128)(2,1)S(1)}, u32[]{:S(2)}, u32[]{:S(2)}) %collective-permute-start.9) | collective-permute-done | bytes 196640 | tf_op jit(solution)/shard_map/ppermute | solution.py:490
  176.9 1.5 collective-permute-done.14
  178.4 16.4 %collective-permute-start.8 = (bf16[128,768]{1,0:T(8,128)(2,1)}, bf16[128,768]{1,0:T(8,128)(2,1)S(1)}, u32[]{:S(2)}, u32[]{:S(2)}) collective-permute-start(bf16[128,768]{1,0:T(8,128)(2,1)} %get-tuple-element.96), channel_id=1, source_target_pairs={{0,1},{1,0},{2,3},{3,2},{4,5},{5,4},{6,7},{7,6},{8,9},{9,8},{10,11... | collective-permute-start | bytes 589832 | tf_op jit(solution)/shard_map/ppermute | solution.py:490
  194.9 1.5 add_convert_fusion.15
  196.4 3.1 %collective-permute-start.15 = (bf16[1,3,48,768]{3,2,1,0:T(8,128)(2,1)S(1)}, bf16[1,3,48,768]{3,2,1,0:T(8,128)(2,1)S(1)}, u32[]{:S(2)}, u32[]{:S(2)}) collective-permute-start(bf16[1,3,48,768]{3,2,1,0:T(8,128)(2,1)S(1)} %add_convert_fusion.15), channel_id=1, source_target_pairs={{0,16},{1,5},{2,18},{3,7},{4,20},{5,1},{6,22},{7,3},{8,24},{9,13},... | collective-permute-start | bytes 663560 | tf_op jit(solution)/shard_map/ppermute | solution.py:534
  199.6 1.4 select_bitcast_fusion.5
  200.9 4.9 %collective-permute-done.15 = bf16[1,3,48,768]{3,2,1,0:T(8,128)(2,1)S(1)} collective-permute-done((bf16[1,3,48,768]{3,2,1,0:T(8,128)(2,1)S(1)}, bf16[1,3,48,768]{3,2,1,0:T(8,128)(2,1)S(1)}, u32[]{:S(2)}, u32[]{:S(2)}) %collective-permute-start.15) | collective-permute-done | bytes 221216 | tf_op jit(solution)/shard_map/ppermute | solution.py:534
  205.8 1.4 fusion.1
  207.8 1.3 add_convert_fusion.3
  209.3 1.5 add_convert_fusion.4
  211.9 2.0 collective-permute-start.26
  216.0 9.4 %collective-permute-done.32 = bf16[2,1,192,768]{3,2,1,0:T(8,128)(2,1)S(1)} collective-permute-done((bf16[2,1,192,768]{3,2,1,0:T(8,128)(2,1)S(1)}, bf16[2,1,192,768]{3,2,1,0:T(8,128)(2,1)S(1)}, u32[]{:S(2)}, u32[]{:S(2)}) %collective-permute-start.32) | collective-permute-done | bytes 589856 | tf_op jit(solution)/shard_map/ppermute | solution.py:534
  227.2 16.9 %collective-permute-done.26 = bf16[2,5,48,768]{3,2,1,0:T(8,128)(2,1)S(1)} collective-permute-done((bf16[2,5,48,768]{3,2,1,0:T(8,128)(2,1)S(1)}, bf16[2,5,48,768]{3,2,1,0:T(8,128)(2,1)S(1)}, u32[]{:S(2)}, u32[]{:S(2)}) %collective-permute-start.26) | collective-permute-done | bytes 737312 | tf_op jit(solution)/shard_map/ppermute | solution.py:534
  244.0 1.2 add_convert_fusion.11
  247.5 1.6 collective-permute-start.34
  249.1 8.6 %collective-permute-done.27 = bf16[1,5,48,768]{3,2,1,0:T(8,128)(2,1)S(1)} collective-permute-done((bf16[1,5,48,768]{3,2,1,0:T(8,128)(2,1)S(1)}, bf16[1,5,48,768]{3,2,1,0:T(8,128)(2,1)S(1)}, u32[]{:S(2)}, u32[]{:S(2)}) %collective-permute-start.27) | collective-permute-done | bytes 368672 | tf_op jit(solution)/shard_map/ppermute | solution.py:534
  257.7 1.2 add_convert_fusion.10
  259.9 1.6 collective-permute-start.28
  261.7 5.8 %collective-permute-done.28 = bf16[5,48,768]{2,1,0:T(8,128)(2,1)S(1)} collective-permute-done((bf16[5,48,768]{2,1,0:T(8,128)(2,1)S(1)}, bf16[5,48,768]{2,1,0:T(8,128)(2,1)S(1)}, u32[]{:S(2)}, u32[]{:S(2)}) %collective-permute-start.28) | collective-permute-done | bytes 368672 | tf_op jit(solution)/shard_map/ppermute | solution.py:534
  (151 shorter events, 33.7 us)
Async XLA Ops:
  0.7 7.5 %copy-start.20 = (f32[768]{0:T(1024)S(1)}, f32[768]{0:T(1024)}, u32[]{:S(2)}) copy-start(f32[768]{0:T(1024)} %param.28) | copy-start | bytes 9220
  0.7 8.1 %copy-start.21 = (f32[768]{0:T(1024)S(1)}, f32[768]{0:T(1024)}, u32[]{:S(2)}) copy-start(f32[768]{0:T(1024)} %param.32) | copy-start | bytes 9220
  0.7 8.7 %copy-start.22 = (f32[768]{0:T(1024)S(1)}, f32[768]{0:T(1024)}, u32[]{:S(2)}) copy-start(f32[768]{0:T(1024)} %param.33) | copy-start | bytes 9220
  0.7 9.3 %copy-start.23 = (f32[768]{0:T(1024)S(1)}, f32[768]{0:T(1024)}, u32[]{:S(2)}) copy-start(f32[768]{0:T(1024)} %param.34) | copy-start | bytes 9220
  0.8 14.9 %copy-start.7 = (bf16[4,128,768]{2,1,0:T(8,128)(2,1)S(1)}, bf16[4,128,768]{2,1,0:T(8,128)(2,1)}, u32[]{:S(2)}) copy-start(bf16[4,128,768]{2,1,0:T(8,128)(2,1)} %param.35) | copy-start | bytes 2359300
  2.1 8.6 %collective-permute-start = (bf16[128,768]{1,0:T(8,128)(2,1)S(1)}, bf16[128,768]{1,0:T(8,128)(2,1)S(1)}, u32[]{:S(2)}, u32[]{:S(2)}) collective-permute-start(bf16[128,768]{1,0:T(8,128)(2,1)S(1)} %get-tuple-element.104), channel_id=1, source_target_pairs={{0,1},{1,0},{2,3},{3,2},{4,5},{5,4},{6,7},{7,6},{8,9},{9,8},{10,11... | collective-permute-start | bytes 589832 | tf_op jit(solution)/shard_map/ppermute | solution.py:490
  2.7 8.3 %collective-permute-start.1 = (bf16[128,768]{1,0:T(8,128)(2,1)S(1)}, bf16[128,768]{1,0:T(8,128)(2,1)S(1)}, u32[]{:S(2)}, u32[]{:S(2)}) collective-permute-start(bf16[128,768]{1,0:T(8,128)(2,1)S(1)} %get-tuple-element.106), channel_id=1, source_target_pairs={{0,2},{1,3},{2,0},{3,1},{4,6},{5,7},{6,4},{7,5},{8,10},{9,11},{10,... | collective-permute-start | bytes 589832 | tf_op jit(solution)/shard_map/ppermute | solution.py:490
  5.3 9.4 %collective-permute-start.2 = (bf16[128,768]{1,0:T(8,128)(2,1)S(1)}, bf16[128,768]{1,0:T(8,128)(2,1)S(1)}, u32[]{:S(2)}, u32[]{:S(2)}) collective-permute-start(bf16[128,768]{1,0:T(8,128)(2,1)S(1)} %get-tuple-element.105), channel_id=1, source_target_pairs={{0,3},{1,2},{2,1},{3,0},{4,7},{5,6},{6,5},{7,4},{8,11},{9,10},{10,... | collective-permute-start | bytes 589832 | tf_op jit(solution)/shard_map/ppermute | solution.py:490
  15.7 25.9 %collective-permute-start.3 = (bf16[128,768]{1,0:T(8,128)(2,1)S(1)}, bf16[128,768]{1,0:T(8,128)(2,1)S(1)}, u32[]{:S(2)}, u32[]{:S(2)}) collective-permute-start(bf16[128,768]{1,0:T(8,128)(2,1)S(1)} %get-tuple-element.102), channel_id=1, source_target_pairs={{0,1},{1,0},{2,3},{3,2},{4,5},{5,4},{6,7},{7,6},{8,9},{9,8},{10,11... | collective-permute-start | bytes 589832 | tf_op jit(solution)/shard_map/ppermute | solution.py:490
  15.9 25.8 %collective-permute-start.4 = (bf16[128,768]{1,0:T(8,128)(2,1)S(1)}, bf16[128,768]{1,0:T(8,128)(2,1)S(1)}, u32[]{:S(2)}, u32[]{:S(2)}) collective-permute-start(bf16[128,768]{1,0:T(8,128)(2,1)S(1)} %get-tuple-element.101), channel_id=1, source_target_pairs={{0,2},{1,3},{2,0},{3,1},{4,6},{5,7},{6,4},{7,5},{8,10},{9,11},{10,... | collective-permute-start | bytes 589832 | tf_op jit(solution)/shard_map/ppermute | solution.py:490
  17.6 24.1 %collective-permute-start.5 = (bf16[128,768]{1,0:T(8,128)(2,1)S(1)}, bf16[128,768]{1,0:T(8,128)(2,1)S(1)}, u32[]{:S(2)}, u32[]{:S(2)}) collective-permute-start(bf16[128,768]{1,0:T(8,128)(2,1)S(1)} %get-tuple-element.100), channel_id=1, source_target_pairs={{0,3},{1,2},{2,1},{3,0},{4,7},{5,6},{6,5},{7,4},{8,11},{9,10},{10,... | collective-permute-start | bytes 589832 | tf_op jit(solution)/shard_map/ppermute | solution.py:490
  70.3 78.4 %collective-permute-start.30 = (bf16[8,1,192,768]{3,2,1,0:T(8,128)(2,1)}, bf16[8,1,192,768]{3,2,1,0:T(8,128)(2,1)S(1)}, u32[]{:S(2)}, u32[]{:S(2)}) collective-permute-start(bf16[8,1,192,768]{3,2,1,0:T(8,128)(2,1)} %get-tuple-element.76), channel_id=1, source_target_pairs={{0,1},{1,0},{2,3},{3,2},{4,5},{5,4},{6,7},{7,6},{8,9},{9,8},{10,11... | collective-permute-start | bytes 7077896 | tf_op jit(solution)/shard_map/ppermute | solution.py:534
  99.8 17.1 %copy-start.15 = (f32[8,768]{1,0:T(8,128)S(1)}, f32[8,768]{1,0:T(8,128)}, u32[]{:S(2)}) copy-start(f32[8,768]{1,0:T(8,128)} %get-tuple-element.67) | copy-start | bytes 73732
  99.8 17.6 %copy-start.13 = (f32[1,3072]{1,0:T(1,128)S(1)}, f32[1,3072]{1,0:T(1,128)}, u32[]{:S(2)}) copy-start(f32[1,3072]{1,0:T(1,128)} %get-tuple-element.70) | copy-start | bytes 36868
  99.8 18.3 %copy-start.14 = (f32[8,768]{1,0:T(8,128)S(1)}, f32[8,768]{1,0:T(8,128)}, u32[]{:S(2)}) copy-start(f32[8,768]{1,0:T(8,128)} %get-tuple-element.66) | copy-start | bytes 73732
  116.3 27.5 %collective-permute-start.12 = (bf16[8,3,48,768]{3,2,1,0:T(8,128)(2,1)}, bf16[8,3,48,768]{3,2,1,0:T(8,128)(2,1)}, u32[]{:S(2)}, u32[]{:S(2)}) collective-permute-start(bf16[8,3,48,768]{3,2,1,0:T(8,128)(2,1)} %get-tuple-element.65), channel_id=1, source_target_pairs={{0,1},{1,0},{2,3},{3,2},{4,5},{5,4},{6,7},{7,6},{8,9},{9,8},{10,11... | collective-permute-start | bytes 5308424 | tf_op jit(solution)/shard_map/ppermute | solution.py:534
  116.5 37.0 %collective-permute-start.23 = (bf16[8,4,48,768]{3,2,1,0:T(8,128)(2,1)}, bf16[8,4,48,768]{3,2,1,0:T(8,128)(2,1)}, u32[]{:S(2)}, u32[]{:S(2)}) collective-permute-start(bf16[8,4,48,768]{3,2,1,0:T(8,128)(2,1)} %get-tuple-element.72), channel_id=1, source_target_pairs={{0,1},{1,0},{2,3},{3,2},{4,5},{5,4},{6,7},{7,6},{8,9},{9,8},{10,11... | collective-permute-start | bytes 7077896 | tf_op jit(solution)/shard_map/ppermute | solution.py:534
  118.8 4.9 %collective-permute-start.18 = (f32[12,768]{1,0:T(8,128)S(1)}, f32[12,768]{1,0:T(8,128)S(1)}, u32[]{:S(2)}, u32[]{:S(2)}) collective-permute-start(f32[12,768]{1,0:T(8,128)S(1)} %concatenate.47), channel_id=1, source_target_pairs={{0,1},{1,0},{2,3},{3,2},{4,5},{5,4},{6,7},{7,6},{8,9},{9,8},{10,11... | collective-permute-start | bytes 110600 | tf_op jit(solution)/shard_map/ppermute | solution.py:573
  123.8 4.1 %collective-permute-start.19 = (f32[12,768]{1,0:T(8,128)S(1)}, f32[12,768]{1,0:T(8,128)S(1)}, u32[]{:S(2)}, u32[]{:S(2)}) collective-permute-start(f32[12,768]{1,0:T(8,128)S(1)} %add.345), channel_id=1, source_target_pairs={{0,2},{1,3},{2,0},{3,1},{4,6},{5,7},{6,4},{7,5},{8,10},{9,11},{10,... | collective-permute-start | bytes 110600 | tf_op jit(solution)/shard_map/ppermute | solution.py:573
  125.5 22.5 %collective-permute-start.24 = (bf16[8,1,48,768]{3,2,1,0:T(8,128)(2,1)}, bf16[8,1,48,768]{3,2,1,0:T(8,128)(2,1)S(1)}, u32[]{:S(2)}, u32[]{:S(2)}) collective-permute-start(bf16[8,1,48,768]{3,2,1,0:T(8,128)(2,1)} %get-tuple-element.74), channel_id=1, source_target_pairs={{0,1},{1,0},{2,3},{3,2},{4,5},{5,4},{6,7},{7,6},{8,9},{9,8},{10,11... | collective-permute-start | bytes 1769480 | tf_op jit(solution)/shard_map/ppermute | solution.py:534
  127.9 10.2 %collective-permute-start.20 = (f32[12,768]{1,0:T(8,128)S(1)}, f32[12,768]{1,0:T(8,128)S(1)}, u32[]{:S(2)}, u32[]{:S(2)}) collective-permute-start(f32[12,768]{1,0:T(8,128)S(1)} %add.346), channel_id=1, source_target_pairs={{0,4},{1,5},{2,6},{3,7},{4,0},{5,1},{6,2},{7,3},{8,12},{9,13},{10,... | collective-permute-start | bytes 110600 | tf_op jit(solution)/shard_map/ppermute | solution.py:573
  129.7 16.8 %copy-start.5 = (bf16[8,3,48,768]{3,2,1,0:T(8,128)(2,1)S(1)}, bf16[8,3,48,768]{3,2,1,0:T(8,128)(2,1)}, u32[]{:S(2)}) copy-start(bf16[8,3,48,768]{3,2,1,0:T(8,128)(2,1)} %get-tuple-element.64) | copy-start | bytes 5308420
  138.1 4.2 %collective-permute-start.21 = (f32[12,768]{1,0:T(8,128)S(1)}, f32[12,768]{1,0:T(8,128)S(1)}, u32[]{:S(2)}, u32[]{:S(2)}) collective-permute-start(f32[12,768]{1,0:T(8,128)S(1)} %add.347), channel_id=1, source_target_pairs={{0,8},{1,9},{2,10},{3,11},{4,12},{5,13},{6,14},{7,15},{8,0},{9,1},... | collective-permute-start | bytes 110600 | tf_op jit(solution)/shard_map/ppermute | solution.py:573
  142.3 26.8 %collective-permute-start.10 = (bf16[128,768]{1,0:T(8,128)(2,1)}, bf16[128,768]{1,0:T(8,128)(2,1)}, u32[]{:S(2)}, u32[]{:S(2)}) collective-permute-start(bf16[128,768]{1,0:T(8,128)(2,1)} %get-tuple-element.94), channel_id=1, source_target_pairs={{0,2},{1,3},{2,0},{3,1},{4,6},{5,7},{6,4},{7,5},{8,10},{9,11},{10,... | collective-permute-start | bytes 589832 | tf_op jit(solution)/shard_map/ppermute | solution.py:490
  143.8 21.9 %collective-permute-start.22 = (f32[12,768]{1,0:T(8,128)S(1)}, f32[12,768]{1,0:T(8,128)S(1)}, u32[]{:S(2)}, u32[]{:S(2)}) collective-permute-start(f32[12,768]{1,0:T(8,128)S(1)} %add.348), channel_id=1, source_target_pairs={{0,16},{1,17},{2,18},{3,19},{4,20},{5,21},{6,22},{7,23},{8,24},{9,... | collective-permute-start | bytes 110600 | tf_op jit(solution)/shard_map/ppermute | solution.py:573
  148.0 13.1 %collective-permute-start.13 = (bf16[4,3,48,768]{3,2,1,0:T(8,128)(2,1)S(1)}, bf16[4,3,48,768]{3,2,1,0:T(8,128)(2,1)S(1)}, u32[]{:S(2)}, u32[]{:S(2)}) collective-permute-start(bf16[4,3,48,768]{3,2,1,0:T(8,128)(2,1)S(1)} %add_convert_fusion.2), channel_id=1, source_target_pairs={{0,4},{1,9},{2,6},{3,11},{4,0},{5,13},{6,2},{7,15},{8,12},{9,1},{1... | collective-permute-start | bytes 2654216 | tf_op jit(solution)/shard_map/ppermute | solution.py:534
  152.0 55.9 %collective-permute-start.31 = (bf16[4,1,192,768]{3,2,1,0:T(8,128)(2,1)S(1)}, bf16[4,1,192,768]{3,2,1,0:T(8,128)(2,1)}, u32[]{:S(2)}, u32[]{:S(2)}) collective-permute-start(bf16[4,1,192,768]{3,2,1,0:T(8,128)(2,1)S(1)} %add_convert_fusion), channel_id=1, source_target_pairs={{0,4},{1,9},{2,6},{3,11},{4,0},{5,13},{6,2},{7,15},{8,12},{9,1},{1... | collective-permute-start | bytes 3538952 | tf_op jit(solution)/shard_map/ppermute | solution.py:534
  156.2 8.7 %copy-start.8 = (bf16[512,768]{1,0:T(8,128)(2,1)S(1)}, bf16[512,768]{1,0:T(8,128)(2,1)}, u32[]{:S(2)}) copy-start(bf16[512,768]{1,0:T(8,128)(2,1)} %get-tuple-element.49) | copy-start | bytes 2359300
  156.2 53.0 %collective-permute-start.25 = (bf16[4,5,48,768]{3,2,1,0:T(8,128)(2,1)}, bf16[4,5,48,768]{3,2,1,0:T(8,128)(2,1)}, u32[]{:S(2)}, u32[]{:S(2)}) collective-permute-start(bf16[4,5,48,768]{3,2,1,0:T(8,128)(2,1)} %pad_maximum_fusion), channel_id=1, source_target_pairs={{0,4},{1,9},{2,6},{3,11},{4,0},{5,13},{6,2},{7,15},{8,12},{9,1},{1... | collective-permute-start | bytes 4423688 | tf_op jit(solution)/shard_map/ppermute | solution.py:534
  163.4 15.0 %collective-permute-start.14 = (bf16[2,3,48,768]{3,2,1,0:T(8,128)(2,1)}, bf16[2,3,48,768]{3,2,1,0:T(8,128)(2,1)}, u32[]{:S(2)}, u32[]{:S(2)}) collective-permute-start(bf16[2,3,48,768]{3,2,1,0:T(8,128)(2,1)} %add_convert_fusion.5), channel_id=1, source_target_pairs={{0,8},{1,17},{2,10},{3,19},{4,12},{5,21},{6,14},{7,23},{8,0},{9,25... | collective-permute-start | bytes 1327112 | tf_op jit(solution)/shard_map/ppermute | solution.py:534
  165.8 4.5 %collective-permute-start.11 = (bf16[128,768]{1,0:T(8,128)(2,1)}, bf16[128,768]{1,0:T(8,128)(2,1)}, u32[]{:S(2)}, u32[]{:S(2)}) collective-permute-start(bf16[128,768]{1,0:T(8,128)(2,1)} %get-tuple-element.93), channel_id=1, source_target_pairs={{0,1},{1,0},{2,3},{3,2},{4,5},{5,4},{6,7},{7,6},{8,9},{9,8},{10,11... | collective-permute-start | bytes 589832 | tf_op jit(solution)/shard_map/ppermute | solution.py:490
  169.1 6.7 %collective-permute-start.9 = (bf16[128,768]{1,0:T(8,128)(2,1)}, bf16[128,768]{1,0:T(8,128)(2,1)S(1)}, u32[]{:S(2)}, u32[]{:S(2)}) collective-permute-start(bf16[128,768]{1,0:T(8,128)(2,1)} %get-tuple-element.95), channel_id=1, source_target_pairs={{0,3},{1,2},{2,1},{3,0},{4,7},{5,6},{6,5},{7,4},{8,11},{9,10},{10,... | collective-permute-start | bytes 589832 | tf_op jit(solution)/shard_map/ppermute | solution.py:490
  170.3 26.1 %collective-permute-start.6 = (bf16[128,768]{1,0:T(8,128)(2,1)}, bf16[128,768]{1,0:T(8,128)(2,1)S(1)}, u32[]{:S(2)}, u32[]{:S(2)}) collective-permute-start(bf16[128,768]{1,0:T(8,128)(2,1)} %get-tuple-element.98), channel_id=1, source_target_pairs={{0,3},{1,2},{2,1},{3,0},{4,7},{5,6},{6,5},{7,4},{8,11},{9,10},{10,... | collective-permute-start | bytes 589832 | tf_op jit(solution)/shard_map/ppermute | solution.py:490
  175.9 23.7 %collective-permute-start.7 = (bf16[128,768]{1,0:T(8,128)(2,1)}, bf16[128,768]{1,0:T(8,128)(2,1)S(1)}, u32[]{:S(2)}, u32[]{:S(2)}) collective-permute-start(bf16[128,768]{1,0:T(8,128)(2,1)} %get-tuple-element.97), channel_id=1, source_target_pairs={{0,2},{1,3},{2,0},{3,1},{4,6},{5,7},{6,4},{7,5},{8,10},{9,11},{10,... | collective-permute-start | bytes 589832 | tf_op jit(solution)/shard_map/ppermute | solution.py:490
  178.4 21.1 %collective-permute-start.8 = (bf16[128,768]{1,0:T(8,128)(2,1)}, bf16[128,768]{1,0:T(8,128)(2,1)S(1)}, u32[]{:S(2)}, u32[]{:S(2)}) collective-permute-start(bf16[128,768]{1,0:T(8,128)(2,1)} %get-tuple-element.96), channel_id=1, source_target_pairs={{0,1},{1,0},{2,3},{3,2},{4,5},{5,4},{6,7},{7,6},{8,9},{9,8},{10,11... | collective-permute-start | bytes 589832 | tf_op jit(solution)/shard_map/ppermute | solution.py:490
  194.9 13.0 %copy-start.4 = (bf16[8,1,192,768]{3,2,1,0:T(8,128)(2,1)S(1)}, bf16[8,1,192,768]{3,2,1,0:T(8,128)(2,1)}, u32[]{:S(2)}) copy-start(bf16[8,1,192,768]{3,2,1,0:T(8,128)(2,1)} %copy-done.3) | copy-start | bytes 7077892
  196.4 11.5 %copy-start.2 = (bf16[8,1,192,768]{3,2,1,0:T(8,128)(2,1)S(1)}, bf16[8,1,192,768]{3,2,1,0:T(8,128)(2,1)}, u32[]{:S(2)}) copy-start(bf16[8,1,192,768]{3,2,1,0:T(8,128)(2,1)} %get-tuple-element.75) | copy-start | bytes 7077892
  196.4 9.4 %collective-permute-start.15 = (bf16[1,3,48,768]{3,2,1,0:T(8,128)(2,1)S(1)}, bf16[1,3,48,768]{3,2,1,0:T(8,128)(2,1)S(1)}, u32[]{:S(2)}, u32[]{:S(2)}) collective-permute-start(bf16[1,3,48,768]{3,2,1,0:T(8,128)(2,1)S(1)} %add_convert_fusion.15), channel_id=1, source_target_pairs={{0,16},{1,5},{2,18},{3,7},{4,20},{5,1},{6,22},{7,3},{8,24},{9,13},... | collective-permute-start | bytes 663560 | tf_op jit(solution)/shard_map/ppermute | solution.py:534
  207.2 8.6 %collective-permute-start.16 = (bf16[3,48,768]{2,1,0:T(8,128)(2,1)S(1)}, bf16[3,48,768]{2,1,0:T(8,128)(2,1)S(1)}, u32[]{:S(2)}, u32[]{:S(2)}) collective-permute-start(bf16[3,48,768]{2,1,0:T(8,128)(2,1)S(1)} %fusion.1), channel_id=1, source_target_pairs={{0,2},{1,3},{2,0},{3,1},{4,6},{5,7},{6,4},{7,5},{8,10},{9,11},{10,... | collective-permute-start | bytes 663560 | tf_op jit(solution)/shard_map/ppermute | solution.py:534
  209.2 16.2 %collective-permute-start.32 = (bf16[2,1,192,768]{3,2,1,0:T(8,128)(2,1)S(1)}, bf16[2,1,192,768]{3,2,1,0:T(8,128)(2,1)S(1)}, u32[]{:S(2)}, u32[]{:S(2)}) collective-permute-start(bf16[2,1,192,768]{3,2,1,0:T(8,128)(2,1)S(1)} %add_convert_fusion.3), channel_id=1, source_target_pairs={{0,8},{1,17},{2,10},{3,19},{4,12},{5,21},{6,14},{7,23},{8,0},{9,25... | collective-permute-start | bytes 1769480 | tf_op jit(solution)/shard_map/ppermute | solution.py:534
  211.9 32.2 %collective-permute-start.26 = (bf16[2,5,48,768]{3,2,1,0:T(8,128)(2,1)S(1)}, bf16[2,5,48,768]{3,2,1,0:T(8,128)(2,1)S(1)}, u32[]{:S(2)}, u32[]{:S(2)}) collective-permute-start(bf16[2,5,48,768]{3,2,1,0:T(8,128)(2,1)S(1)} %pad_maximum_fusion.6), channel_id=1, source_target_pairs={{0,8},{1,17},{2,10},{3,19},{4,12},{5,21},{6,14},{7,23},{8,0},{9,25... | collective-permute-start | bytes 2211848 | tf_op jit(solution)/shard_map/ppermute | solution.py:534
  215.9 30.4 %collective-permute-start.17 = (bf16[3,48,768]{2,1,0:T(8,128)(2,1)S(1)}, bf16[3,48,768]{2,1,0:T(8,128)(2,1)S(1)}, u32[]{:S(2)}, u32[]{:S(2)}) collective-permute-start(bf16[3,48,768]{2,1,0:T(8,128)(2,1)S(1)} %add_convert_fusion.13), channel_id=1, source_target_pairs={{0,1},{1,0},{2,3},{3,2},{4,5},{5,4},{6,7},{7,6},{8,9},{9,8},{10,11... | collective-permute-start | bytes 663560 | tf_op jit(solution)/shard_map/ppermute | solution.py:534
  226.5 19.9 %collective-permute-start.33 = (bf16[1,1,192,768]{3,2,1,0:T(8,128)(2,1)S(1)}, bf16[1,1,192,768]{3,2,1,0:T(8,128)(2,1)S(1)}, u32[]{:S(2)}, u32[]{:S(2)}) collective-permute-start(bf16[1,1,192,768]{3,2,1,0:T(8,128)(2,1)S(1)} %add_convert_fusion.9), channel_id=1, source_target_pairs={{0,16},{1,5},{2,18},{3,7},{4,20},{5,1},{6,22},{7,3},{8,24},{9,13},... | collective-permute-start | bytes 884744 | tf_op jit(solution)/shard_map/ppermute | solution.py:534
  246.2 11.4 %collective-permute-start.27 = (bf16[1,5,48,768]{3,2,1,0:T(8,128)(2,1)S(1)}, bf16[1,5,48,768]{3,2,1,0:T(8,128)(2,1)S(1)}, u32[]{:S(2)}, u32[]{:S(2)}) collective-permute-start(bf16[1,5,48,768]{3,2,1,0:T(8,128)(2,1)S(1)} %pad_maximum_fusion.7), channel_id=1, source_target_pairs={{0,16},{1,5},{2,18},{3,7},{4,20},{5,1},{6,22},{7,3},{8,24},{9,13},... | collective-permute-start | bytes 1105928 | tf_op jit(solution)/shard_map/ppermute | solution.py:534
  247.5 13.9 %collective-permute-start.34 = (bf16[1,192,768]{2,1,0:T(8,128)(2,1)S(1)}, bf16[1,192,768]{2,1,0:T(8,128)(2,1)S(1)}, u32[]{:S(2)}, u32[]{:S(2)}) collective-permute-start(bf16[1,192,768]{2,1,0:T(8,128)(2,1)S(1)} %fusion), channel_id=1, source_target_pairs={{0,2},{1,3},{2,0},{3,1},{4,6},{5,7},{6,4},{7,5},{8,10},{9,11},{10,... | collective-permute-start | bytes 884744 | tf_op jit(solution)/shard_map/ppermute | solution.py:534
  259.9 7.6 %collective-permute-start.28 = (bf16[5,48,768]{2,1,0:T(8,128)(2,1)S(1)}, bf16[5,48,768]{2,1,0:T(8,128)(2,1)S(1)}, u32[]{:S(2)}, u32[]{:S(2)}) collective-permute-start(bf16[5,48,768]{2,1,0:T(8,128)(2,1)S(1)} %maximum_bitcast_fusion), channel_id=1, source_target_pairs={{0,2},{1,3},{2,0},{3,1},{4,6},{5,7},{6,4},{7,5},{8,10},{9,11},{10,... | collective-permute-start | bytes 1105928 | tf_op jit(solution)/shard_map/ppermute | solution.py:534
  261.5 6.1 %collective-permute-start.35 = (bf16[1,192,768]{2,1,0:T(8,128)(2,1)S(1)}, bf16[1,192,768]{2,1,0:T(8,128)(2,1)S(1)}, u32[]{:S(2)}, u32[]{:S(2)}) collective-permute-start(bf16[1,192,768]{2,1,0:T(8,128)(2,1)S(1)} %add_convert_fusion.7), channel_id=1, source_target_pairs={{0,1},{1,0},{2,3},{3,2},{4,5},{5,4},{6,7},{7,6},{8,9},{9,8},{10,11... | collective-permute-start | bytes 884744 | tf_op jit(solution)/shard_map/ppermute | solution.py:534
  267.6 1.8 collective-permute-start.29
  (13 other events, 50.6 us)
where the time goes:
time: 273 us; the launch traced here: 272 us
  Pallas kernels  104 us (38%)
  waiting for transfers between devices  67.9 us (25%)
  starting transfers between devices  49 us (18%)
  other arithmetic  32.3 us (12%)
  local copies, waits for them, and re-layouts  17.4 us (6%)
    ppermute x19, waiting for transfers between devices, permute(): return lax.ppermute(values, BOTH, pairs(self.n_dp, self.n_seq, partner))  51.9 us
    pallas_call x1, Pallas kernels, ffn_up(): pl.pallas_call(lambda *refs: up_kernel(ROWS, *refs), out_shape=(jax.Shape...  27.6 us
    ppermute x12, starting transfers between devices, exchange(): lax.ppermute(blocks[k], 'seq', [(s, s ^ k) for s in range(n_seq)])  25.9 us
    pallas_call x1, Pallas kernels, attention_forward(): pl.pallas_call(lambda *refs: attn_kernel(ROWS, *refs), out_shape=(low, lo...  22.3 us
    convert_element_type x14, other arithmetic, added(): return total.astype(BF16)  17.9 us
    pallas_call x1, Pallas kernels, attention_back(): pl.pallas_call(lambda *refs: back_kernel(ROWS, *refs), out_shape=(low, lo...  16.4 us
    pallas_call x1, Pallas kernels, ffn_down(): pl.pallas_call(lambda *refs: down_kernel(ROWS, *refs), out_shape=(jax.Sha...  15.2 us
    ppermute x19, starting transfers between devices, permute(): return lax.ppermute(values, BOTH, pairs(self.n_dp, self.n_seq, partner))  15.1 us
  transfers between devices with their start and end apart: 36, of which 14 were waited for; matrix products, arithmetic and copies ran while one was open for 16% of the time, Pallas kernels for 28%

commit v1 on v0

--- a/solution.py
+++ b/solution.py
@@ -15,6 +15,8 @@
 BOTH = ("dp", "seq")
 
 
+LN_ROWS = 256
+
 TAIL = (
     0.11283793300390244, 0.11283480376005173, 0.10392128676176071, 0.08427156507968903, 0.07071308046579361,
     -0.0027973579708486795, 0.08453421294689178, -0.0914449393749237, 0.025129476562142372,
@@ -29,7 +31,7 @@
 
 def gelu_and_slope(x):
     t = 1.0 / (1.0 + (0.4 / math.sqrt(2.0)) * jnp.abs(x))
-    bell = jnp.exp(x * x * -0.5)
+    bell = jnp.exp2(x * x * (-0.5 * math.log2(math.e)))
     poly = TAIL[-1]
     for c in TAIL[-2::-1]:
         poly = poly * t + c
@@ -88,7 +90,7 @@
 
     @pl.when(f == nf - 1)
     def _():
-        step = 32
+        step = LN_ROWS
 
         def body(i, sums):
             rows = pl.ds(pl.multiple_of(i * step, step), step)
@@ -116,7 +118,7 @@
     return pl.BlockSpec(shape, lambda *_: (0,) * len(shape))
 
 
-def ffn_up(n_dp, slots, hat, gain1, shift1, wi, bi, wo, bo, gain2, shift2, cot, ROWS=128):
+def ffn_up(n_dp, slots, hat, gain1, shift1, wi, bi, wo, bo, gain2, shift2, cot, ROWS=512):
     tokens, width = hat.shape
     ff = wi.shape[1]
     nf = ff // width
@@ -158,12 +160,13 @@
                 pltpu.VMEM((tokens, width), BF16),
             ],
         ),
-        compiler_params=pltpu.CompilerParams(vmem_limit_bytes=58 << 20),
+        compiler_params=pltpu.CompilerParams(vmem_limit_bytes=20 << 20),
         name="ffn_up",
     )(slots, hat, gain1, shift1, wi, bi, wo, bo, gain2, shift2, cot)
 
 
-def attn_kernel(ROWS, x, bias, wq, bq, wk, wv, bv, wo, bo, q_out, k_out, v_out, p_out, c_out, hat_out, r_out, acc_s):
+def attn_kernel(x, bias, wq, bq, wk, wv, bv, wo, bo,
+                q_out, k_out, v_out, e_out, inv_out, c_out, hat_out, r_out, acc_s):
     g = pl.program_id(0)
     tokens = x.shape[0]
     xs = x[...]
@@ -173,24 +176,26 @@
     q_out[...] = qs
     k_out[...] = ks
     v_out[...] = vs
-    lane = lax.broadcasted_iota(jnp.int32, (1, 2 * HEAD_DIM), 1) < HEAD_DIM
+    lanes = lax.broadcasted_iota(jnp.int32, (1, 2 * HEAD_DIM), 1)
+    low = lanes < HEAD_DIM
+    mine = (low, jnp.logical_not(low))
     nil = jnp.zeros((), BF16)
+    one = jnp.ones((), BF16)
     for pair in range(qs.shape[1] // (2 * HEAD_DIM)):
         cols = slice(pair * 2 * HEAD_DIM, (pair + 1) * 2 * HEAD_DIM)
         q2, k2, v2 = qs[:, cols], ks[:, cols], vs[:, cols]
-        mine = (lane, jnp.logical_not(lane))
-        vm = [jnp.where(m, v2, nil) for m in mine]
-        for r in range(0, tokens, ROWS):
-            rows = slice(r, r + ROWS)
-            total = None
-            for h in range(2):
-                s = dot(jnp.where(mine[h], q2[rows], nil), k2, (1, 1)) + bias[...]
-                e = jnp.exp(s - jnp.max(s, -1, keepdims=True))
-                p = (e * (1.0 / jnp.sum(e, -1, keepdims=True))).astype(BF16)
-                p_out[pair * 2 + h, rows] = p
-                part = dot(p, vm[h])
-                total = part if total is None else total + part
-            c_out[rows, cols] = total.astype(BF16)
+        sums = []
+        for h in range(2):
+            spare = lanes == (HEAD_DIM if h == 0 else 0)
+            qa = jnp.where(mine[h], q2, jnp.where(spare, one, nil))
+            ka = jnp.where(mine[h], k2, jnp.where(spare, bias[...], nil))
+            s = dot(qa, ka, (1, 1))
+            e = jnp.exp(s - jnp.max(s, -1, keepdims=True)).astype(BF16)
+            e_out[pair * 2 + h] = e
+            sums.append(dot(e, jnp.where(mine[h], v2, one)))
+        inv = 1.0 / pltpu.roll(jnp.where(low, sums[1], sums[0]), HEAD_DIM, 1)
+        inv_out[:, cols] = inv
+        c_out[:, cols] = (jnp.where(low, sums[0], sums[1]) * inv).astype(BF16)
     more = dot(c_out[...], wo[...])
 
     @pl.when(g == 0)
@@ -203,7 +208,7 @@
 
     @pl.when(g == pl.num_programs(0) - 1)
     def _():
-        step = 32
+        step = LN_ROWS
 
         def body(i, _):
             rows = pl.ds(pl.multiple_of(i * step, step), step)
@@ -215,7 +220,7 @@
         lax.fori_loop(0, tokens // step, body, 0)
 
 
-def attention_forward(x, bias, wq, bq, wk, wv, bv, wo, bo, ROWS=128):
+def attention_forward(x, bias, wq, bq, wk, wv, bv, wo, bo):
     tokens, width = x.shape
     group = 4 * HEAD_DIM
     n = width // group
@@ -223,27 +228,28 @@
     col = lambda rows: pl.BlockSpec((rows, group), lambda g: (0, g))
     low = jax.ShapeDtypeStruct((tokens, width), BF16)
     return pl.pallas_call(
-        lambda *refs: attn_kernel(ROWS, *refs),
+        attn_kernel,
         out_shape=(
             low, low, low,
             jax.ShapeDtypeStruct((heads, tokens, tokens), BF16),
+            jax.ShapeDtypeStruct((tokens, width), F32),
             low,
             jax.ShapeDtypeStruct((tokens, width), F32),
             jax.ShapeDtypeStruct((tokens, 1), F32),
         ),
         grid=(n,),
         in_specs=[
-            whole((tokens, width)), whole((1, tokens)),
+            whole((tokens, width)), whole((tokens, 2 * HEAD_DIM)),
             col(width), col(1), col(width), col(width), col(1),
             pl.BlockSpec((group, width), lambda g: (g, 0)), whole((1, width)),
         ],
         out_specs=[
             col(tokens), col(tokens), col(tokens),
             pl.BlockSpec((4, tokens, tokens), lambda g: (g, 0, 0)),
-            col(tokens), whole((tokens, width)), whole((tokens, 1)),
+            col(tokens), col(tokens), whole((tokens, width)), whole((tokens, 1)),
         ],
         scratch_shapes=[pltpu.VMEM((tokens, width), F32)],
-        compiler_params=pltpu.CompilerParams(vmem_limit_bytes=58 << 20),
+        compiler_params=pltpu.CompilerParams(vmem_limit_bytes=14 << 20),
         name="attention_forward",
     )(x, bias, wq, bq, wk, wv, bv, wo, bo)
 
@@ -267,7 +273,7 @@
     put_units(keep, send, slots, 0, dot(nt_s[...], gi[...]), f)
 
 
-def ffn_down(n_dp, slots, gpre, slope, hat, gain1, shift1, wo, ROWS=128):
+def ffn_down(n_dp, slots, gpre, slope, hat, gain1, shift1, wo, ROWS=512):
     tokens, width = hat.shape
     ff = wo.shape[0]
     nf = ff // width
@@ -300,7 +306,7 @@
                 pltpu.VMEM((width, tokens), BF16),
             ],
         ),
-        compiler_params=pltpu.CompilerParams(vmem_limit_bytes=58 << 20),
+        compiler_params=pltpu.CompilerParams(vmem_limit_bytes=8 << 20),
         name="ffn_down",
     )(slots, gpre, slope, hat, gain1, shift1, wo)
 
@@ -320,7 +326,7 @@
 
     @pl.when(f == pl.num_programs(0) - 1)
     def _():
-        step = 32
+        step = LN_ROWS
 
         def body(i, sums):
             rows = pl.ds(pl.multiple_of(i * step, step), step)
@@ -367,16 +373,13 @@
             out_specs=[full, full, whole((8, width)), whole(shape), whole(shape)],
             scratch_shapes=[pltpu.VMEM((tokens, width), F32), pltpu.VMEM((tokens, width), BF16)],
         ),
-        compiler_params=pltpu.CompilerParams(vmem_limit_bytes=58 << 20),
+        compiler_params=pltpu.CompilerParams(vmem_limit_bytes=12 << 20),
         name="middle",
     )(slots, gpre, gi, hat, r1, gain1, wi, wa, ctx)
 
 
-def back_kernel(
-    ROWS, slots, x, q, k, v, c, gc, p, dq, dk, dv, qb, vb, keep, send, xt_s, ds_s
-):
+def back_kernel(slots, x, q, k, v, c, gc, inv, e, dq, dk, dv, qb, vb, keep, send, xt_s):
     g = pl.program_id(0)
-    tokens = x.shape[0]
     scale = 1.0 / math.sqrt(HEAD_DIM)
     pair_width = 2 * HEAD_DIM
 
@@ -384,30 +387,28 @@
     def _():
         xt_s[...] = x[...].T
 
-    lane = lax.broadcasted_iota(jnp.int32, (1, pair_width), 1) < HEAD_DIM
-    mine = (lane, jnp.logical_not(lane))
+    low = lax.broadcasted_iota(jnp.int32, (1, pair_width), 1) < HEAD_DIM
+    mine = (low, jnp.logical_not(low))
     nil = jnp.zeros((), BF16)
     for pair in range(q.shape[1] // pair_width):
         cols = slice(pair * pair_width, (pair + 1) * pair_width)
-        q2, k2, v2, c2, g2 = q[:, cols], k[:, cols], v[:, cols], c[:, cols], gc[:, cols]
+        q2, k2, v2 = q[:, cols], k[:, cols], v[:, cols]
+        scaled = gc[:, cols].astype(F32) * inv[:, cols]
+        prod = scaled * c[:, cols].astype(F32)
+        g2 = scaled.astype(BF16)
         qt, gt = q2.T, g2.T
-        prod = g2.astype(F32) * c2.astype(F32)
-        dkt, dvt = [], []
-        for r in range(0, tokens, ROWS):
-            rows = slice(r, r + ROWS)
-            total = None
-            for h in range(2):
-                delta = jnp.sum(jnp.where(mine[h], prod[rows], 0.0), -1, keepdims=True)
-                dp = dot(jnp.where(mine[h], g2[rows], nil), v2, (1, 1))
-                ds = (p[pair * 2 + h, rows].astype(F32) * (dp - delta)).astype(BF16)
-                ds_s[h, rows] = ds
-                part = dot(ds, jnp.where(mine[h], k2, nil))
-                total = part if total is None else total + part
-            dq[rows, cols] = (total * scale).astype(BF16)
+        dkt, dvt, total = [], [], None
         for h in range(2):
             rows = slice(h * HEAD_DIM, (h + 1) * HEAD_DIM)
-            dvt.append(dot(gt[rows], p[pair * 2 + h]))
-            dkt.append(dot(qt[rows], ds_s[h]))
+            eh = e[pair * 2 + h]
+            delta = jnp.sum(jnp.where(mine[h], prod, 0.0), -1, keepdims=True)
+            dp = dot(jnp.where(mine[h], g2, nil), v2, (1, 1))
+            ds = (eh.astype(F32) * (dp - delta)).astype(BF16)
+            part = dot(ds, jnp.where(mine[h], k2, nil))
+            total = part if total is None else total + part
+            dvt.append(dot(gt[rows], eh))
+            dkt.append(dot(qt[rows], ds))
+        dq[:, cols] = (total * scale).astype(BF16)
         dv[:, cols] = jnp.concatenate(dvt, 0).astype(BF16).T
         dk[:, cols] = jnp.concatenate(dkt, 0).astype(BF16).T
     qb[...] = jnp.sum(fold8(dq[...].astype(F32)), 0, keepdims=True)
@@ -418,7 +419,7 @@
         put_units(keep, send, slots, 0, dot(xt_s[...], grad[...]), n, cols)
 
 
-def attention_back(n_dp, slots, x, q, k, v, c, gc, p, ROWS=128):
+def attention_back(n_dp, slots, x, q, k, v, c, gc, inv, e):
     tokens, width = x.shape
     group = 4 * HEAD_DIM
     col = pl.BlockSpec((tokens, group), lambda g, s: (0, g))
@@ -428,22 +429,19 @@
     shape = (n_dp, 3, width // (2 * n_dp), width)
     units = jax.ShapeDtypeStruct(shape, BF16)
     return pl.pallas_call(
-        lambda *refs: back_kernel(ROWS, *refs),
+        back_kernel,
         out_shape=(low, low, low, vector, vector, units, units),
         grid_spec=pltpu.PrefetchScalarGridSpec(
             num_scalar_prefetch=1,
             grid=(width // group,),
-            in_specs=[whole((tokens, width)), col, col, col, col, col,
+            in_specs=[whole((tokens, width)), col, col, col, col, col, col,
                       pl.BlockSpec((4, tokens, tokens), lambda g, s: (g, 0, 0))],
             out_specs=[col, col, col, row, row, whole(shape), whole(shape)],
-            scratch_shapes=[
-                pltpu.VMEM((width, tokens), BF16),
-                pltpu.VMEM((2, tokens, tokens), BF16),
-            ],
+            scratch_shapes=[pltpu.VMEM((width, tokens), BF16)],
         ),
-        compiler_params=pltpu.CompilerParams(vmem_limit_bytes=58 << 20),
+        compiler_params=pltpu.CompilerParams(vmem_limit_bytes=12 << 20),
         name="attention_back",
-    )(slots, x, q, k, v, c, gc, p)
+    )(slots, x, q, k, v, c, gc, inv, e)
 
 
 def input_kernel(gmid, dq, dk, dv, wq, wk, wv, out):
@@ -454,16 +452,17 @@
 
 def input_gradient(gmid, dq, dk, dv, wq, wk, wv):
     tokens, width = gmid.shape
-    rows = tokens // 4
-    act = pl.BlockSpec((rows, width), lambda i: (i, 0))
-    weight = whole((width, width))
+    group = 256
+    act = whole((tokens, width))
+    col = pl.BlockSpec((tokens, group), lambda i: (0, i))
+    weight = pl.BlockSpec((group, width), lambda i: (i, 0))
     return pl.pallas_call(
         input_kernel,
         out_shape=jax.ShapeDtypeStruct((tokens, width), BF16),
-        grid=(4,),
-        in_specs=[act, act, act, act, weight, weight, weight],
-        out_specs=act,
-        compiler_params=pltpu.CompilerParams(vmem_limit_bytes=58 << 20),
+        grid=(width // group,),
+        in_specs=[col, act, act, act, weight, weight, weight],
+        out_specs=col,
+        compiler_params=pltpu.CompilerParams(vmem_limit_bytes=4 << 20),
         name="input_gradient",
     )(gmid, dq, dk, dv, wq, wk, wv)
 
@@ -493,7 +492,7 @@
 
 def bit_orders(n_dp):
     bits = list(range(n_dp.bit_length() - 1))
-    return bits, bits[1:] + bits[:1]
+    return bits, bits[1::-1] + bits[2:]
 
 
 def slot_table(n_dp, d, s):
@@ -621,9 +620,10 @@
     cot = to_passage(after(cotangent, x))
     spots = lax.iota(jnp.int32, tokens)
     spots = ((spots // slice_rows) ^ s) * slice_rows + spots % slice_rows
-    bias = row(jnp.where(spots < pick(lengths, s), 0.0, MASKED))
-
-    query, key, value, probs, context, hat, r1 = attention_forward(
+    bias = jnp.where(spots < pick(lengths, s), 0.0, MASKED).astype(BF16)
+    bias = jnp.broadcast_to(bias.reshape(tokens, 1), (tokens, 2 * HEAD_DIM))
+
+    query, key, value, exps, inverse, context, hat, r1 = attention_forward(
         x, bias, query_weight, row(query_bias), key_weight, value_weight, row(value_bias),
         out_weight, row(out_bias),
     )
@@ -645,7 +645,7 @@
     a2 = outer.step()
     b1 = inner.step()
     grad_query, grad_key, grad_value, qbias, vbias, *attn_units = attention_back(
-        n_dp, slots, x, query, key, value, context, grad_context, probs,
+        n_dp, slots, x, query, key, value, context, grad_context, inverse, exps,
     )
     attn = Halving(*attn_units, n_dp, n_seq)
     input_low = input_gradient(

time: 273 us -> 231 us (0.85)
  Pallas kernels: 104 us -> 59.9 us
  starting transfers between devices: 49 us -> 34.9 us
  local copies, waits for them, and re-layouts: 17.4 us -> 30.2 us
  other arithmetic: 32.3 us -> 35.7 us
    pallas_call x2, Pallas kernels: 38.7 us -> 21.9 us  [the longest x1 12.2 us: attention_back(): pl.pallas_call(back_kernel, out_shape=(low, low, low, vector, vector, uni...]
    ppermute x12, starting transfers between devices: 25.9 us -> 9.99 us  [exchange(): lax.ppermute(blocks[k], 'seq', [(s, s ^ k) for s in range(n_seq)])]
    unnamed x50 -> x90, local copies, waits for them, and re-layouts: 1.62 us -> 13.9 us
    ppermute x12, waiting for transfers between devices: 8.34 us -> 18.2 us  [exchange(): lax.ppermute(blocks[k], 'seq', [(s, s ^ k) for s in range(n_seq)])]
    pallas_call x1, Pallas kernels: 27.6 us -> 19.2 us  [ffn_up(): pl.pallas_call(lambda *refs: up_kernel(ROWS, *refs), out_shape=(jax.Shape...]
    ppermute x19, waiting for transfers between devices: 51.9 us -> 44.1 us  [permute(): return lax.ppermute(values, BOTH, pairs(self.n_dp, self.n_seq, partner))]
    pallas_call x1, Pallas kernels: 13.9 us -> 7.45 us  [middle(): pl.pallas_call(mid_kernel, out_shape=(jax.ShapeDtypeStruct((tokens, width...]
    pallas_call x1, Pallas kernels: 15.2 us -> 8.74 us  [ffn_down(): pl.pallas_call(lambda *refs: down_kernel(ROWS, *refs), out_shape=(jax.Sha...]
  transfers between devices with their start and end apart: 36 -> 36, of which waited for: 14 -> 17; matrix products, arithmetic and copies ran while one was open for 16% -> 20% of each run, Pallas kernels for 28% -> 18%
where the time goes in v1:
time: 231 us; the launch traced here: 230 us
  waiting for transfers between devices  67.7 us (29%)
  Pallas kernels  59.9 us (26%)
  other arithmetic  35.7 us (15%)
  starting transfers between devices  34.9 us (15%)
  local copies, waits for them, and re-layouts  30.2 us (13%)
    ppermute x19, waiting for transfers between devices, permute(): return lax.ppermute(values, BOTH, pairs(self.n_dp, self.n_seq, partner))  44.1 us
    convert_element_type x14, other arithmetic, added(): return total.astype(BF16)  20.1 us
    pallas_call x1, Pallas kernels, ffn_up(): pl.pallas_call(lambda *refs: up_kernel(ROWS, *refs), out_shape=(jax.Shape...  19.2 us
    ppermute x12, waiting for transfers between devices, exchange(): lax.ppermute(blocks[k], 'seq', [(s, s ^ k) for s in range(n_seq)])  18.2 us
    ppermute x19, starting transfers between devices, permute(): return lax.ppermute(values, BOTH, pairs(self.n_dp, self.n_seq, partner))  17.3 us
    unnamed x90, local copies, waits for them, and re-layouts  13.9 us
    pallas_call x1, Pallas kernels, attention_back(): pl.pallas_call(back_kernel, out_shape=(low, low, low, vector, vector, uni...  12.2 us
    ppermute x12, starting transfers between devices, exchange(): lax.ppermute(blocks[k], 'seq', [(s, s ^ k) for s in range(n_seq)])  9.99 us
  transfers between devices with their start and end apart: 36, of which 17 were waited for; matrix products, arithmetic and copies ran while one was open for 20% of the time, Pallas kernels for 18%

profile of v1, /device:TPU:0, one launch (start us, length us, event | category | flops | bytes accessed | tf_op | source)
XLA Modules:
  0.0 229.9 jit_solution(16858132202821780819)
XLA Ops:
  0.8 2.0 dynamic-slice_bitcast_fusion.7
  3.3 2.5 %collective-permute-start.1 = (bf16[128,768]{1,0:T(8,128)(2,1)S(1)}, bf16[128,768]{1,0:T(8,128)(2,1)S(1)}, u32[]{:S(2)}, u32[]{:S(2)}) collective-permute-start(bf16[128,768]{1,0:T(8,128)(2,1)S(1)} %get-tuple-element.108), channel_id=1, source_target_pairs={{0,2},{1,3},{2,0},{3,1},{4,6},{5,7},{6,4},{7,5},{8,10},{9,11},{10,... | collective-permute-start | bytes 589832 | tf_op jit(solution)/shard_map/ppermute | solution.py:489
  7.0 4.5 %collective-permute-done.1 = bf16[128,768]{1,0:T(8,128)(2,1)S(1)} collective-permute-done((bf16[128,768]{1,0:T(8,128)(2,1)S(1)}, bf16[128,768]{1,0:T(8,128)(2,1)S(1)}, u32[]{:S(2)}, u32[]{:S(2)}) %collective-permute-start.1) | collective-permute-done | bytes 196640 | tf_op jit(solution)/shard_map/ppermute | solution.py:489
  11.6 4.0 %collective-permute-done.2 = bf16[128,768]{1,0:T(8,128)(2,1)} collective-permute-done((bf16[128,768]{1,0:T(8,128)(2,1)S(1)}, bf16[128,768]{1,0:T(8,128)(2,1)}, u32[]{:S(2)}, u32[]{:S(2)}) %collective-permute-start.2) | collective-permute-done | bytes 196640 | tf_op jit(solution)/shard_map/ppermute | solution.py:489
  16.7 1.6 dynamic-slice_bitcast_fusion.3
  18.4 1.6 collective-permute-start.4
  22.3 1.3 copy-done.6
  23.6 9.6 %attention_forward.1 = (bf16[512,768]{1,0:T(8,128)(2,1)S(1)}, bf16[512,768]{1,0:T(8,128)(2,1)S(1)}, bf16[512,768]{1,0:T(8,128)(2,1)S(1)}, bf16[12,512,512]{2,1,0...) custom-call(bf16[512,768]{1,0:T(8,128)(2,1)S(1)} %pad_maximum_fusion, ...), custom_call_target="tpu_custom_call" | custom-call | tf_op jit(solution)/shard_map/attention_forward/pallas_call | solution.py:230
  34.0 19.2 %ffn_up.1 = (bf16[512,768]{1,0:T(8,128)(2,1)S(1)}, bf16[512,3072]{1,0:T(8,128)(2,1)S(1)}, f32[512,768]{1,0:T(8,128)S(1)}, f32[8,768]{1,0:T(8,128)S(1)}, bf16[8,1...) custom-call(s32[17]{0:T(128)S(1)} %pad_add_fusion.refs_0_.slots, ...), custom_call_target="tpu_custom_call" | custom-call | tf_op jit(solution)/shard_map/ffn_up/pallas_call | solution.py:128
  53.5 8.7 %ffn_down.1 = (bf16[512,3072]{1,0:T(8,128)(2,1)S(1)}, f32[1,3072]{1,0:T(1,128)S(1)}, bf16[8,4,48,768]{3,2,1,0:T(8,128)(2,1)S(1)}, bf16[8,4,48,768]{3,2,1,0:T(8,128)(2,1)}) custom-call(s32[17]{0:T(128)S(1)} %pad_add_fusion.refs_0_.slots, f32[512,768]{1,0:T(8,128)S(1)} %get-tuple-element.51.refs_1_.gpre, bf16[512,3072]{1,0:T(8,128)(2,1)S(1)} %get-tuple-element.52.refs_2_, ...), custom_call_target="tpu_custom_call" | custom-call | tf_op jit(solution)/shard_map/ffn_down/pallas_call | solution.py:285
  62.3 7.4 %middle.1 = (f32[512,768]{1,0:T(8,128)S(1)}, bf16[512,768]{1,0:T(8,128)(2,1)S(1)}, f32[8,768]{1,0:T(8,128)S(1)}, bf16[8,1,48,768]{3,2,1,0:T(8,128)(2,1)S(1)}, bf16[8,1,48,768]{3,2,1,0:T(8,128)(2,1)S(1)}) custom-call(s32[17]{0:T(128)S(1)} %pad_add_fusion.refs_0_.slots, f32[512,768]{1,0:T(8,128)S(1)} %get-tuple-element.51.refs_1_.gpre, ...), custom_call_target="tpu_custom_call" | custom-call | tf_op jit(solution)/shard_map/middle/pallas_call | solution.py:355
  71.8 12.2 %attention_back.1 = (bf16[512,768]{1,0:T(8,128)(2,1)S(1)}, bf16[512,768]{1,0:T(8,128)(2,1)S(1)}, bf16[512,768]{1,0:T(8,128)(2,1)S(1)}, f32[1,768]{1,0:T(1,128)S(...) custom-call(s32[17]{0:T(128)S(1)} %pad_add_fusion.refs_0_.slots, ...), custom_call_target="tpu_custom_call" | custom-call | tf_op jit(solution)/shard_map/attention_back/pallas_call | solution.py:431
  89.5 1.3 reduce.3
  91.5 1.3 slice.348
  92.8 2.0 concatenate.47
  95.0 1.3 collective-permute-done.18
  97.1 1.6 collective-permute-start.19
  98.7 2.4 %collective-permute-done.19 = f32[12,768]{1,0:T(8,128)S(1)} collective-permute-done((f32[12,768]{1,0:T(8,128)S(1)}, f32[12,768]{1,0:T(8,128)S(1)}, u32[]{:S(2)}, u32[]{:S(2)}) %collective-permute-start.19) | collective-permute-done | bytes 36896 | tf_op jit(solution)/shard_map/ppermute | solution.py:572
  101.8 1.6 collective-permute-start.20
  103.4 1.4 copy-done.17
  108.2 2.6 %input_gradient.1 = bf16[512,768]{1,0:T(8,128)(2,1)S(1)} custom-call(f32[512,768]{1,0:T(8,128)S(1)} %copy-done.17, bf16[512,768]{1,0:T(8,128)(2,1)S(1)} %copy-done.21, bf16[512,768]{1,0:T(8,128)(2,1)S(1)} %copy-done.23, bf16[512,768]{1,0:T(8,128)(2,1)S(1)} %copy-done.25, bf16[768,768]{1,0:T(8,128)(2,1)S(1)} %copy-done.3, bf16[768,768]{1,0:T(8,128)(2,1)S(1)} %copy-done.5, ...), custom_call_target="tpu_custom_call" | custom-call | tf_op jit(solution)/shard_map/input_gradient/pallas_call | solution.py:459
  111.8 1.6 collective-permute-start.21
  114.2 1.7 collective-permute-done.21
  115.9 1.5 collective-permute-start.10
  117.4 2.7 %collective-permute-start.22 = (f32[12,768]{1,0:T(8,128)S(1)}, f32[12,768]{1,0:T(8,128)S(1)}, u32[]{:S(2)}, u32[]{:S(2)}) collective-permute-start(f32[12,768]{1,0:T(8,128)S(1)} %add.339), channel_id=1, source_target_pairs={{0,16},{1,17},{2,18},{3,19},{4,20},{5,21},{6,22},{7,23},{8,24},{9,... | collective-permute-start | bytes 110600 | tf_op jit(solution)/shard_map/ppermute | solution.py:572
  120.1 1.5 add_convert_fusion.2
  123.3 2.7 %add_convert_fusion = bf16[4,1,192,768]{3,2,1,0:T(8,128)(2,1)} fusion(bf16[8,1,192,768]{3,2,1,0:T(8,128)(2,1)} %collective-permute-done.30, bf16[8,1,192,768]{3,2,1,0:T(8,128)(2,1)S(1)} %copy-done.12), kind=kLoop, calls=%fused_computation | loop fusion | flops 2359296 | bytes 3538944 | tf_op jit(solution)/shard_map/convert_element_type | solution.py:519
  126.1 1.5 collective-permute-start.31
  127.6 1.6 add_convert_fusion.1
  130.9 3.9 %collective-permute-done.13 = bf16[4,3,48,768]{3,2,1,0:T(8,128)(2,1)S(1)} collective-permute-done((bf16[4,3,48,768]{3,2,1,0:T(8,128)(2,1)S(1)}, bf16[4,3,48,768]{3,2,1,0:T(8,128)(2,1)S(1)}, u32[]{:S(2)}, u32[]{:S(2)}) %collective-permute-start.13) | collective-permute-done | bytes 884768 | tf_op jit(solution)/shard_map/ppermute | solution.py:533
  134.8 2.2 add_convert_fusion.5
  137.0 1.6 collective-permute-start.14
  140.6 1.3 dynamic_slice.45
  145.1 4.2 %collective-permute-done.9 = bf16[128,768]{1,0:T(8,128)(2,1)S(1)} collective-permute-done((bf16[128,768]{1,0:T(8,128)(2,1)S(1)}, bf16[128,768]{1,0:T(8,128)(2,1)S(1)}, u32[]{:S(2)}, u32[]{:S(2)}) %collective-permute-start.9) | collective-permute-done | bytes 196640 | tf_op jit(solution)/shard_map/ppermute | solution.py:489
  151.1 1.4 add_convert_fusion.15
  153.8 4.6 %collective-permute-done.7 = bf16[128,768]{1,0:T(8,128)(2,1)S(1)} collective-permute-done((bf16[128,768]{1,0:T(8,128)(2,1)}, bf16[128,768]{1,0:T(8,128)(2,1)S(1)}, u32[]{:S(2)}, u32[]{:S(2)}) %collective-permute-start.7) | collective-permute-done | bytes 196640 | tf_op jit(solution)/shard_map/ppermute | solution.py:489
  158.4 1.3 select_bitcast_fusion.5
  159.7 5.2 %collective-permute-done.15 = bf16[1,3,48,768]{3,2,1,0:T(8,128)(2,1)S(1)} collective-permute-done((bf16[1,3,48,768]{3,2,1,0:T(8,128)(2,1)S(1)}, bf16[1,3,48,768]{3,2,1,0:T(8,128)(2,1)S(1)}, u32[]{:S(2)}, u32[]{:S(2)}) %collective-permute-start.15) | collective-permute-done | bytes 221216 | tf_op jit(solution)/shard_map/ppermute | solution.py:533
  164.9 1.4 fusion.1
  167.4 1.5 add_convert_fusion.3
  169.0 1.5 add_convert_fusion.4
  171.6 2.0 collective-permute-start.26
  175.6 2.3 %collective-permute-start.17 = (bf16[3,48,768]{2,1,0:T(8,128)(2,1)S(1)}, bf16[3,48,768]{2,1,0:T(8,128)(2,1)S(1)}, u32[]{:S(2)}, u32[]{:S(2)}) collective-permute-start(bf16[3,48,768]{2,1,0:T(8,128)(2,1)S(1)} %add_convert_fusion.13), channel_id=1, source_target_pairs={{0,1},{1,0},{2,3},{3,2},{4,5},{5,4},{6,7},{7,6},{8,9},{9,8},{10,11... | collective-permute-start | bytes 663560 | tf_op jit(solution)/shard_map/ppermute | solution.py:533
  180.0 2.3 collective-permute-start.33
  182.3 5.5 %collective-permute-done.26 = bf16[2,5,48,768]{3,2,1,0:T(8,128)(2,1)S(1)} collective-permute-done((bf16[2,5,48,768]{3,2,1,0:T(8,128)(2,1)S(1)}, bf16[2,5,48,768]{3,2,1,0:T(8,128)(2,1)S(1)}, u32[]{:S(2)}, u32[]{:S(2)}) %collective-permute-start.26) | collective-permute-done | bytes 737312 | tf_op jit(solution)/shard_map/ppermute | solution.py:533
  191.1 12.9 %collective-permute-done.33 = bf16[1,1,192,768]{3,2,1,0:T(8,128)(2,1)S(1)} collective-permute-done((bf16[1,1,192,768]{3,2,1,0:T(8,128)(2,1)S(1)}, bf16[1,1,192,768]{3,2,1,0:T(8,128)(2,1)S(1)}, u32[]{:S(2)}, u32[]{:S(2)}) %collective-permute-start.33) | collective-permute-done | bytes 294944 | tf_op jit(solution)/shard_map/ppermute | solution.py:533
  206.4 5.5 %collective-permute-done.27 = bf16[1,5,48,768]{3,2,1,0:T(8,128)(2,1)S(1)} collective-permute-done((bf16[1,5,48,768]{3,2,1,0:T(8,128)(2,1)S(1)}, bf16[1,5,48,768]{3,2,1,0:T(8,128)(2,1)S(1)}, u32[]{:S(2)}, u32[]{:S(2)}) %collective-permute-start.27) | collective-permute-done | bytes 368672 | tf_op jit(solution)/shard_map/ppermute | solution.py:533
  216.2 9.5 %collective-permute-done.28 = bf16[5,48,768]{2,1,0:T(8,128)(2,1)S(1)} collective-permute-done((bf16[5,48,768]{2,1,0:T(8,128)(2,1)S(1)}, bf16[5,48,768]{2,1,0:T(8,128)(2,1)S(1)}, u32[]{:S(2)}, u32[]{:S(2)}) %collective-permute-start.28) | collective-permute-done | bytes 368672 | tf_op jit(solution)/shard_map/ppermute | solution.py:533
  (192 shorter events, 53.2 us)
Async XLA Ops:
  0.8 20.3 %copy-start.3 = (bf16[768,768]{1,0:T(8,128)(2,1)S(1)}, bf16[768,768]{1,0:T(8,128)(2,1)}, u32[]{:S(2)}) copy-start(bf16[768,768]{1,0:T(8,128)(2,1)} %wq.3) | copy-start | bytes 3538948
  2.8 4.2 %collective-permute-start = (bf16[128,768]{1,0:T(8,128)(2,1)}, bf16[128,768]{1,0:T(8,128)(2,1)S(1)}, u32[]{:S(2)}, u32[]{:S(2)}) collective-permute-start(bf16[128,768]{1,0:T(8,128)(2,1)} %get-tuple-element.106), channel_id=1, source_target_pairs={{0,1},{1,0},{2,3},{3,2},{4,5},{5,4},{6,7},{7,6},{8,9},{9,8},{10,11... | collective-permute-start | bytes 589832 | tf_op jit(solution)/shard_map/ppermute | solution.py:489
  3.3 8.3 %collective-permute-start.1 = (bf16[128,768]{1,0:T(8,128)(2,1)S(1)}, bf16[128,768]{1,0:T(8,128)(2,1)S(1)}, u32[]{:S(2)}, u32[]{:S(2)}) collective-permute-start(bf16[128,768]{1,0:T(8,128)(2,1)S(1)} %get-tuple-element.108), channel_id=1, source_target_pairs={{0,2},{1,3},{2,0},{3,1},{4,6},{5,7},{6,4},{7,5},{8,10},{9,11},{10,... | collective-permute-start | bytes 589832 | tf_op jit(solution)/shard_map/ppermute | solution.py:489
  5.8 9.7 %collective-permute-start.2 = (bf16[128,768]{1,0:T(8,128)(2,1)S(1)}, bf16[128,768]{1,0:T(8,128)(2,1)}, u32[]{:S(2)}, u32[]{:S(2)}) collective-permute-start(bf16[128,768]{1,0:T(8,128)(2,1)S(1)} %get-tuple-element.107), channel_id=1, source_target_pairs={{0,3},{1,2},{2,1},{3,0},{4,7},{5,6},{6,5},{7,4},{8,11},{9,10},{10,... | collective-permute-start | bytes 589832 | tf_op jit(solution)/shard_map/ppermute | solution.py:489
  6.7 14.3 %copy-start.2 = (bf16[768,768]{1,0:T(8,128)(2,1)S(1)}, bf16[768,768]{1,0:T(8,128)(2,1)}, u32[]{:S(2)}) copy-start(bf16[768,768]{1,0:T(8,128)(2,1)} %wa.1) | copy-start | bytes 3538948
  15.5 17.8 %copy-start.1 = (bf16[768,3072]{1,0:T(8,128)(2,1)S(1)}, bf16[768,3072]{1,0:T(8,128)(2,1)}, u32[]{:S(2)}) copy-start(bf16[768,3072]{1,0:T(8,128)(2,1)} %wi.1) | copy-start | bytes 14155780
  18.2 15.0 %collective-permute-start.3 = (bf16[128,768]{1,0:T(8,128)(2,1)S(1)}, bf16[128,768]{1,0:T(8,128)(2,1)S(1)}, u32[]{:S(2)}, u32[]{:S(2)}) collective-permute-start(bf16[128,768]{1,0:T(8,128)(2,1)S(1)} %get-tuple-element.104), channel_id=1, source_target_pairs={{0,1},{1,0},{2,3},{3,2},{4,5},{5,4},{6,7},{7,6},{8,9},{9,8},{10,11... | collective-permute-start | bytes 589832 | tf_op jit(solution)/shard_map/ppermute | solution.py:489
  18.4 14.9 %collective-permute-start.4 = (bf16[128,768]{1,0:T(8,128)(2,1)S(1)}, bf16[128,768]{1,0:T(8,128)(2,1)S(1)}, u32[]{:S(2)}, u32[]{:S(2)}) collective-permute-start(bf16[128,768]{1,0:T(8,128)(2,1)S(1)} %get-tuple-element.103), channel_id=1, source_target_pairs={{0,2},{1,3},{2,0},{3,1},{4,6},{5,7},{6,4},{7,5},{8,10},{9,11},{10,... | collective-permute-start | bytes 589832 | tf_op jit(solution)/shard_map/ppermute | solution.py:489
  20.0 13.2 %collective-permute-start.5 = (bf16[128,768]{1,0:T(8,128)(2,1)S(1)}, bf16[128,768]{1,0:T(8,128)(2,1)S(1)}, u32[]{:S(2)}, u32[]{:S(2)}) collective-permute-start(bf16[128,768]{1,0:T(8,128)(2,1)S(1)} %get-tuple-element.102), channel_id=1, source_target_pairs={{0,3},{1,2},{2,1},{3,0},{4,7},{5,6},{6,5},{7,4},{8,11},{9,10},{10,... | collective-permute-start | bytes 589832 | tf_op jit(solution)/shard_map/ppermute | solution.py:489
  23.6 9.8 %copy-start = (bf16[3072,768]{1,0:T(8,128)(2,1)S(1)}, bf16[3072,768]{1,0:T(8,128)(2,1)}, u32[]{:S(2)}) copy-start(bf16[3072,768]{1,0:T(8,128)(2,1)} %refs_6_.3) | copy-start | bytes 14155780
  53.1 9.1 %copy-start.18 = (bf16[512,768]{1,0:T(8,128)(2,1)}, bf16[512,768]{1,0:T(8,128)(2,1)S(1)}, u32[]{:S(2)}) copy-start(bf16[512,768]{1,0:T(8,128)(2,1)S(1)} %get-tuple-element.50) | copy-start | bytes 2359300
  53.1 9.1 %copy-start.30 = (f32[8,768]{1,0:T(8,128)}, f32[8,768]{1,0:T(8,128)S(1)}, u32[]{:S(2)}) copy-start(f32[8,768]{1,0:T(8,128)S(1)} %get-tuple-element.68) | copy-start | bytes 73732
  53.1 70.1 %collective-permute-start.30 = (bf16[8,1,192,768]{3,2,1,0:T(8,128)(2,1)}, bf16[8,1,192,768]{3,2,1,0:T(8,128)(2,1)}, u32[]{:S(2)}, u32[]{:S(2)}) collective-permute-start(bf16[8,1,192,768]{3,2,1,0:T(8,128)(2,1)} %get-tuple-element.78), channel_id=1, source_target_pairs={{0,1},{1,0},{2,3},{3,2},{4,5},{5,4},{6,7},{7,6},{8,9},{9,8},{10,11... | collective-permute-start | bytes 7077896 | tf_op jit(solution)/shard_map/ppermute | solution.py:533
  71.8 12.3 %copy-start.26 = (bf16[8,1,48,768]{3,2,1,0:T(8,128)(2,1)}, bf16[8,1,48,768]{3,2,1,0:T(8,128)(2,1)S(1)}, u32[]{:S(2)}) copy-start(bf16[8,1,48,768]{3,2,1,0:T(8,128)(2,1)S(1)} %get-tuple-element.75) | copy-start | bytes 1769476
  71.8 31.6 %copy-start.5 = (bf16[768,768]{1,0:T(8,128)(2,1)S(1)}, bf16[768,768]{1,0:T(8,128)(2,1)}, u32[]{:S(2)}) copy-start(bf16[768,768]{1,0:T(8,128)(2,1)} %wk.3) | copy-start | bytes 3538948
  71.8 31.6 %copy-start.7 = (bf16[768,768]{1,0:T(8,128)(2,1)S(1)}, bf16[768,768]{1,0:T(8,128)(2,1)}, u32[]{:S(2)}) copy-start(bf16[768,768]{1,0:T(8,128)(2,1)} %wv.3) | copy-start | bytes 3538948
  87.9 29.5 %collective-permute-start.12 = (bf16[8,3,48,768]{3,2,1,0:T(8,128)(2,1)}, bf16[8,3,48,768]{3,2,1,0:T(8,128)(2,1)}, u32[]{:S(2)}, u32[]{:S(2)}) collective-permute-start(bf16[8,3,48,768]{3,2,1,0:T(8,128)(2,1)} %get-tuple-element.67), channel_id=1, source_target_pairs={{0,1},{1,0},{2,3},{3,2},{4,5},{5,4},{6,7},{7,6},{8,9},{9,8},{10,11... | collective-permute-start | bytes 5308424 | tf_op jit(solution)/shard_map/ppermute | solution.py:533
  88.0 39.5 %collective-permute-start.23 = (bf16[8,4,48,768]{3,2,1,0:T(8,128)(2,1)}, bf16[8,4,48,768]{3,2,1,0:T(8,128)(2,1)}, u32[]{:S(2)}, u32[]{:S(2)}) collective-permute-start(bf16[8,4,48,768]{3,2,1,0:T(8,128)(2,1)} %get-tuple-element.74), channel_id=1, source_target_pairs={{0,1},{1,0},{2,3},{3,2},{4,5},{5,4},{6,7},{7,6},{8,9},{9,8},{10,11... | collective-permute-start | bytes 7077896 | tf_op jit(solution)/shard_map/ppermute | solution.py:533
  94.8 1.4 collective-permute-start.18
  97.1 4.1 %collective-permute-start.19 = (f32[12,768]{1,0:T(8,128)S(1)}, f32[12,768]{1,0:T(8,128)S(1)}, u32[]{:S(2)}, u32[]{:S(2)}) collective-permute-start(f32[12,768]{1,0:T(8,128)S(1)} %add.336), channel_id=1, source_target_pairs={{0,2},{1,3},{2,0},{3,1},{4,6},{5,7},{6,4},{7,5},{8,10},{9,11},{10,... | collective-permute-start | bytes 110600 | tf_op jit(solution)/shard_map/ppermute | solution.py:572
  98.7 22.9 %collective-permute-start.24 = (bf16[8,1,48,768]{3,2,1,0:T(8,128)(2,1)}, bf16[8,1,48,768]{3,2,1,0:T(8,128)(2,1)}, u32[]{:S(2)}, u32[]{:S(2)}) collective-permute-start(bf16[8,1,48,768]{3,2,1,0:T(8,128)(2,1)} %copy-done.32), channel_id=1, source_target_pairs={{0,1},{1,0},{2,3},{3,2},{4,5},{5,4},{6,7},{7,6},{8,9},{9,8},{10,11... | collective-permute-start | bytes 1769480 | tf_op jit(solution)/shard_map/ppermute | solution.py:533
  101.8 9.1 %collective-permute-start.20 = (f32[12,768]{1,0:T(8,128)}, f32[12,768]{1,0:T(8,128)}, u32[]{:S(2)}, u32[]{:S(2)}) collective-permute-start(f32[12,768]{1,0:T(8,128)} %add.337), channel_id=1, source_target_pairs={{0,4},{1,5},{2,6},{3,7},{4,0},{5,1},{6,2},{7,3},{8,12},{9,13},{10,... | collective-permute-start | bytes 110600 | tf_op jit(solution)/shard_map/ppermute | solution.py:572
  108.2 11.9 %copy-start.15 = (bf16[8,3,48,768]{3,2,1,0:T(8,128)(2,1)S(1)}, bf16[8,3,48,768]{3,2,1,0:T(8,128)(2,1)}, u32[]{:S(2)}) copy-start(bf16[8,3,48,768]{3,2,1,0:T(8,128)(2,1)} %copy-done.14) | copy-start | bytes 5308420
  111.8 4.1 %collective-permute-start.21 = (f32[12,768]{1,0:T(8,128)S(1)}, f32[12,768]{1,0:T(8,128)S(1)}, u32[]{:S(2)}, u32[]{:S(2)}) collective-permute-start(f32[12,768]{1,0:T(8,128)S(1)} %add.338), channel_id=1, source_target_pairs={{0,8},{1,9},{2,10},{3,11},{4,12},{5,13},{6,14},{7,15},{8,0},{9,1},... | collective-permute-start | bytes 110600 | tf_op jit(solution)/shard_map/ppermute | solution.py:572
  115.9 26.9 %collective-permute-start.10 = (bf16[128,768]{1,0:T(8,128)(2,1)}, bf16[128,768]{1,0:T(8,128)(2,1)}, u32[]{:S(2)}, u32[]{:S(2)}) collective-permute-start(bf16[128,768]{1,0:T(8,128)(2,1)} %get-tuple-element.96), channel_id=1, source_target_pairs={{0,2},{1,3},{2,0},{3,1},{4,6},{5,7},{6,4},{7,5},{8,10},{9,11},{10,... | collective-permute-start | bytes 589832 | tf_op jit(solution)/shard_map/ppermute | solution.py:489
  117.4 22.0 %collective-permute-start.22 = (f32[12,768]{1,0:T(8,128)S(1)}, f32[12,768]{1,0:T(8,128)S(1)}, u32[]{:S(2)}, u32[]{:S(2)}) collective-permute-start(f32[12,768]{1,0:T(8,128)S(1)} %add.339), channel_id=1, source_target_pairs={{0,16},{1,17},{2,18},{3,19},{4,20},{5,21},{6,22},{7,23},{8,24},{9,... | collective-permute-start | bytes 110600 | tf_op jit(solution)/shard_map/ppermute | solution.py:572
  121.7 13.1 %collective-permute-start.13 = (bf16[4,3,48,768]{3,2,1,0:T(8,128)(2,1)S(1)}, bf16[4,3,48,768]{3,2,1,0:T(8,128)(2,1)S(1)}, u32[]{:S(2)}, u32[]{:S(2)}) collective-permute-start(bf16[4,3,48,768]{3,2,1,0:T(8,128)(2,1)S(1)} %add_convert_fusion.2), channel_id=1, source_target_pairs={{0,4},{1,9},{2,6},{3,11},{4,0},{5,13},{6,2},{7,15},{8,12},{9,1},{1... | collective-permute-start | bytes 2654216 | tf_op jit(solution)/shard_map/ppermute | solution.py:533
  126.1 41.3 %collective-permute-start.31 = (bf16[4,1,192,768]{3,2,1,0:T(8,128)(2,1)}, bf16[4,1,192,768]{3,2,1,0:T(8,128)(2,1)}, u32[]{:S(2)}, u32[]{:S(2)}) collective-permute-start(bf16[4,1,192,768]{3,2,1,0:T(8,128)(2,1)} %add_convert_fusion), channel_id=1, source_target_pairs={{0,4},{1,9},{2,6},{3,11},{4,0},{5,13},{6,2},{7,15},{8,12},{9,1},{1... | collective-permute-start | bytes 3538952 | tf_op jit(solution)/shard_map/ppermute | solution.py:533
  130.4 12.4 %copy-start.34 = (bf16[128,768]{1,0:T(8,128)(2,1)S(1)}, bf16[128,768]{1,0:T(8,128)(2,1)}, u32[]{:S(2)}) copy-start(bf16[128,768]{1,0:T(8,128)(2,1)} %get-tuple-element.97) | copy-start | bytes 589828
  130.4 38.6 %collective-permute-start.25 = (bf16[4,5,48,768]{3,2,1,0:T(8,128)(2,1)}, bf16[4,5,48,768]{3,2,1,0:T(8,128)(2,1)}, u32[]{:S(2)}, u32[]{:S(2)}) collective-permute-start(bf16[4,5,48,768]{3,2,1,0:T(8,128)(2,1)} %pad_maximum_fusion), channel_id=1, source_target_pairs={{0,4},{1,9},{2,6},{3,11},{4,0},{5,13},{6,2},{7,15},{8,12},{9,1},{1... | collective-permute-start | bytes 4423688 | tf_op jit(solution)/shard_map/ppermute | solution.py:533
  137.0 13.4 %collective-permute-start.14 = (bf16[2,3,48,768]{3,2,1,0:T(8,128)(2,1)}, bf16[2,3,48,768]{3,2,1,0:T(8,128)(2,1)}, u32[]{:S(2)}, u32[]{:S(2)}) collective-permute-start(bf16[2,3,48,768]{3,2,1,0:T(8,128)(2,1)} %add_convert_fusion.5), channel_id=1, source_target_pairs={{0,8},{1,5},{2,10},{3,7},{4,12},{5,1},{6,14},{7,3},{8,0},{9,13},{1... | collective-permute-start | bytes 1327112 | tf_op jit(solution)/shard_map/ppermute | solution.py:533
  139.4 4.5 %collective-permute-start.11 = (bf16[128,768]{1,0:T(8,128)(2,1)}, bf16[128,768]{1,0:T(8,128)(2,1)S(1)}, u32[]{:S(2)}, u32[]{:S(2)}) collective-permute-start(bf16[128,768]{1,0:T(8,128)(2,1)} %get-tuple-element.95), channel_id=1, source_target_pairs={{0,1},{1,0},{2,3},{3,2},{4,5},{5,4},{6,7},{7,6},{8,9},{9,8},{10,11... | collective-permute-start | bytes 589832 | tf_op jit(solution)/shard_map/ppermute | solution.py:489
  142.8 6.5 %collective-permute-start.9 = (bf16[128,768]{1,0:T(8,128)(2,1)S(1)}, bf16[128,768]{1,0:T(8,128)(2,1)S(1)}, u32[]{:S(2)}, u32[]{:S(2)}) collective-permute-start(bf16[128,768]{1,0:T(8,128)(2,1)S(1)} %copy-done.34), channel_id=1, source_target_pairs={{0,3},{1,2},{2,1},{3,0},{4,7},{5,6},{6,5},{7,4},{8,11},{9,10},{10,... | collective-permute-start | bytes 589832 | tf_op jit(solution)/shard_map/ppermute | solution.py:489
  143.9 9.6 %collective-permute-start.6 = (bf16[128,768]{1,0:T(8,128)(2,1)}, bf16[128,768]{1,0:T(8,128)(2,1)S(1)}, u32[]{:S(2)}, u32[]{:S(2)}) collective-permute-start(bf16[128,768]{1,0:T(8,128)(2,1)} %get-tuple-element.100), channel_id=1, source_target_pairs={{0,3},{1,2},{2,1},{3,0},{4,7},{5,6},{6,5},{7,4},{8,11},{9,10},{10,... | collective-permute-start | bytes 589832 | tf_op jit(solution)/shard_map/ppermute | solution.py:489
  149.3 9.1 %collective-permute-start.7 = (bf16[128,768]{1,0:T(8,128)(2,1)}, bf16[128,768]{1,0:T(8,128)(2,1)S(1)}, u32[]{:S(2)}, u32[]{:S(2)}) collective-permute-start(bf16[128,768]{1,0:T(8,128)(2,1)} %get-tuple-element.99), channel_id=1, source_target_pairs={{0,2},{1,3},{2,0},{3,1},{4,6},{5,7},{6,4},{7,5},{8,10},{9,11},{10,... | collective-permute-start | bytes 589832 | tf_op jit(solution)/shard_map/ppermute | solution.py:489
  150.4 8.0 %collective-permute-start.8 = (bf16[128,768]{1,0:T(8,128)(2,1)}, bf16[128,768]{1,0:T(8,128)(2,1)S(1)}, u32[]{:S(2)}, u32[]{:S(2)}) collective-permute-start(bf16[128,768]{1,0:T(8,128)(2,1)} %get-tuple-element.98), channel_id=1, source_target_pairs={{0,1},{1,0},{2,3},{3,2},{4,5},{5,4},{6,7},{7,6},{8,9},{9,8},{10,11... | collective-permute-start | bytes 589832 | tf_op jit(solution)/shard_map/ppermute | solution.py:489
  152.5 14.9 %copy-start.13 = (bf16[8,1,192,768]{3,2,1,0:T(8,128)(2,1)S(1)}, bf16[8,1,192,768]{3,2,1,0:T(8,128)(2,1)}, u32[]{:S(2)}) copy-start(bf16[8,1,192,768]{3,2,1,0:T(8,128)(2,1)} %copy-done.11) | copy-start | bytes 7077892
  153.5 11.4 %collective-permute-start.15 = (bf16[1,3,48,768]{3,2,1,0:T(8,128)(2,1)S(1)}, bf16[1,3,48,768]{3,2,1,0:T(8,128)(2,1)S(1)}, u32[]{:S(2)}, u32[]{:S(2)}) collective-permute-start(bf16[1,3,48,768]{3,2,1,0:T(8,128)(2,1)S(1)} %add_convert_fusion.15), channel_id=1, source_target_pairs={{0,16},{1,17},{2,18},{3,19},{4,20},{5,21},{6,22},{7,23},{8,24},{9,... | collective-permute-start | bytes 663560 | tf_op jit(solution)/shard_map/ppermute | solution.py:533
  166.3 9.3 %collective-permute-start.16 = (bf16[3,48,768]{2,1,0:T(8,128)(2,1)S(1)}, bf16[3,48,768]{2,1,0:T(8,128)(2,1)S(1)}, u32[]{:S(2)}, u32[]{:S(2)}) collective-permute-start(bf16[3,48,768]{2,1,0:T(8,128)(2,1)S(1)} %fusion.1), channel_id=1, source_target_pairs={{0,2},{1,3},{2,0},{3,1},{4,6},{5,7},{6,4},{7,5},{8,10},{9,11},{10,... | collective-permute-start | bytes 663560 | tf_op jit(solution)/shard_map/ppermute | solution.py:533
  168.9 9.9 %collective-permute-start.32 = (bf16[2,1,192,768]{3,2,1,0:T(8,128)(2,1)S(1)}, bf16[2,1,192,768]{3,2,1,0:T(8,128)(2,1)S(1)}, u32[]{:S(2)}, u32[]{:S(2)}) collective-permute-start(bf16[2,1,192,768]{3,2,1,0:T(8,128)(2,1)S(1)} %add_convert_fusion.3), channel_id=1, source_target_pairs={{0,8},{1,5},{2,10},{3,7},{4,12},{5,1},{6,14},{7,3},{8,0},{9,13},{1... | collective-permute-start | bytes 1769480 | tf_op jit(solution)/shard_map/ppermute | solution.py:533
  171.6 16.2 %collective-permute-start.26 = (bf16[2,5,48,768]{3,2,1,0:T(8,128)(2,1)S(1)}, bf16[2,5,48,768]{3,2,1,0:T(8,128)(2,1)S(1)}, u32[]{:S(2)}, u32[]{:S(2)}) collective-permute-start(bf16[2,5,48,768]{3,2,1,0:T(8,128)(2,1)S(1)} %pad_maximum_fusion.6), channel_id=1, source_target_pairs={{0,8},{1,5},{2,10},{3,7},{4,12},{5,1},{6,14},{7,3},{8,0},{9,13},{1... | collective-permute-start | bytes 2211848 | tf_op jit(solution)/shard_map/ppermute | solution.py:533
  175.6 15.4 %collective-permute-start.17 = (bf16[3,48,768]{2,1,0:T(8,128)(2,1)S(1)}, bf16[3,48,768]{2,1,0:T(8,128)(2,1)S(1)}, u32[]{:S(2)}, u32[]{:S(2)}) collective-permute-start(bf16[3,48,768]{2,1,0:T(8,128)(2,1)S(1)} %add_convert_fusion.13), channel_id=1, source_target_pairs={{0,1},{1,0},{2,3},{3,2},{4,5},{5,4},{6,7},{7,6},{8,9},{9,8},{10,11... | collective-permute-start | bytes 663560 | tf_op jit(solution)/shard_map/ppermute | solution.py:533
  180.0 24.0 %collective-permute-start.33 = (bf16[1,1,192,768]{3,2,1,0:T(8,128)(2,1)S(1)}, bf16[1,1,192,768]{3,2,1,0:T(8,128)(2,1)S(1)}, u32[]{:S(2)}, u32[]{:S(2)}) collective-permute-start(bf16[1,1,192,768]{3,2,1,0:T(8,128)(2,1)S(1)} %add_convert_fusion.9), channel_id=1, source_target_pairs={{0,16},{1,17},{2,18},{3,19},{4,20},{5,21},{6,22},{7,23},{8,24},{9,... | collective-permute-start | bytes 884744 | tf_op jit(solution)/shard_map/ppermute | solution.py:533
  190.1 21.8 %collective-permute-start.27 = (bf16[1,5,48,768]{3,2,1,0:T(8,128)(2,1)S(1)}, bf16[1,5,48,768]{3,2,1,0:T(8,128)(2,1)S(1)}, u32[]{:S(2)}, u32[]{:S(2)}) collective-permute-start(bf16[1,5,48,768]{3,2,1,0:T(8,128)(2,1)S(1)} %pad_maximum_fusion.7), channel_id=1, source_target_pairs={{0,16},{1,17},{2,18},{3,19},{4,20},{5,21},{6,22},{7,23},{8,24},{9,... | collective-permute-start | bytes 1105928 | tf_op jit(solution)/shard_map/ppermute | solution.py:533
  205.3 10.0 %collective-permute-start.34 = (bf16[1,192,768]{2,1,0:T(8,128)(2,1)S(1)}, bf16[1,192,768]{2,1,0:T(8,128)(2,1)S(1)}, u32[]{:S(2)}, u32[]{:S(2)}) collective-permute-start(bf16[1,192,768]{2,1,0:T(8,128)(2,1)S(1)} %fusion), channel_id=1, source_target_pairs={{0,2},{1,3},{2,0},{3,1},{4,6},{5,7},{6,4},{7,5},{8,10},{9,11},{10,... | collective-permute-start | bytes 884744 | tf_op jit(solution)/shard_map/ppermute | solution.py:533
  214.2 11.5 %collective-permute-start.28 = (bf16[5,48,768]{2,1,0:T(8,128)(2,1)S(1)}, bf16[5,48,768]{2,1,0:T(8,128)(2,1)S(1)}, u32[]{:S(2)}, u32[]{:S(2)}) collective-permute-start(bf16[5,48,768]{2,1,0:T(8,128)(2,1)S(1)} %maximum_bitcast_fusion), channel_id=1, source_target_pairs={{0,2},{1,3},{2,0},{3,1},{4,6},{5,7},{6,4},{7,5},{8,10},{9,11},{10,... | collective-permute-start | bytes 1105928 | tf_op jit(solution)/shard_map/ppermute | solution.py:533
  215.3 10.6 %collective-permute-start.35 = (bf16[1,192,768]{2,1,0:T(8,128)(2,1)S(1)}, bf16[1,192,768]{2,1,0:T(8,128)(2,1)S(1)}, u32[]{:S(2)}, u32[]{:S(2)}) collective-permute-start(bf16[1,192,768]{2,1,0:T(8,128)(2,1)S(1)} %add_convert_fusion.7), channel_id=1, source_target_pairs={{0,1},{1,0},{2,3},{3,2},{4,5},{5,4},{6,7},{7,6},{8,9},{9,8},{10,11... | collective-permute-start | bytes 884744 | tf_op jit(solution)/shard_map/ppermute | solution.py:533
  225.8 1.8 collective-permute-start.29
  (33 other events, 123.5 us)

commit v2 on v1

--- a/solution.py
+++ b/solution.py
@@ -105,6 +105,7 @@
 
         zero = jnp.zeros((8, hat.shape[1]), F32)
         sums = lax.fori_loop(0, tokens // step, body, (zero, zero, zero))
+        vec[...] = jnp.zeros_like(vec)
         for k in range(3):
             vec[k : k + 1] = jnp.sum(sums[k], 0, keepdims=True)
 
@@ -227,12 +228,13 @@
     heads = width // HEAD_DIM
     col = lambda rows: pl.BlockSpec((rows, group), lambda g: (0, g))
     low = jax.ShapeDtypeStruct((tokens, width), BF16)
+    far = pltpu.HBM((tokens, width), BF16)
     return pl.pallas_call(
         attn_kernel,
         out_shape=(
-            low, low, low,
-            jax.ShapeDtypeStruct((heads, tokens, tokens), BF16),
-            jax.ShapeDtypeStruct((tokens, width), F32),
+            far, far, far,
+            pltpu.HBM((heads, tokens, tokens), BF16),
+            pltpu.HBM((tokens, width), F32),
             low,
             jax.ShapeDtypeStruct((tokens, width), F32),
             jax.ShapeDtypeStruct((tokens, 1), F32),
@@ -262,6 +264,7 @@
     def _():
         gb_s[...] = gpre[...].astype(BF16)
         nt_s[...] = (hat[...] * gain1[...] + shift1[...]).astype(BF16).T
+        ibias[...] = jnp.zeros_like(ibias)
 
     sums = jnp.zeros((8, width), F32)
     for r in range(0, tokens, ROWS):
@@ -269,8 +272,8 @@
         low = (dot(gb_s[rows], wo[...], (1, 1)) * slope[rows].astype(F32)).astype(BF16)
         gi[rows] = low
         sums = sums + fold8(low.astype(F32))
-    ibias[...] = jnp.sum(sums, 0, keepdims=True)
-    put_units(keep, send, slots, 0, dot(nt_s[...], gi[...]), f)
+    ibias[pl.ds(f, 1)] = jnp.sum(sums, 0, keepdims=True)
+    put_units(keep, send, slots, 0, dot(nt_s[...], gi[...]), f ^ slots[slots.shape[0] - 1])
 
 
 def ffn_down(n_dp, slots, gpre, slope, hat, gain1, shift1, wo, ROWS=512):
@@ -286,7 +289,7 @@
         lambda *refs: down_kernel(ROWS, *refs),
         out_shape=(
             jax.ShapeDtypeStruct((tokens, ff), BF16),
-            jax.ShapeDtypeStruct((1, ff), F32),
+            jax.ShapeDtypeStruct((8, width), F32),
             units, units,
         ),
         grid_spec=pltpu.PrefetchScalarGridSpec(
@@ -297,9 +300,7 @@
                 pl.BlockSpec((width, width), lambda f, s: (f, 0)),
             ],
             out_specs=[
-                piece,
-                pl.BlockSpec((1, width), lambda f, s: (0, f)),
-                whole(shape), whole(shape),
+                piece, whole((8, width)), whole(shape), whole(shape),
             ],
             scratch_shapes=[
                 pltpu.VMEM((tokens, width), BF16),
@@ -340,6 +341,7 @@
 
         zero = jnp.zeros((8, width), F32)
         sums = lax.fori_loop(0, tokens // step, body, (zero, zero, zero))
+        vec[...] = jnp.zeros_like(vec)
         for k in range(3):
             vec[k : k + 1] = jnp.sum(sums[k], 0, keepdims=True)
         gctx[...] = dot(gb_s[...], wa[...], (1, 1)).astype(BF16)
@@ -378,14 +380,9 @@
     )(slots, gpre, gi, hat, r1, gain1, wi, wa, ctx)
 
 
-def back_kernel(slots, x, q, k, v, c, gc, inv, e, dq, dk, dv, qb, vb, keep, send, xt_s):
-    g = pl.program_id(0)
+def back_kernel(q, k, v, c, gc, inv, e, dq, dk, dv, vec):
     scale = 1.0 / math.sqrt(HEAD_DIM)
     pair_width = 2 * HEAD_DIM
-
-    @pl.when(g == 0)
-    def _():
-        xt_s[...] = x[...].T
 
     low = lax.broadcasted_iota(jnp.int32, (1, pair_width), 1) < HEAD_DIM
     mine = (low, jnp.logical_not(low))
@@ -411,37 +408,71 @@
         dq[:, cols] = (total * scale).astype(BF16)
         dv[:, cols] = jnp.concatenate(dvt, 0).astype(BF16).T
         dk[:, cols] = jnp.concatenate(dkt, 0).astype(BF16).T
-    qb[...] = jnp.sum(fold8(dq[...].astype(F32)), 0, keepdims=True)
-    vb[...] = jnp.sum(fold8(dv[...].astype(F32)), 0, keepdims=True)
-    width = q.shape[1]
-    cols = pl.ds(pl.multiple_of(g * width, width), width)
-    for n, grad in enumerate((dq, dk, dv)):
-        put_units(keep, send, slots, 0, dot(xt_s[...], grad[...]), n, cols)
-
-
-def attention_back(n_dp, slots, x, q, k, v, c, gc, inv, e):
-    tokens, width = x.shape
+    vec[...] = jnp.zeros_like(vec)
+    vec[0:1] = jnp.sum(fold8(dq[...].astype(F32)), 0, keepdims=True)
+    vec[1:2] = jnp.sum(fold8(dv[...].astype(F32)), 0, keepdims=True)
+
+
+def attention_back(q, k, v, c, gc, inv, e):
+    tokens, width = q.shape
     group = 4 * HEAD_DIM
-    col = pl.BlockSpec((tokens, group), lambda g, s: (0, g))
-    row = pl.BlockSpec((1, group), lambda g, s: (0, g))
+    col = pl.BlockSpec((tokens, group), lambda g: (0, g))
     low = jax.ShapeDtypeStruct((tokens, width), BF16)
-    vector = jax.ShapeDtypeStruct((1, width), F32)
-    shape = (n_dp, 3, width // (2 * n_dp), width)
-    units = jax.ShapeDtypeStruct(shape, BF16)
     return pl.pallas_call(
         back_kernel,
-        out_shape=(low, low, low, vector, vector, units, units),
+        out_shape=(low, low, low, jax.ShapeDtypeStruct((8, width), F32)),
+        grid=(width // group,),
+        in_specs=[col, col, col, col, col, col,
+                  pl.BlockSpec((4, tokens, tokens), lambda g: (g, 0, 0))],
+        out_specs=[col, col, col, pl.BlockSpec((8, group), lambda g: (0, g))],
+        compiler_params=pltpu.CompilerParams(vmem_limit_bytes=12 << 20),
+        name="attention_back",
+    )(q, k, v, c, gc, inv, e)
+
+
+def weights_kernel(slots, x, dq, dk, dv, vec2, vec1, ibias, vec0, keep, send, vkeep, vsend):
+    xt = x[...].T
+    for n, grad in enumerate((dq, dk, dv)):
+        put_units(keep, send, slots, 0, dot(xt, grad[...]), n)
+    n_dp = keep.shape[0]
+    width = x.shape[1]
+    part = width // n_dp
+    odd = slots[0] == 1
+    eight = jnp.concatenate([vec2[0:3], vec1[0:3], vec0[0:2]], 0)
+
+    def two(rows):
+        high = rows.astype(BF16).astype(F32)
+        return jnp.concatenate([high, rows - high], 0).astype(BF16)
+
+    for j in range(n_dp):
+        start = 4 * part * j
+        row = ibias[start // width : start // width + 1]
+        row = jnp.broadcast_to(row, (8, width))
+        first = two(pltpu.roll(eight, (width - part * j) % width, 1))
+        second = two(pltpu.roll(row, (width - start % width) % width, 1))
+        vkeep[slots[1 + j]] = jnp.where(odd, second, first)
+        vsend[slots[1 + n_dp + j]] = jnp.where(odd, first, second)
+
+
+def weight_gradients(n_dp, slots, x, dq, dk, dv, *vectors):
+    tokens, width = x.shape
+    full = whole((tokens, width))
+    shape = (n_dp, 3, width // (2 * n_dp), width)
+    tiny = (n_dp, 16, width)
+    units = jax.ShapeDtypeStruct(shape, BF16)
+    small = jax.ShapeDtypeStruct(tiny, BF16)
+    return pl.pallas_call(
+        weights_kernel,
+        out_shape=(units, units, small, small),
         grid_spec=pltpu.PrefetchScalarGridSpec(
             num_scalar_prefetch=1,
-            grid=(width // group,),
-            in_specs=[whole((tokens, width)), col, col, col, col, col, col,
-                      pl.BlockSpec((4, tokens, tokens), lambda g, s: (g, 0, 0))],
-            out_specs=[col, col, col, row, row, whole(shape), whole(shape)],
-            scratch_shapes=[pltpu.VMEM((width, tokens), BF16)],
+            grid=(1,),
+            in_specs=[full, full, full, full] + [whole((8, width))] * 4,
+            out_specs=[whole(shape), whole(shape), whole(tiny), whole(tiny)],
         ),
         compiler_params=pltpu.CompilerParams(vmem_limit_bytes=12 << 20),
-        name="attention_back",
-    )(slots, x, q, k, v, c, gc, inv, e)
+        name="weight_gradients",
+    )(slots, x, dq, dk, dv, *vectors)
 
 
 def input_kernel(gmid, dq, dk, dv, wq, wk, wv, out):
@@ -509,7 +540,7 @@
         by_core.append(jnp.stack(entries))
     kept = jnp.where(odd, by_core[1], by_core[0])
     sent = jnp.where(odd, by_core[0], by_core[1])
-    return jnp.concatenate([(s & 1)[None], kept, sent]).astype(jnp.int32)
+    return jnp.concatenate([(s & 1)[None], kept, sent, (s & 2)[None]]).astype(jnp.int32)
 
 
 def added(pieces, cut):
@@ -519,58 +550,98 @@
     return total.astype(BF16)
 
 
+def added_in_two(pieces, cut):
+    total = 0.0
+    for piece in pieces:
+        rows = piece[cut].astype(F32)
+        total = total + (rows[..., :8, :] + rows[..., 8:, :])
+    high = total.astype(BF16)
+    return jnp.concatenate([high, (total - high.astype(F32)).astype(BF16)], -2)
+
+
 class Halving:
-    def __init__(self, keep, send, n_dp, n_seq):
+    def __init__(self, keep, send, n_dp, n_seq, small=()):
+        self.y_cut = False
         self.n_dp = n_dp
         self.n_seq = n_seq
         self.flips = [
             lambda d, s, zero=zero, one=one: (d ^ (1 << (one if s & 1 else zero)), s)
             for zero, one in zip(*bit_orders(n_dp))
         ]
-        self.families = [[keep, self.permute(send, lambda d, s: (d, s ^ 1))]]
+        flat = lambda units: units.reshape(n_dp, -1, units.shape[-1])
+        keep, send = flat(keep), flat(send)
+        rows = keep.shape[1]
+        self.adders = [added]
+        self.families = [[keep]]
+        if small:
+            self.adders.append(added_in_two)
+            self.families.append([small[0]])
+            send = jnp.concatenate([send, small[1]], 1)
+        self.take(self.permute(send, lambda d, s: (d, s ^ 1)))
 
     def permute(self, values, partner):
         return lax.ppermute(values, BOTH, pairs(self.n_dp, self.n_seq, partner))
 
+    def take(self, got):
+        for pieces, part in zip(self.families, self.split(got)):
+            pieces.append(part)
+
     def join(self, other):
         self.families += other.families
+        self.adders += other.adders
 
     def sums(self, cut):
-        return jnp.concatenate([added(pieces, cut) for pieces in self.families], 1)
-
-    def step(self, *wait):
+        parts = [add(pieces, cut) for add, pieces in zip(self.adders, self.families)]
+        return parts[0] if len(parts) == 1 else jnp.concatenate(parts, -2)
+
+    def cut_y(self):
+        half = self.families[0][0].shape[1] // 2
+        self.y_cut = True
+        got = self.permute(
+            self.sums((slice(None), slice(half, None))), lambda d, s: (d, s ^ 2)
+        )
+        self.families[0] = [piece[:, :half] for piece in self.families[0]]
+        self.take(got)
+
+    def step(self):
         half = self.families[0][0].shape[0] // 2
-        send = self.sums(slice(half, None))
-        got = self.permute(after(send, *wait) if wait else send, self.flips.pop(0))
-        families, first = [], 0
+        got = self.permute(self.sums(slice(half, None)), self.flips.pop(0))
+        self.families = [[piece[:half] for piece in pieces] for pieces in self.families]
+        self.take(got)
+
+    def share_y(self):
+        mine = self.sums(0)
+        got = self.permute(mine, lambda d, s: (d, s ^ 2))
+        self.families = [[piece] for piece in self.split(mine)]
+        self.take(got)
+        if not self.y_cut:
+            self.mine = self.sums(Ellipsis)
+            return
+        high = (lax.axis_index("seq") & 2) == 2
+        own, other = self.families[0]
+        both = [jnp.where(high, other, own), jnp.where(high, own, other)]
+        rest = [add(p, Ellipsis) for add, p in zip(self.adders[1:], self.families[1:])]
+        self.mine = jnp.concatenate(both + rest, -2)
+        self.families[0] = [jnp.concatenate(both, -2)]
+
+    def split(self, values):
+        parts, first = [], 0
         for pieces in self.families:
-            n = pieces[0].shape[1]
-            families.append([piece[:half] for piece in pieces] + [got[:, first : first + n]])
-            first += n
-        self.families = families
-        return got
-
-    def share_y(self):
-        mine = self.sums(slice(None))[0]
-        got = self.permute(mine, lambda d, s: (d, s ^ 2))
-        self.mine = (mine.astype(F32) + got.astype(F32)).astype(BF16)
-        return got
+            rows = pieces[0].shape[-2]
+            parts.append(values[..., first : first + rows, :])
+            first += rows
+        return parts
 
     def share_core(self):
         other = self.permute(self.mine, lambda d, s: (d, s ^ 1))
         odd = (lax.axis_index("seq") & 1) == 1
-        first = jnp.where(odd, other, self.mine)
-        second = jnp.where(odd, self.mine, other)
-        return jnp.concatenate([first, second], 1).astype(F32)
-
-
-def sum_all(values, n_dp, n_seq):
-    flips = [lambda d, s, k=k: (d, s ^ k) for k in (1, 2)]
-    for bit in range(n_dp.bit_length() - 1):
-        flips.append(lambda d, s, bit=bit: (d ^ (1 << bit), s))
-    for flip in flips:
-        values = values + lax.ppermute(values, BOTH, pairs(n_dp, n_seq, flip))
-    return values
+        halves = (jnp.where(odd, other, self.mine), jnp.where(odd, self.mine, other))
+        return [[part.astype(F32) for part in pair] for pair in zip(*map(self.split, halves))]
+
+
+def joined(pair, count):
+    first, second = (half.reshape(count, -1, half.shape[-1]) for half in pair)
+    return jnp.concatenate([first, second], 1)
 
 
 def local(
@@ -601,9 +672,9 @@
     tokens = slice_rows * n_seq
     slots = slot_table(n_dp, d, s)
 
-    def to_passage(values):
-        blocks = exchange([pick(values, s ^ k) for k in range(n_seq)], n_seq)
-        return jnp.concatenate(blocks, 0)
+    def to_passage(values, *wait):
+        blocks = [pick(values, s ^ k) for k in range(n_seq)]
+        return jnp.concatenate(exchange(after(blocks, *wait), n_seq), 0)
 
     def to_slots(values):
         values = values.reshape(n_seq, slice_rows, width)
@@ -617,7 +688,7 @@
         return vector.reshape(1, -1)
 
     x = to_passage(hidden_states)
-    cot = to_passage(after(cotangent, x))
+    cot = to_passage(cotangent, x)
     spots = lax.iota(jnp.int32, tokens)
     spots = ((spots // slice_rows) ^ s) * slice_rows + spots % slice_rows
     bias = jnp.where(spots < pick(lengths, s), 0.0, MASKED).astype(BF16)
@@ -641,39 +712,34 @@
     grad_mid, grad_context, vec1, *out_units = middle(
         n_dp, slots, grad_pre, grad_inner, hat, r1, gain1, inner_weight, out_weight, context,
     )
+    inner.cut_y()
     inner.join(Halving(*out_units, n_dp, n_seq))
-    a2 = outer.step()
-    b1 = inner.step()
-    grad_query, grad_key, grad_value, qbias, vbias, *attn_units = attention_back(
-        n_dp, slots, x, query, key, value, context, grad_context, inverse, exps,
-    )
-    attn = Halving(*attn_units, n_dp, n_seq)
+    grad_query, grad_key, grad_value, vec0 = attention_back(
+        query, key, value, context, grad_context, inverse, exps,
+    )
+    outer.step()
+    keep, send, *small = weight_gradients(
+        n_dp, slots, x, grad_query, grad_key, grad_value, vec2, vec1, ibias, vec0,
+    )
+    attn = Halving(keep, send, n_dp, n_seq, small)
     input_low = input_gradient(
         grad_mid, grad_query, grad_key, grad_value, query_weight, key_weight, value_weight,
     )
-    vectors = jnp.concatenate([vec2[:3], vec1[:3], qbias, vbias, ibias.reshape(4, width)], 0)
-    c1 = attn.step()
-    b2 = inner.step()
-    a3 = outer.step()
-    c2 = attn.step()
-    b3 = inner.step()
-    outer.share_y()
-    c3 = attn.step()
-    while attn.flips:
-        attn.step()
-        inner.step()
-        outer.step()
-    inner.share_y()
-    attn.share_y()
-    vectors = sum_all(vectors, n_dp, n_seq)
+    for group in (attn, inner, outer):
+        while group.flips:
+            group.step()
+        group.share_y()
     block_output = to_slots(result)
     input_grad = to_slots(input_low)
-    outer_sum = outer.share_core()
-    inner_sum = inner.share_core()
-    attn_sum = attn.share_core()
+    ((outer_pair),) = outer.share_core()
+    inner_pair, out_pair = inner.share_core()
+    attn_pair, small_pair = attn.share_core()
+    outer_sum = joined(outer_pair, 1)[0]
+    inner_sum = joined(inner_pair, 4)
+    attn_sum = joined(attn_pair, 3)
     part = width // n_dp
-    mine = lax.dynamic_slice_in_dim(vectors[:8], d * part, part, 1)
-    ibias_part = lax.dynamic_slice_in_dim(vectors[8:].reshape(4 * width), d * 4 * part, 4 * part, 0)
+    small_sum = [half[:8] + half[8:] for half in small_pair]
+    mine = small_sum[0][:, :part]
     return (
         block_output,
         input_grad,
@@ -682,13 +748,13 @@
         attn_sum[1],
         attn_sum[2],
         mine[7],
-        inner_sum[4],
+        joined(out_pair, 1)[0],
         mine[3],
         mine[4],
         mine[5],
         jnp.concatenate([inner_sum[t] for t in range(4)], 1),
-        ibias_part,
-        outer_sum[0],
+        small_sum[1][0, : 4 * part],
+        outer_sum,
         mine[0],
         mine[1],
         mine[2],

time: 231 us -> 194 us (0.84)
  other arithmetic: 35.7 us -> 10.4 us
  local copies, waits for them, and re-layouts: 30.2 us -> 14.4 us
  starting transfers between devices: 34.9 us -> 39.6 us
  waiting for transfers between devices: 67.7 us -> 71.5 us
  Pallas kernels: 59.9 us -> 56.2 us
    convert_element_type x14 -> x20, other arithmetic: 20.1 us -> 2.91 us  [added(): return total.astype(BF16)]
    ppermute x19 -> x20, starting transfers between devices: 17.3 us -> 29.5 us  [permute(): return lax.ppermute(values, BOTH, pairs(self.n_dp, self.n_seq, partner))]
    ppermute x19 -> x20, waiting for transfers between devices: 44.1 us -> 55.5 us  [permute(): return lax.ppermute(values, BOTH, pairs(self.n_dp, self.n_seq, partner))]
    unnamed x90 -> x43, local copies, waits for them, and re-layouts: 13.9 us -> 6.12 us
    ppermute x5 -> x0, starting transfers between devices: 7.65 us -> none  [sum_all(): values = values + lax.ppermute(values, BOTH, pairs(n_dp, n_seq, flip))]
    ppermute x5 -> x0, waiting for transfers between devices: 5.44 us -> none  [sum_all(): values = values + lax.ppermute(values, BOTH, pairs(n_dp, n_seq, flip))]
    add x5 -> x1, other arithmetic: 2.4 us -> 0.01 us  [local(): small_sum = [half[:8] + half[8:] for half in small_pair]]
    slice x4 -> x8, local copies, waits for them, and re-layouts: 2.55 us -> 0.2 us  [the longest x2 0.09 us: added(): total = pieces[0][cut].astype(F32)]
  transfers between devices with their start and end apart: 36 -> 32, of which waited for: 17 -> 16; matrix products, arithmetic and copies ran while one was open for 20% -> 9% of each run, Pallas kernels for 18% -> 7%
where the time goes in v2:
time: 194 us
  waiting for transfers between devices  71.5 us (37%)
  Pallas kernels  56.2 us (29%)
  starting transfers between devices  39.6 us (20%)
  local copies, waits for them, and re-layouts  14.4 us (7%)
  other arithmetic  10.4 us (5%)
    ppermute x20, waiting for transfers between devices, permute(): return lax.ppermute(values, BOTH, pairs(self.n_dp, self.n_seq, partner))  55.5 us
    ppermute x20, starting transfers between devices, permute(): return lax.ppermute(values, BOTH, pairs(self.n_dp, self.n_seq, partner))  29.5 us
    pallas_call x1, Pallas kernels, ffn_up(): pl.pallas_call(lambda *refs: up_kernel(ROWS, *refs), out_shape=(jax.Shape...  17.7 us
    ppermute x12, waiting for transfers between devices, exchange(): lax.ppermute(blocks[k], 'seq', [(s, s ^ k) for s in range(n_seq)])  16 us
    pallas_call x1, Pallas kernels, attention_forward(): pl.pallas_call(attn_kernel, out_shape=(far, far, far, pltpu.HBM((heads, t...  11.2 us
    ppermute x12, starting transfers between devices, exchange(): lax.ppermute(blocks[k], 'seq', [(s, s ^ k) for s in range(n_seq)])  10.1 us
    pallas_call x1, Pallas kernels, attention_back(): pl.pallas_call(back_kernel, out_shape=(low, low, low, jax.ShapeDtypeStruc...  7.42 us
    pallas_call x1, Pallas kernels, middle(): pl.pallas_call(mid_kernel, out_shape=(jax.ShapeDtypeStruct((tokens, width...  7.37 us
  transfers between devices with their start and end apart: 32, of which 16 were waited for; matrix products, arithmetic and copies ran while one was open for 9% of the time, Pallas kernels for 7%

profile of v2, /device:TPU:0, one launch (start us, length us, event | category | flops | bytes accessed | tf_op | source)
XLA Modules:
  0.0 193.7 jit_solution(3988061194953898146)
XLA Ops:
  0.7 1.4 dynamic-slice_bitcast_fusion.4
  2.7 2.6 %collective-permute-start.1 = (bf16[128,768]{1,0:T(8,128)(2,1)S(1)}, bf16[128,768]{1,0:T(8,128)(2,1)}, u32[]{:S(2)}, u32[]{:S(2)}) collective-permute-start(bf16[128,768]{1,0:T(8,128)(2,1)S(1)} %get-tuple-element.58), channel_id=1, source_target_pairs={{0,2},{1,3},{2,0},{3,1},{4,6},{5,7},{6,4},{7,5},{8,10},{9,11},{10,... | collective-permute-start | bytes 589832 | tf_op jit(solution)/shard_map/ppermute | solution.py:520
  5.3 1.3 dynamic_slice.33
  8.9 1.4 dynamic-slice_bitcast_fusion
  10.4 1.2 constant_dynamic-update-slice_fusion.2
  11.6 0.9 constant_dynamic-update-slice_fusion.1
  12.6 2.1 %collective-permute-done.2 = bf16[128,768]{1,0:T(8,128)(2,1)S(1)} collective-permute-done((bf16[128,768]{1,0:T(8,128)(2,1)S(1)}, bf16[128,768]{1,0:T(8,128)(2,1)S(1)}, u32[]{:S(2)}, u32[]{:S(2)}) %collective-permute-start.2) | collective-permute-done | bytes 196640 | tf_op jit(solution)/shard_map/ppermute | solution.py:520
  14.9 1.7 collective-permute-start.4
  17.5 1.3 copy-done.4
  18.8 1.3 copy-done.6
  20.0 11.2 %attention_forward.1 = (bf16[512,768]{1,0:T(8,128)(2,1)}, bf16[512,768]{1,0:T(8,128)(2,1)}, bf16[512,768]{1,0:T(8,128)(2,1)}, bf16[12,512,512]{2,1,0:T(8,128)(2,...) custom-call(bf16[512,768]{1,0:T(8,128)(2,1)S(1)} %constant_dynamic-update, ...), custom_call_target="tpu_custom_call" | custom-call | tf_op jit(solution)/shard_map/attention_forward/pallas_call | solution.py:232
  31.3 17.7 %ffn_up.1 = (bf16[512,768]{1,0:T(8,128)(2,1)S(1)}, bf16[512,3072]{1,0:T(8,128)(2,1)S(1)}, f32[512,768]{1,0:T(8,128)S(1)}, f32[8,768]{1,0:T(8,128)S(1)}, bf16[8,1...) custom-call(s32[18]{0:T(128)S(1)} %pad_add_fusion.refs_0_.slots, ...), custom_call_target="tpu_custom_call" | custom-call | tf_op jit(solution)/shard_map/ffn_up/pallas_call | solution.py:129
  49.1 7.3 %ffn_down.1 = (bf16[512,3072]{1,0:T(8,128)(2,1)S(1)}, f32[8,768]{1,0:T(8,128)S(1)}, bf16[8,4,48,768]{3,2,1,0:T(8,128)(2,1)S(1)}, bf16[8,4,48,768]{3,2,1,0:T(8,128)(2,1)S(1)}) custom-call(s32[18]{0:T(128)S(1)} %pad_add_fusion.refs_0_.slots, f32[512,768]{1,0:T(8,128)S(1)} %get-tuple-element.66.refs_1_.gpre, bf16[512,3072]{1,0:T(8,128)(2,1)S(1)} %get-tuple-element.67.refs_2_, ...), custom_call_target="tpu_custom_call" | custom-call | tf_op jit(solution)/shard_map/ffn_down/pallas_call | solution.py:288
  56.4 7.4 %middle.1 = (f32[512,768]{1,0:T(8,128)S(1)}, bf16[512,768]{1,0:T(8,128)(2,1)S(1)}, f32[8,768]{1,0:T(8,128)S(1)}, bf16[8,1,48,768]{3,2,1,0:T(8,128)(2,1)S(1)}, bf16[8,1,48,768]{3,2,1,0:T(8,128)(2,1)S(1)}) custom-call(s32[18]{0:T(128)S(1)} %pad_add_fusion.refs_0_.slots, f32[512,768]{1,0:T(8,128)S(1)} %get-tuple-element.66.refs_1_.gpre, ...), custom_call_target="tpu_custom_call" | custom-call | tf_op jit(solution)/shard_map/middle/pallas_call | solution.py:357
  63.9 7.4 %attention_back.1 = (bf16[512,768]{1,0:T(8,128)(2,1)S(1)}, bf16[512,768]{1,0:T(8,128)(2,1)S(1)}, bf16[512,768]{1,0:T(8,128)(2,1)S(1)}, f32[8,768]{1,0:T(8,128)S(1)}) custom-call(bf16[512,768]{1,0:T(8,128)(2,1)S(1)} %copy-done.9, bf16[512,768]{1,0:T(8,128)(2,1)S(1)} %copy-done.10, bf16[512,768]{1,0:T(8,128)(2,1)S(1)} %copy-done.11, ...), custom_call_target="tpu_custom_call" | custom-call | tf_op jit(solution)/shard_map/attention_back/pallas_call | solution.py:421
  71.3 2.6 %weight_gradients.1 = (bf16[8,3,48,768]{3,2,1,0:T(8,128)(2,1)S(1)}, bf16[8,3,48,768]{3,2,1,0:T(8,128)(2,1)S(1)}, bf16[8,16,768]{2,1,0:T(8,128)(2,1)S(1)}, bf16[8,16,768]{2,1,0:T(8,128)(2,1)S(1)}) custom-call(s32[18]{0:T(128)S(1)} %pad_add_fusion.refs_0_.slots, bf16[512,768]{1,0:T(8,128)(2,1)S(1)} %constant_dynamic-update-slice_fusion.x, ...), custom_call_target="tpu_custom_call" | custom-call | tf_op jit(solution)/shard_map/weight_gradients/pallas_call | solution.py:464
  74.8 0.9 copy-done.5
  76.1 2.6 %input_gradient.1 = bf16[512,768]{1,0:T(8,128)(2,1)S(1)} custom-call(f32[512,768]{1,0:T(8,128)S(1)} %get-tuple-element.71.gmid, bf16[512,768]{1,0:T(8,128)(2,1)S(1)} %get-tuple-element.78.dq, bf16[512,768]{1,0:T(8,128)(2,1)S(1)} %get-tuple-element.79.dk, bf16[512,768]{1,0:T(8,128)(2,1)S(1)} %get-tuple-element.80.dv, bf16[768,768]{1,0:T(8,128)(2,1)S(1)} %copy-done.3, ...), custom_call_target="tpu_custom_call" | custom-call | tf_op jit(solution)/shard_map/input_gradient/pallas_call | solution.py:490
  78.8 1.8 collective-permute-start.10
  81.1 5.5 %collective-permute-done.10 = bf16[128,768]{1,0:T(8,128)(2,1)S(1)} collective-permute-done((bf16[128,768]{1,0:T(8,128)(2,1)S(1)}, bf16[128,768]{1,0:T(8,128)(2,1)S(1)}, u32[]{:S(2)}, u32[]{:S(2)}) %collective-permute-start.10) | collective-permute-done | bytes 196640 | tf_op jit(solution)/shard_map/ppermute | solution.py:520
  86.6 1.7 collective-permute-start.7
  88.4 1.1 collective-permute-done.9
  89.4 1.1 collective-permute-start.8
  90.5 3.3 %collective-permute-done.6 = bf16[128,768]{1,0:T(8,128)(2,1)S(1)} collective-permute-done((bf16[128,768]{1,0:T(8,128)(2,1)S(1)}, bf16[128,768]{1,0:T(8,128)(2,1)S(1)}, u32[]{:S(2)}, u32[]{:S(2)}) %collective-permute-start.6) | collective-permute-done | bytes 196640 | tf_op jit(solution)/shard_map/ppermute | solution.py:520
  94.4 4.0 %collective-permute-done.7 = bf16[128,768]{1,0:T(8,128)(2,1)S(1)} collective-permute-done((bf16[128,768]{1,0:T(8,128)(2,1)S(1)}, bf16[128,768]{1,0:T(8,128)(2,1)S(1)}, u32[]{:S(2)}, u32[]{:S(2)}) %collective-permute-start.7) | collective-permute-done | bytes 196640 | tf_op jit(solution)/shard_map/ppermute | solution.py:520
  98.6 1.0 pad_maximum_fusion.6
  99.6 1.0 pad_maximum_fusion.5
  100.9 1.7 collective-permute-start.13
  103.5 11.6 %collective-permute-done.13 = bf16[4,160,768]{2,1,0:T(8,128)(2,1)S(1)} collective-permute-done((bf16[4,160,768]{2,1,0:T(8,128)(2,1)S(1)}, bf16[4,160,768]{2,1,0:T(8,128)(2,1)S(1)}, u32[]{:S(2)}, u32[]{:S(2)}) %collective-permute-start.13) | collective-permute-done | bytes 983072 | tf_op jit(solution)/shard_map/ppermute | solution.py:583
  115.4 1.7 collective-permute-start.14
  117.4 1.6 collective-permute-start.19
  119.0 10.5 %collective-permute-done.14 = bf16[2,160,768]{2,1,0:T(8,128)(2,1)S(1)} collective-permute-done((bf16[2,160,768]{2,1,0:T(8,128)(2,1)S(1)}, bf16[2,160,768]{2,1,0:T(8,128)(2,1)S(1)}, u32[]{:S(2)}, u32[]{:S(2)}) %collective-permute-start.14) | collective-permute-done | bytes 491552 | tf_op jit(solution)/shard_map/ppermute | solution.py:583
  129.7 2.7 %collective-permute-start.15 = (bf16[1,160,768]{2,1,0:T(8,128)(2,1)S(1)}, bf16[1,160,768]{2,1,0:T(8,128)(2,1)S(1)}, u32[]{:S(2)}, u32[]{:S(2)}) collective-permute-start(bf16[1,160,768]{2,1,0:T(8,128)(2,1)S(1)} %pad_maximum_fusion.10), channel_id=1, source_target_pairs={{0,16},{1,17},{2,18},{3,19},{4,20},{5,21},{6,22},{7,23},{8,24},{9,... | collective-permute-start | bytes 737288 | tf_op jit(solution)/shard_map/ppermute | solution.py:583
  133.2 1.7 collective-permute-start.28
  135.0 9.7 %collective-permute-done.19 = bf16[8,96,768]{2,1,0:T(8,128)(2,1)S(1)} collective-permute-done((bf16[8,96,768]{2,1,0:T(8,128)(2,1)S(1)}, bf16[8,96,768]{2,1,0:T(8,128)(2,1)S(1)}, u32[]{:S(2)}, u32[]{:S(2)}) %collective-permute-start.19) | collective-permute-done | bytes 1179680 | tf_op jit(solution)/shard_map/ppermute | solution.py:583
  145.1 1.6 collective-permute-start.16
  147.4 4.1 %collective-permute-done.16 = bf16[160,768]{1,0:T(8,128)(2,1)S(1)} collective-permute-done((bf16[160,768]{1,0:T(8,128)(2,1)S(1)}, bf16[160,768]{1,0:T(8,128)(2,1)S(1)}, u32[]{:S(2)}, u32[]{:S(2)}) %collective-permute-start.16) | collective-permute-done | bytes 245792 | tf_op jit(solution)/shard_map/ppermute | solution.py:583
  151.8 2.7 %collective-permute-start.29 = (bf16[1,192,768]{2,1,0:T(8,128)(2,1)S(1)}, bf16[1,192,768]{2,1,0:T(8,128)(2,1)S(1)}, u32[]{:S(2)}, u32[]{:S(2)}) collective-permute-start(bf16[1,192,768]{2,1,0:T(8,128)(2,1)S(1)} %fusion.10), channel_id=1, source_target_pairs={{0,16},{1,17},{2,18},{3,19},{4,20},{5,21},{6,22},{7,23},{8,24},{9,... | collective-permute-start | bytes 884744 | tf_op jit(solution)/shard_map/ppermute | solution.py:583
  155.4 4.5 %collective-permute-done.21 = bf16[4,144,768]{2,1,0:T(8,128)(2,1)S(1)} collective-permute-done((bf16[4,144,768]{2,1,0:T(8,128)(2,1)S(1)}, bf16[4,144,768]{2,1,0:T(8,128)(2,1)S(1)}, u32[]{:S(2)}, u32[]{:S(2)}) %collective-permute-start.21) | collective-permute-done | bytes 884768 | tf_op jit(solution)/shard_map/ppermute | solution.py:583
  160.1 1.6 collective-permute-start.22
  163.2 7.3 %collective-permute-done.22 = bf16[2,144,768]{2,1,0:T(8,128)(2,1)S(1)} collective-permute-done((bf16[2,144,768]{2,1,0:T(8,128)(2,1)S(1)}, bf16[2,144,768]{2,1,0:T(8,128)(2,1)S(1)}, u32[]{:S(2)}, u32[]{:S(2)}) %collective-permute-start.22) | collective-permute-done | bytes 442400 | tf_op jit(solution)/shard_map/ppermute | solution.py:583
  170.8 5.1 %collective-permute-start.23 = (bf16[1,144,768]{2,1,0:T(8,128)(2,1)S(1)}, bf16[1,144,768]{2,1,0:T(8,128)(2,1)S(1)}, u32[]{:S(2)}, u32[]{:S(2)}) collective-permute-start(bf16[1,144,768]{2,1,0:T(8,128)(2,1)S(1)} %pad_maximum_fusion.13), channel_id=1, source_target_pairs={{0,16},{1,17},{2,18},{3,19},{4,20},{5,21},{6,22},{7,23},{8,24},{9,... | collective-permute-start | bytes 663560 | tf_op jit(solution)/shard_map/ppermute | solution.py:583
  176.1 3.3 %collective-permute-start.30 = (bf16[192,768]{1,0:T(8,128)(2,1)S(1)}, bf16[192,768]{1,0:T(8,128)(2,1)S(1)}, u32[]{:S(2)}, u32[]{:S(2)}) collective-permute-start(bf16[192,768]{1,0:T(8,128)(2,1)S(1)} %fusion.7), channel_id=1, source_target_pairs={{0,2},{1,3},{2,0},{3,1},{4,6},{5,7},{6,4},{7,5},{8,10},{9,11},{10,... | collective-permute-start | bytes 884744 | tf_op jit(solution)/shard_map/ppermute | solution.py:583
  179.4 2.9 %collective-permute-done.23 = bf16[1,144,768]{2,1,0:T(8,128)(2,1)S(1)} collective-permute-done((bf16[1,144,768]{2,1,0:T(8,128)(2,1)S(1)}, bf16[1,144,768]{2,1,0:T(8,128)(2,1)S(1)}, u32[]{:S(2)}, u32[]{:S(2)}) %collective-permute-start.23) | collective-permute-done | bytes 221216 | tf_op jit(solution)/shard_map/ppermute | solution.py:583
  182.5 3.1 %collective-permute-start.24 = (bf16[144,768]{1,0:T(8,128)(2,1)S(1)}, bf16[144,768]{1,0:T(8,128)(2,1)S(1)}, u32[]{:S(2)}, u32[]{:S(2)}) collective-permute-start(bf16[144,768]{1,0:T(8,128)(2,1)S(1)} %pad_maximum_fusion.14), channel_id=1, source_target_pairs={{0,2},{1,3},{2,0},{3,1},{4,6},{5,7},{6,4},{7,5},{8,10},{9,11},{10,... | collective-permute-start | bytes 663560 | tf_op jit(solution)/shard_map/ppermute | solution.py:583
  186.4 3.2 %collective-permute-done.24 = bf16[144,768]{1,0:T(8,128)(2,1)S(1)} collective-permute-done((bf16[144,768]{1,0:T(8,128)(2,1)S(1)}, bf16[144,768]{1,0:T(8,128)(2,1)S(1)}, u32[]{:S(2)}, u32[]{:S(2)}) %collective-permute-start.24) | collective-permute-done | bytes 221216 | tf_op jit(solution)/shard_map/ppermute | solution.py:583
  189.8 1.1 fusion.6
  192.6 1.1 pad_maximum_fusion.1
  (164 shorter events, 16.4 us)
Async XLA Ops:
  0.7 8.0 %copy-start.13 = (f32[768]{0:T(1024)S(1)}, f32[768]{0:T(1024)}, u32[]{:S(2)}) copy-start(f32[768]{0:T(1024)} %param.27) | copy-start | bytes 9220
  0.7 8.0 %copy-start.14 = (f32[768]{0:T(1024)S(1)}, f32[768]{0:T(1024)}, u32[]{:S(2)}) copy-start(f32[768]{0:T(1024)} %param.28) | copy-start | bytes 9220
  0.7 8.0 %copy-start.15 = (f32[768]{0:T(1024)S(1)}, f32[768]{0:T(1024)}, u32[]{:S(2)}) copy-start(f32[768]{0:T(1024)} %param.32) | copy-start | bytes 9220
  0.7 8.0 %copy-start.16 = (f32[768]{0:T(1024)S(1)}, f32[768]{0:T(1024)}, u32[]{:S(2)}) copy-start(f32[768]{0:T(1024)} %param.33) | copy-start | bytes 9220
  0.7 8.0 %copy-start.17 = (f32[768]{0:T(1024)S(1)}, f32[768]{0:T(1024)}, u32[]{:S(2)}) copy-start(f32[768]{0:T(1024)} %param.34) | copy-start | bytes 9220
  0.7 16.7 %copy-start.3 = (bf16[768,768]{1,0:T(8,128)(2,1)S(1)}, bf16[768,768]{1,0:T(8,128)(2,1)}, u32[]{:S(2)}) copy-start(bf16[768,768]{1,0:T(8,128)(2,1)} %wq.3) | copy-start | bytes 3538948
  2.1 8.3 %collective-permute-start = (bf16[128,768]{1,0:T(8,128)(2,1)S(1)}, bf16[128,768]{1,0:T(8,128)(2,1)}, u32[]{:S(2)}, u32[]{:S(2)}) collective-permute-start(bf16[128,768]{1,0:T(8,128)(2,1)S(1)} %get-tuple-element.57), channel_id=1, source_target_pairs={{0,1},{1,0},{2,3},{3,2},{4,5},{5,4},{6,7},{7,6},{8,9},{9,8},{10,11... | collective-permute-start | bytes 589832 | tf_op jit(solution)/shard_map/ppermute | solution.py:520
  2.7 9.0 %collective-permute-start.1 = (bf16[128,768]{1,0:T(8,128)(2,1)S(1)}, bf16[128,768]{1,0:T(8,128)(2,1)}, u32[]{:S(2)}, u32[]{:S(2)}) collective-permute-start(bf16[128,768]{1,0:T(8,128)(2,1)S(1)} %get-tuple-element.58), channel_id=1, source_target_pairs={{0,2},{1,3},{2,0},{3,1},{4,6},{5,7},{6,4},{7,5},{8,10},{9,11},{10,... | collective-permute-start | bytes 589832 | tf_op jit(solution)/shard_map/ppermute | solution.py:520
  5.2 9.4 %collective-permute-start.2 = (bf16[128,768]{1,0:T(8,128)(2,1)S(1)}, bf16[128,768]{1,0:T(8,128)(2,1)S(1)}, u32[]{:S(2)}, u32[]{:S(2)}) collective-permute-start(bf16[128,768]{1,0:T(8,128)(2,1)S(1)} %get-tuple-element.59), channel_id=1, source_target_pairs={{0,3},{1,2},{2,1},{3,0},{4,7},{5,6},{6,5},{7,4},{8,11},{9,10},{10,... | collective-permute-start | bytes 589832 | tf_op jit(solution)/shard_map/ppermute | solution.py:520
  8.6 8.9 %copy-start.2 = (bf16[768,768]{1,0:T(8,128)(2,1)S(1)}, bf16[768,768]{1,0:T(8,128)(2,1)}, u32[]{:S(2)}) copy-start(bf16[768,768]{1,0:T(8,128)(2,1)} %wa.1) | copy-start | bytes 3538948
  8.9 22.4 %copy-start.1 = (bf16[768,3072]{1,0:T(8,128)(2,1)S(1)}, bf16[768,3072]{1,0:T(8,128)(2,1)}, u32[]{:S(2)}) copy-start(bf16[768,3072]{1,0:T(8,128)(2,1)} %wi.1) | copy-start | bytes 14155780
  14.7 16.5 %collective-permute-start.3 = (bf16[128,768]{1,0:T(8,128)(2,1)S(1)}, bf16[128,768]{1,0:T(8,128)(2,1)S(1)}, u32[]{:S(2)}, u32[]{:S(2)}) collective-permute-start(bf16[128,768]{1,0:T(8,128)(2,1)S(1)} %get-tuple-element.62), channel_id=1, source_target_pairs={{0,1},{1,0},{2,3},{3,2},{4,5},{5,4},{6,7},{7,6},{8,9},{9,8},{10,11... | collective-permute-start | bytes 589832 | tf_op jit(solution)/shard_map/ppermute | solution.py:520
  14.9 16.4 %collective-permute-start.4 = (bf16[128,768]{1,0:T(8,128)(2,1)S(1)}, bf16[128,768]{1,0:T(8,128)(2,1)S(1)}, u32[]{:S(2)}, u32[]{:S(2)}) collective-permute-start(bf16[128,768]{1,0:T(8,128)(2,1)S(1)} %get-tuple-element.63), channel_id=1, source_target_pairs={{0,2},{1,3},{2,0},{3,1},{4,6},{5,7},{6,4},{7,5},{8,10},{9,11},{10,... | collective-permute-start | bytes 589832 | tf_op jit(solution)/shard_map/ppermute | solution.py:520
  16.6 14.6 %collective-permute-start.5 = (bf16[128,768]{1,0:T(8,128)(2,1)S(1)}, bf16[128,768]{1,0:T(8,128)(2,1)S(1)}, u32[]{:S(2)}, u32[]{:S(2)}) collective-permute-start(bf16[128,768]{1,0:T(8,128)(2,1)S(1)} %get-tuple-element.64), channel_id=1, source_target_pairs={{0,3},{1,2},{2,1},{3,0},{4,7},{5,6},{6,5},{7,4},{8,11},{9,10},{10,... | collective-permute-start | bytes 589832 | tf_op jit(solution)/shard_map/ppermute | solution.py:520
  20.0 11.3 %copy-start = (bf16[3072,768]{1,0:T(8,128)(2,1)S(1)}, bf16[3072,768]{1,0:T(8,128)(2,1)}, u32[]{:S(2)}) copy-start(bf16[3072,768]{1,0:T(8,128)(2,1)} %refs_6_.3) | copy-start | bytes 14155780
  20.0 11.3 %copy-start.12 = (f32[3072]{0:T(1024)S(1)}, f32[3072]{0:T(1024)}, u32[]{:S(2)}) copy-start(f32[3072]{0:T(1024)} %param.30) | copy-start | bytes 36868
  56.4 7.4 %slice-start = ((s8[6291456]{0:T(1024)(128)(4,1)}), s8[4194304]{0:T(1024)(128)(4,1)S(1)}, s32[]{:S(2)}) async-start(s8[6291456]{0:T(1024)(128)(4,1)} %bitcast.217), calls=%async_computation | async-start | bytes 8388608
  56.4 7.4 %slice-start.1 = ((s8[6291456]{0:T(1024)(128)(4,1)}), s8[2097152]{0:T(1024)(128)(4,1)S(1)}, s32[]{:S(2)}) async-start(s8[6291456]{0:T(1024)(128)(4,1)} %bitcast.217), calls=%async_computation.1 | async-start | bytes 4194304
  56.4 7.4 %copy-start.8 = (f32[512,768]{1,0:T(8,128)S(1)}, f32[512,768]{1,0:T(8,128)}, u32[]{:S(2)}) copy-start(f32[512,768]{1,0:T(8,128)} %get-tuple-element.76.inv) | copy-start | bytes 4718596
  56.4 7.4 %copy-start.9 = (bf16[512,768]{1,0:T(8,128)(2,1)S(1)}, bf16[512,768]{1,0:T(8,128)(2,1)}, u32[]{:S(2)}) copy-start(bf16[512,768]{1,0:T(8,128)(2,1)} %get-tuple-element.72.q) | copy-start | bytes 2359300
  56.4 7.4 %copy-start.10 = (bf16[512,768]{1,0:T(8,128)(2,1)S(1)}, bf16[512,768]{1,0:T(8,128)(2,1)}, u32[]{:S(2)}) copy-start(bf16[512,768]{1,0:T(8,128)(2,1)} %get-tuple-element.73.k) | copy-start | bytes 2359300
  56.4 7.4 %copy-start.11 = (bf16[512,768]{1,0:T(8,128)(2,1)S(1)}, bf16[512,768]{1,0:T(8,128)(2,1)}, u32[]{:S(2)}) copy-start(bf16[512,768]{1,0:T(8,128)(2,1)} %get-tuple-element.74.v) | copy-start | bytes 2359300
  74.0 28.7 %collective-permute-start.26 = (bf16[8,192,768]{2,1,0:T(8,128)(2,1)S(1)}, bf16[8,192,768]{2,1,0:T(8,128)(2,1)S(1)}, u32[]{:S(2)}, u32[]{:S(2)}) collective-permute-start(bf16[8,192,768]{2,1,0:T(8,128)(2,1)S(1)} %bitcast.231), channel_id=1, source_target_pairs={{0,1},{1,0},{2,3},{3,2},{4,5},{5,4},{6,7},{7,6},{8,9},{9,8},{10,11... | collective-permute-start | bytes 7077896 | tf_op jit(solution)/shard_map/ppermute | solution.py:583
  74.6 25.9 %collective-permute-start.12 = (bf16[8,160,768]{2,1,0:T(8,128)(2,1)S(1)}, bf16[8,160,768]{2,1,0:T(8,128)(2,1)S(1)}, u32[]{:S(2)}, u32[]{:S(2)}) collective-permute-start(bf16[8,160,768]{2,1,0:T(8,128)(2,1)S(1)} %pad_maximum_fusion), channel_id=1, source_target_pairs={{0,1},{1,0},{2,3},{3,2},{4,5},{5,4},{6,7},{7,6},{8,9},{9,8},{10,11... | collective-permute-start | bytes 5898248 | tf_op jit(solution)/shard_map/ppermute | solution.py:583
  78.8 7.8 %collective-permute-start.10 = (bf16[128,768]{1,0:T(8,128)(2,1)S(1)}, bf16[128,768]{1,0:T(8,128)(2,1)S(1)}, u32[]{:S(2)}, u32[]{:S(2)}) collective-permute-start(bf16[128,768]{1,0:T(8,128)(2,1)S(1)} %get-tuple-element.127), channel_id=1, source_target_pairs={{0,2},{1,3},{2,0},{3,1},{4,6},{5,7},{6,4},{7,5},{8,10},{9,11},{10,... | collective-permute-start | bytes 589832 | tf_op jit(solution)/shard_map/ppermute | solution.py:520
  80.6 6.1 %collective-permute-start.11 = (bf16[128,768]{1,0:T(8,128)(2,1)S(1)}, bf16[128,768]{1,0:T(8,128)(2,1)S(1)}, u32[]{:S(2)}, u32[]{:S(2)}) collective-permute-start(bf16[128,768]{1,0:T(8,128)(2,1)S(1)} %get-tuple-element.126), channel_id=1, source_target_pairs={{0,1},{1,0},{2,3},{3,2},{4,5},{5,4},{6,7},{7,6},{8,9},{9,8},{10,11... | collective-permute-start | bytes 589832 | tf_op jit(solution)/shard_map/ppermute | solution.py:520
  80.6 8.8 %collective-permute-start.9 = (bf16[128,768]{1,0:T(8,128)(2,1)S(1)}, bf16[128,768]{1,0:T(8,128)(2,1)S(1)}, u32[]{:S(2)}, u32[]{:S(2)}) collective-permute-start(bf16[128,768]{1,0:T(8,128)(2,1)S(1)} %get-tuple-element.128), channel_id=1, source_target_pairs={{0,3},{1,2},{2,1},{3,0},{4,7},{5,6},{6,5},{7,4},{8,11},{9,10},{10,... | collective-permute-start | bytes 589832 | tf_op jit(solution)/shard_map/ppermute | solution.py:520
  86.6 7.2 %collective-permute-start.6 = (bf16[128,768]{1,0:T(8,128)(2,1)S(1)}, bf16[128,768]{1,0:T(8,128)(2,1)S(1)}, u32[]{:S(2)}, u32[]{:S(2)}) collective-permute-start(bf16[128,768]{1,0:T(8,128)(2,1)S(1)} %get-tuple-element.131), channel_id=1, source_target_pairs={{0,3},{1,2},{2,1},{3,0},{4,7},{5,6},{6,5},{7,4},{8,11},{9,10},{10,... | collective-permute-start | bytes 589832 | tf_op jit(solution)/shard_map/ppermute | solution.py:520
  86.6 11.8 %collective-permute-start.7 = (bf16[128,768]{1,0:T(8,128)(2,1)S(1)}, bf16[128,768]{1,0:T(8,128)(2,1)S(1)}, u32[]{:S(2)}, u32[]{:S(2)}) collective-permute-start(bf16[128,768]{1,0:T(8,128)(2,1)S(1)} %get-tuple-element.130), channel_id=1, source_target_pairs={{0,2},{1,3},{2,0},{3,1},{4,6},{5,7},{6,4},{7,5},{8,10},{9,11},{10,... | collective-permute-start | bytes 589832 | tf_op jit(solution)/shard_map/ppermute | solution.py:520
  89.4 9.0 %collective-permute-start.8 = (bf16[128,768]{1,0:T(8,128)(2,1)S(1)}, bf16[128,768]{1,0:T(8,128)(2,1)S(1)}, u32[]{:S(2)}, u32[]{:S(2)}) collective-permute-start(bf16[128,768]{1,0:T(8,128)(2,1)S(1)} %get-tuple-element.129), channel_id=1, source_target_pairs={{0,1},{1,0},{2,3},{3,2},{4,5},{5,4},{6,7},{7,6},{8,9},{9,8},{10,11... | collective-permute-start | bytes 589832 | tf_op jit(solution)/shard_map/ppermute | solution.py:520
  93.8 23.3 %collective-permute-start.18 = (bf16[8,192,768]{2,1,0:T(8,128)(2,1)S(1)}, bf16[8,192,768]{2,1,0:T(8,128)(2,1)S(1)}, u32[]{:S(2)}, u32[]{:S(2)}) collective-permute-start(bf16[8,192,768]{2,1,0:T(8,128)(2,1)S(1)} %bitcast.230), channel_id=1, source_target_pairs={{0,1},{1,0},{2,3},{3,2},{4,5},{5,4},{6,7},{7,6},{8,9},{9,8},{10,11... | collective-permute-start | bytes 7077896 | tf_op jit(solution)/shard_map/ppermute | solution.py:583
  98.4 4.2 %collective-permute-start.20 = (bf16[8,48,768]{2,1,0:T(8,128)(2,1)S(1)}, bf16[8,48,768]{2,1,0:T(8,128)(2,1)S(1)}, u32[]{:S(2)}, u32[]{:S(2)}) collective-permute-start(bf16[8,48,768]{2,1,0:T(8,128)(2,1)S(1)} %bitcast.232), channel_id=1, source_target_pairs={{0,1},{1,0},{2,3},{3,2},{4,5},{5,4},{6,7},{7,6},{8,9},{9,8},{10,11... | collective-permute-start | bytes 1769480 | tf_op jit(solution)/shard_map/ppermute | solution.py:583
  100.9 14.2 %collective-permute-start.13 = (bf16[4,160,768]{2,1,0:T(8,128)(2,1)S(1)}, bf16[4,160,768]{2,1,0:T(8,128)(2,1)S(1)}, u32[]{:S(2)}, u32[]{:S(2)}) collective-permute-start(bf16[4,160,768]{2,1,0:T(8,128)(2,1)S(1)} %pad_maximum_fusion.2), channel_id=1, source_target_pairs={{0,4},{1,9},{2,6},{3,11},{4,0},{5,13},{6,2},{7,15},{8,12},{9,1},{1... | collective-permute-start | bytes 2949128 | tf_op jit(solution)/shard_map/ppermute | solution.py:583
  103.0 30.0 %collective-permute-start.27 = (bf16[4,192,768]{2,1,0:T(8,128)(2,1)S(1)}, bf16[4,192,768]{2,1,0:T(8,128)(2,1)S(1)}, u32[]{:S(2)}, u32[]{:S(2)}) collective-permute-start(bf16[4,192,768]{2,1,0:T(8,128)(2,1)S(1)} %fusion), channel_id=1, source_target_pairs={{0,4},{1,9},{2,6},{3,11},{4,0},{5,13},{6,2},{7,15},{8,12},{9,1},{1... | collective-permute-start | bytes 3538952 | tf_op jit(solution)/shard_map/ppermute | solution.py:583
  115.4 14.2 %collective-permute-start.14 = (bf16[2,160,768]{2,1,0:T(8,128)(2,1)S(1)}, bf16[2,160,768]{2,1,0:T(8,128)(2,1)S(1)}, u32[]{:S(2)}, u32[]{:S(2)}) collective-permute-start(bf16[2,160,768]{2,1,0:T(8,128)(2,1)S(1)} %pad_maximum_fusion.7), channel_id=1, source_target_pairs={{0,8},{1,5},{2,10},{3,7},{4,12},{5,1},{6,14},{7,3},{8,0},{9,13},{1... | collective-permute-start | bytes 1474568 | tf_op jit(solution)/shard_map/ppermute | solution.py:583
  117.4 27.2 %collective-permute-start.19 = (bf16[8,96,768]{2,1,0:T(8,128)(2,1)S(1)}, bf16[8,96,768]{2,1,0:T(8,128)(2,1)S(1)}, u32[]{:S(2)}, u32[]{:S(2)}) collective-permute-start(bf16[8,96,768]{2,1,0:T(8,128)(2,1)S(1)} %add_convert_fusion), channel_id=1, source_target_pairs={{0,2},{1,3},{2,0},{3,1},{4,6},{5,7},{6,4},{7,5},{8,10},{9,11},{10,... | collective-permute-start | bytes 3538952 | tf_op jit(solution)/shard_map/ppermute | solution.py:583
  129.7 15.1 %collective-permute-start.15 = (bf16[1,160,768]{2,1,0:T(8,128)(2,1)S(1)}, bf16[1,160,768]{2,1,0:T(8,128)(2,1)S(1)}, u32[]{:S(2)}, u32[]{:S(2)}) collective-permute-start(bf16[1,160,768]{2,1,0:T(8,128)(2,1)S(1)} %pad_maximum_fusion.10), channel_id=1, source_target_pairs={{0,16},{1,17},{2,18},{3,19},{4,20},{5,21},{6,22},{7,23},{8,24},{9,... | collective-permute-start | bytes 737288 | tf_op jit(solution)/shard_map/ppermute | solution.py:583
  133.2 18.5 %collective-permute-start.28 = (bf16[2,192,768]{2,1,0:T(8,128)(2,1)S(1)}, bf16[2,192,768]{2,1,0:T(8,128)(2,1)S(1)}, u32[]{:S(2)}, u32[]{:S(2)}) collective-permute-start(bf16[2,192,768]{2,1,0:T(8,128)(2,1)S(1)} %fusion.3), channel_id=1, source_target_pairs={{0,8},{1,5},{2,10},{3,7},{4,12},{5,1},{6,14},{7,3},{8,0},{9,13},{1... | collective-permute-start | bytes 1769480 | tf_op jit(solution)/shard_map/ppermute | solution.py:583
  145.1 6.4 %collective-permute-start.16 = (bf16[160,768]{1,0:T(8,128)(2,1)S(1)}, bf16[160,768]{1,0:T(8,128)(2,1)S(1)}, u32[]{:S(2)}, u32[]{:S(2)}) collective-permute-start(bf16[160,768]{1,0:T(8,128)(2,1)S(1)} %pad_maximum_fusion.11), channel_id=1, source_target_pairs={{0,2},{1,3},{2,0},{3,1},{4,6},{5,7},{6,4},{7,5},{8,10},{9,11},{10,... | collective-permute-start | bytes 737288 | tf_op jit(solution)/shard_map/ppermute | solution.py:583
  146.8 13.1 %collective-permute-start.21 = (bf16[4,144,768]{2,1,0:T(8,128)(2,1)S(1)}, bf16[4,144,768]{2,1,0:T(8,128)(2,1)S(1)}, u32[]{:S(2)}, u32[]{:S(2)}) collective-permute-start(bf16[4,144,768]{2,1,0:T(8,128)(2,1)S(1)} %pad_maximum_fusion.3), channel_id=1, source_target_pairs={{0,4},{1,9},{2,6},{3,11},{4,0},{5,13},{6,2},{7,15},{8,12},{9,1},{1... | collective-permute-start | bytes 2654216 | tf_op jit(solution)/shard_map/ppermute | solution.py:583
  151.6 2.9 %collective-permute-start.17 = (bf16[160,768]{1,0:T(8,128)(2,1)S(1)}, bf16[160,768]{1,0:T(8,128)(2,1)S(1)}, u32[]{:S(2)}, u32[]{:S(2)}) collective-permute-start(bf16[160,768]{1,0:T(8,128)(2,1)S(1)} %pad_maximum_fusion.12), channel_id=1, source_target_pairs={{0,1},{1,0},{2,3},{3,2},{4,5},{5,4},{6,7},{7,6},{8,9},{9,8},{10,11... | collective-permute-start | bytes 737288 | tf_op jit(solution)/shard_map/ppermute | solution.py:583
  151.8 24.0 %collective-permute-start.29 = (bf16[1,192,768]{2,1,0:T(8,128)(2,1)S(1)}, bf16[1,192,768]{2,1,0:T(8,128)(2,1)S(1)}, u32[]{:S(2)}, u32[]{:S(2)}) collective-permute-start(bf16[1,192,768]{2,1,0:T(8,128)(2,1)S(1)} %fusion.10), channel_id=1, source_target_pairs={{0,16},{1,17},{2,18},{3,19},{4,20},{5,21},{6,22},{7,23},{8,24},{9,... | collective-permute-start | bytes 884744 | tf_op jit(solution)/shard_map/ppermute | solution.py:583
  160.1 10.5 %collective-permute-start.22 = (bf16[2,144,768]{2,1,0:T(8,128)(2,1)S(1)}, bf16[2,144,768]{2,1,0:T(8,128)(2,1)S(1)}, u32[]{:S(2)}, u32[]{:S(2)}) collective-permute-start(bf16[2,144,768]{2,1,0:T(8,128)(2,1)S(1)} %pad_maximum_fusion.8), channel_id=1, source_target_pairs={{0,8},{1,5},{2,10},{3,7},{4,12},{5,1},{6,14},{7,3},{8,0},{9,13},{1... | collective-permute-start | bytes 1327112 | tf_op jit(solution)/shard_map/ppermute | solution.py:583
  170.8 11.6 %collective-permute-start.23 = (bf16[1,144,768]{2,1,0:T(8,128)(2,1)S(1)}, bf16[1,144,768]{2,1,0:T(8,128)(2,1)S(1)}, u32[]{:S(2)}, u32[]{:S(2)}) collective-permute-start(bf16[1,144,768]{2,1,0:T(8,128)(2,1)S(1)} %pad_maximum_fusion.13), channel_id=1, source_target_pairs={{0,16},{1,17},{2,18},{3,19},{4,20},{5,21},{6,22},{7,23},{8,24},{9,... | collective-permute-start | bytes 663560 | tf_op jit(solution)/shard_map/ppermute | solution.py:583
  176.1 10.2 %collective-permute-start.30 = (bf16[192,768]{1,0:T(8,128)(2,1)S(1)}, bf16[192,768]{1,0:T(8,128)(2,1)S(1)}, u32[]{:S(2)}, u32[]{:S(2)}) collective-permute-start(bf16[192,768]{1,0:T(8,128)(2,1)S(1)} %fusion.7), channel_id=1, source_target_pairs={{0,2},{1,3},{2,0},{3,1},{4,6},{5,7},{6,4},{7,5},{8,10},{9,11},{10,... | collective-permute-start | bytes 884744 | tf_op jit(solution)/shard_map/ppermute | solution.py:583
  182.5 7.1 %collective-permute-start.24 = (bf16[144,768]{1,0:T(8,128)(2,1)S(1)}, bf16[144,768]{1,0:T(8,128)(2,1)S(1)}, u32[]{:S(2)}, u32[]{:S(2)}) collective-permute-start(bf16[144,768]{1,0:T(8,128)(2,1)S(1)} %pad_maximum_fusion.14), channel_id=1, source_target_pairs={{0,2},{1,3},{2,0},{3,1},{4,6},{5,7},{6,4},{7,5},{8,10},{9,11},{10,... | collective-permute-start | bytes 663560 | tf_op jit(solution)/shard_map/ppermute | solution.py:583
  186.3 3.4 %collective-permute-start.31 = (bf16[192,768]{1,0:T(8,128)(2,1)S(1)}, bf16[192,768]{1,0:T(8,128)(2,1)S(1)}, u32[]{:S(2)}, u32[]{:S(2)}) collective-permute-start(bf16[192,768]{1,0:T(8,128)(2,1)S(1)} %add_convert_fusion.2), channel_id=1, source_target_pairs={{0,1},{1,0},{2,3},{3,2},{4,5},{5,4},{6,7},{7,6},{8,9},{9,8},{10,11... | collective-permute-start | bytes 884744 | tf_op jit(solution)/shard_map/ppermute | solution.py:583
  189.7 1.8 collective-permute-start.25
  (4 other events, 5.4 us)

commit v3 on v2

--- a/solution.py
+++ b/solution.py
@@ -229,6 +229,7 @@
     col = lambda rows: pl.BlockSpec((rows, group), lambda g: (0, g))
     low = jax.ShapeDtypeStruct((tokens, width), BF16)
     far = pltpu.HBM((tokens, width), BF16)
+    wq, wk, wv = (pltpu.with_memory_space_constraint(w, pltpu.HBM) for w in (wq, wk, wv))
     return pl.pallas_call(
         attn_kernel,
         out_shape=(
@@ -251,7 +252,7 @@
             col(tokens), col(tokens), whole((tokens, width)), whole((tokens, 1)),
         ],
         scratch_shapes=[pltpu.VMEM((tokens, width), F32)],
-        compiler_params=pltpu.CompilerParams(vmem_limit_bytes=14 << 20),
+        compiler_params=pltpu.CompilerParams(vmem_limit_bytes=17 << 20),
         name="attention_forward",
     )(x, bias, wq, bq, wk, wv, bv, wo, bo)
 
@@ -430,14 +431,21 @@
     )(q, k, v, c, gc, inv, e)
 
 
-def weights_kernel(slots, x, dq, dk, dv, vec2, vec1, ibias, vec0, keep, send, vkeep, vsend):
+def weights_kernel(slots, x, dq, dk, dv, vec2, vec1, ibias, vec0, keep, send):
+    n_dp = keep.shape[0]
+    width = x.shape[1]
+    h = width // (2 * n_dp)
+    odd = slots[0] == 1
     xt = x[...].T
     for n, grad in enumerate((dq, dk, dv)):
-        put_units(keep, send, slots, 0, dot(xt, grad[...]), n)
-    n_dp = keep.shape[0]
-    width = x.shape[1]
+        low = dot(xt, grad[...]).astype(BF16)
+        rows = slice(n * h, (n + 1) * h)
+        for j in range(n_dp):
+            first = low[2 * j * h : (2 * j + 1) * h]
+            second = low[(2 * j + 1) * h : (2 * j + 2) * h]
+            keep[slots[1 + j], rows] = jnp.where(odd, second, first)
+            send[slots[1 + n_dp + j], rows] = jnp.where(odd, first, second)
     part = width // n_dp
-    odd = slots[0] == 1
     eight = jnp.concatenate([vec2[0:3], vec1[0:3], vec0[0:2]], 0)
 
     def two(rows):
@@ -450,25 +458,23 @@
         row = jnp.broadcast_to(row, (8, width))
         first = two(pltpu.roll(eight, (width - part * j) % width, 1))
         second = two(pltpu.roll(row, (width - start % width) % width, 1))
-        vkeep[slots[1 + j]] = jnp.where(odd, second, first)
-        vsend[slots[1 + n_dp + j]] = jnp.where(odd, first, second)
+        keep[slots[1 + j], 3 * h :] = jnp.where(odd, second, first)
+        send[slots[1 + n_dp + j], 3 * h :] = jnp.where(odd, first, second)
 
 
 def weight_gradients(n_dp, slots, x, dq, dk, dv, *vectors):
     tokens, width = x.shape
     full = whole((tokens, width))
-    shape = (n_dp, 3, width // (2 * n_dp), width)
-    tiny = (n_dp, 16, width)
+    shape = (n_dp, 3 * (width // (2 * n_dp)) + 16, width)
     units = jax.ShapeDtypeStruct(shape, BF16)
-    small = jax.ShapeDtypeStruct(tiny, BF16)
     return pl.pallas_call(
         weights_kernel,
-        out_shape=(units, units, small, small),
+        out_shape=(units, units),
         grid_spec=pltpu.PrefetchScalarGridSpec(
             num_scalar_prefetch=1,
             grid=(1,),
             in_specs=[full, full, full, full] + [whole((8, width))] * 4,
-            out_specs=[whole(shape), whole(shape), whole(tiny), whole(tiny)],
+            out_specs=[whole(shape), whole(shape)],
         ),
         compiler_params=pltpu.CompilerParams(vmem_limit_bytes=12 << 20),
         name="weight_gradients",
@@ -555,12 +561,12 @@
     for piece in pieces:
         rows = piece[cut].astype(F32)
         total = total + (rows[..., :8, :] + rows[..., 8:, :])
-    high = total.astype(BF16)
-    return jnp.concatenate([high, (total - high.astype(F32)).astype(BF16)], -2)
+    high = lax.reduce_precision(total, 8, 7)
+    return jnp.concatenate([high, total - high], -2).astype(BF16)
 
 
 class Halving:
-    def __init__(self, keep, send, n_dp, n_seq, small=()):
+    def __init__(self, keep, send, n_dp, n_seq, small=0):
         self.y_cut = False
         self.n_dp = n_dp
         self.n_seq = n_seq
@@ -570,13 +576,11 @@
         ]
         flat = lambda units: units.reshape(n_dp, -1, units.shape[-1])
         keep, send = flat(keep), flat(send)
-        rows = keep.shape[1]
         self.adders = [added]
         self.families = [[keep]]
         if small:
             self.adders.append(added_in_two)
-            self.families.append([small[0]])
-            send = jnp.concatenate([send, small[1]], 1)
+            self.families = [[keep[:, :-small]], [keep[:, -small:]]]
         self.take(self.permute(send, lambda d, s: (d, s ^ 1)))
 
     def permute(self, values, partner):
@@ -718,10 +722,10 @@
         query, key, value, context, grad_context, inverse, exps,
     )
     outer.step()
-    keep, send, *small = weight_gradients(
+    attn_units = weight_gradients(
         n_dp, slots, x, grad_query, grad_key, grad_value, vec2, vec1, ibias, vec0,
     )
-    attn = Halving(keep, send, n_dp, n_seq, small)
+    attn = Halving(*attn_units, n_dp, n_seq, small=16)
     input_low = input_gradient(
         grad_mid, grad_query, grad_key, grad_value, query_weight, key_weight, value_weight,
     )

time: 194 us -> 204 us (1.052)
  other arithmetic: 10.4 us -> 16.6 us
  Pallas kernels: 56.2 us -> 58.8 us
    convert_element_type x20, other arithmetic: 2.91 us -> 6.84 us  [added(): return total.astype(BF16)]
    ppermute x20, waiting for transfers between devices: 55.5 us -> 52.7 us  [permute(): return lax.ppermute(values, BOTH, pairs(self.n_dp, self.n_seq, partner))]
    convert_element_type x12, other arithmetic: 0.11 us -> 2.56 us  [added_in_two(): rows = piece[cut].astype(F32)]
    ppermute x12, waiting for transfers between devices: 16 us -> 18.4 us  [exchange(): lax.ppermute(blocks[k], 'seq', [(s, s ^ k) for s in range(n_seq)])]
    unnamed x43 -> x89, local copies, waits for them, and re-layouts: 6.12 us -> 7.72 us
  transfers between devices with their start and end apart: 32 -> 32, of which waited for: 16 -> 16; matrix products, arithmetic and copies ran while one was open for 9% -> 10% of each run, Pallas kernels for 7% -> 7%
where the time goes in v3:
time: 204 us
  waiting for transfers between devices  71.1 us (35%)
  Pallas kernels  58.8 us (29%)
  starting transfers between devices  40.8 us (20%)
  other arithmetic  16.6 us (8%)
  local copies, waits for them, and re-layouts  14.5 us (7%)
    ppermute x20, waiting for transfers between devices, permute(): return lax.ppermute(values, BOTH, pairs(self.n_dp, self.n_seq, partner))  52.7 us
    ppermute x20, starting transfers between devices, permute(): return lax.ppermute(values, BOTH, pairs(self.n_dp, self.n_seq, partner))  30.4 us
    ppermute x12, waiting for transfers between devices, exchange(): lax.ppermute(blocks[k], 'seq', [(s, s ^ k) for s in range(n_seq)])  18.4 us
    pallas_call x1, Pallas kernels, ffn_up(): pl.pallas_call(lambda *refs: up_kernel(ROWS, *refs), out_shape=(jax.Shape...  17.7 us
    pallas_call x1, Pallas kernels, attention_forward(): pl.pallas_call(attn_kernel, out_shape=(far, far, far, pltpu.HBM((heads, t...  12.4 us
    ppermute x12, starting transfers between devices, exchange(): lax.ppermute(blocks[k], 'seq', [(s, s ^ k) for s in range(n_seq)])  10.4 us
    unnamed x89, local copies, waits for them, and re-layouts  7.72 us
    pallas_call x1, Pallas kernels, attention_back(): pl.pallas_call(back_kernel, out_shape=(low, low, low, jax.ShapeDtypeStruc...  7.42 us
  transfers between devices with their start and end apart: 32, of which 16 were waited for; matrix products, arithmetic and copies ran while one was open for 10% of the time, Pallas kernels for 7%

profile of v3, /device:TPU:0, one launch (start us, length us, event | category | flops | bytes accessed | tf_op | source)
XLA Modules:
  0.0 203.5 jit_solution(13282187024080537343)
XLA Ops:
  0.7 1.3 dynamic-slice_bitcast_fusion.4
  2.6 2.6 %collective-permute-start.1 = (bf16[128,768]{1,0:T(8,128)(2,1)S(1)}, bf16[128,768]{1,0:T(8,128)(2,1)S(1)}, u32[]{:S(2)}, u32[]{:S(2)}) collective-permute-start(bf16[128,768]{1,0:T(8,128)(2,1)S(1)} %get-tuple-element.56), channel_id=1, source_target_pairs={{0,2},{1,3},{2,0},{3,1},{4,6},{5,7},{6,4},{7,5},{8,10},{9,11},{10,... | collective-permute-start | bytes 589832 | tf_op jit(solution)/shard_map/ppermute | solution.py:526
  5.3 1.2 dynamic_slice.33
  9.0 2.0 collective-permute-done.1
  11.0 3.7 %collective-permute-done.2 = bf16[128,768]{1,0:T(8,128)(2,1)S(1)} collective-permute-done((bf16[128,768]{1,0:T(8,128)(2,1)S(1)}, bf16[128,768]{1,0:T(8,128)(2,1)S(1)}, u32[]{:S(2)}, u32[]{:S(2)}) %collective-permute-start.2) | collective-permute-done | bytes 196640 | tf_op jit(solution)/shard_map/ppermute | solution.py:526
  14.9 1.7 collective-permute-start.4
  17.4 12.4 %attention_forward.1 = (bf16[512,768]{1,0:T(8,128)(2,1)}, bf16[512,768]{1,0:T(8,128)(2,1)}, bf16[512,768]{1,0:T(8,128)(2,1)}, bf16[12,512,512]{2,1,0:T(8,128)(2,...) custom-call(bf16[512,768]{1,0:T(8,128)(2,1)S(1)} %constant_dynamic-update, ...), custom_call_target="tpu_custom_call" | custom-call | tf_op jit(solution)/shard_map/attention_forward/pallas_call | solution.py:233
  29.9 17.7 %ffn_up.1 = (bf16[512,768]{1,0:T(8,128)(2,1)S(1)}, bf16[512,3072]{1,0:T(8,128)(2,1)S(1)}, f32[512,768]{1,0:T(8,128)S(1)}, f32[8,768]{1,0:T(8,128)S(1)}, bf16[8,1...) custom-call(s32[18]{0:T(128)S(1)} %pad_add_fusion.refs_0_.slots, ...), custom_call_target="tpu_custom_call" | custom-call | tf_op jit(solution)/shard_map/ffn_up/pallas_call | solution.py:129
  47.7 1.4 copy-done.31
  49.1 7.3 %ffn_down.1 = (bf16[512,3072]{1,0:T(8,128)(2,1)S(1)}, f32[8,768]{1,0:T(8,128)S(1)}, bf16[8,4,48,768]{3,2,1,0:T(8,128)(2,1)S(1)}, bf16[8,4,48,768]{3,2,1,0:T(8,128)(2,1)S(1)}) custom-call(s32[18]{0:T(128)S(1)} %pad_add_fusion.refs_0_.slots, f32[512,768]{1,0:T(8,128)S(1)} %get-tuple-element.64.refs_1_.gpre, bf16[512,3072]{1,0:T(8,128)(2,1)S(1)} %get-tuple-element.65.refs_2_, ...), custom_call_target="tpu_custom_call" | custom-call | tf_op jit(solution)/shard_map/ffn_down/pallas_call | solution.py:289
  56.4 7.4 %middle.1 = (f32[512,768]{1,0:T(8,128)S(1)}, bf16[512,768]{1,0:T(8,128)(2,1)S(1)}, f32[8,768]{1,0:T(8,128)S(1)}, bf16[8,1,48,768]{3,2,1,0:T(8,128)(2,1)S(1)}, bf16[8,1,48,768]{3,2,1,0:T(8,128)(2,1)S(1)}) custom-call(s32[18]{0:T(128)S(1)} %pad_add_fusion.refs_0_.slots, f32[512,768]{1,0:T(8,128)S(1)} %get-tuple-element.64.refs_1_.gpre, ...), custom_call_target="tpu_custom_call" | custom-call | tf_op jit(solution)/shard_map/middle/pallas_call | solution.py:358
  64.0 7.4 %attention_back.1 = (bf16[512,768]{1,0:T(8,128)(2,1)S(1)}, bf16[512,768]{1,0:T(8,128)(2,1)S(1)}, bf16[512,768]{1,0:T(8,128)(2,1)S(1)}, f32[8,768]{1,0:T(8,128)S(1)}) custom-call(bf16[512,768]{1,0:T(8,128)(2,1)S(1)} %copy-done.21, bf16[512,768]{1,0:T(8,128)(2,1)S(1)} %copy-done.22, bf16[512,768]{1,0:T(8,128)(2,1)S(1)} %copy-done.23, ...), custom_call_target="tpu_custom_call" | custom-call | tf_op jit(solution)/shard_map/attention_back/pallas_call | solution.py:422
  71.5 4.0 %weight_gradients.1 = (bf16[8,160,768]{2,1,0:T(8,128)(2,1)S(1)}, bf16[8,160,768]{2,1,0:T(8,128)(2,1)}) custom-call(s32[18]{0:T(128)S(1)} %pad_add_fusion.refs_0_.slots, bf16[512,768]{1,0:T(8,128)(2,1)S(1)} %constant_dynamic-update-slice_fusion.x, bf16[512,768]{1,0:T(8,128)(2,1)S(1)} %get-tuple-element.76.dq, bf16[512,768]{1,0:T(8,128)(2,1)S(1)} %get-tuple-element.77.dk, ...), custom_call_target="tpu_custom_call" | custom-call | tf_op jit(solution)/shard_map/weight_gradients/pallas_call | solution.py:470
  75.5 1.3 copy-done.16
  77.2 1.1 copy-done.7
  78.3 1.1 copy-done.9
  79.4 1.1 copy-done.11
  80.6 1.4 copy-done.20
  82.0 2.6 %input_gradient.1 = bf16[512,768]{1,0:T(8,128)(2,1)S(1)} custom-call(f32[512,768]{1,0:T(8,128)S(1)} %copy-done.20, bf16[512,768]{1,0:T(8,128)(2,1)S(1)} %copy-done.7, bf16[512,768]{1,0:T(8,128)(2,1)S(1)} %copy-done.9, bf16[512,768]{1,0:T(8,128)(2,1)S(1)} %copy-done.11, bf16[768,768]{1,0:T(8,128)(2,1)S(1)} %copy-done.3, bf16[768,768]{1,0:T(8,128)(2,1)S(1)} %copy-done.4, ...), custom_call_target="tpu_custom_call" | custom-call | tf_op jit(solution)/shard_map/input_gradient/pallas_call | solution.py:496
  84.7 1.8 collective-permute-start.10
  86.9 1.4 collective-permute-start.6
  88.4 4.2 %collective-permute-done.10 = bf16[128,768]{1,0:T(8,128)(2,1)S(1)} collective-permute-done((bf16[128,768]{1,0:T(8,128)(2,1)S(1)}, bf16[128,768]{1,0:T(8,128)(2,1)S(1)}, u32[]{:S(2)}, u32[]{:S(2)}) %collective-permute-start.10) | collective-permute-done | bytes 196640 | tf_op jit(solution)/shard_map/ppermute | solution.py:526
  92.5 1.7 collective-permute-start.7
  94.2 1.7 collective-permute-done.9
  96.8 3.3 %collective-permute-done.6 = bf16[128,768]{1,0:T(8,128)(2,1)S(1)} collective-permute-done((bf16[128,768]{1,0:T(8,128)(2,1)S(1)}, bf16[128,768]{1,0:T(8,128)(2,1)S(1)}, u32[]{:S(2)}, u32[]{:S(2)}) %collective-permute-start.6) | collective-permute-done | bytes 196640 | tf_op jit(solution)/shard_map/ppermute | solution.py:526
  100.8 3.5 %collective-permute-done.7 = bf16[128,768]{1,0:T(8,128)(2,1)S(1)} collective-permute-done((bf16[128,768]{1,0:T(8,128)(2,1)S(1)}, bf16[128,768]{1,0:T(8,128)(2,1)S(1)}, u32[]{:S(2)}, u32[]{:S(2)}) %collective-permute-start.7) | collective-permute-done | bytes 196640 | tf_op jit(solution)/shard_map/ppermute | solution.py:526
  107.3 1.4 add_convert_fusion.1
  108.9 1.7 collective-permute-start.13
  113.4 9.6 %collective-permute-done.13 = bf16[4,160,768]{2,1,0:T(8,128)(2,1)S(1)} collective-permute-done((bf16[4,160,768]{2,1,0:T(8,128)(2,1)S(1)}, bf16[4,160,768]{2,1,0:T(8,128)(2,1)S(1)}, u32[]{:S(2)}, u32[]{:S(2)}) %collective-permute-start.13) | collective-permute-done | bytes 983072 | tf_op jit(solution)/shard_map/ppermute | solution.py:587
  123.1 1.2 add_convert_fusion.3
  124.3 1.8 collective-permute-start.14
  126.4 1.6 collective-permute-start.19
  128.0 10.5 %collective-permute-done.14 = bf16[2,160,768]{2,1,0:T(8,128)(2,1)S(1)} collective-permute-done((bf16[2,160,768]{2,1,0:T(8,128)(2,1)S(1)}, bf16[2,160,768]{2,1,0:T(8,128)(2,1)S(1)}, u32[]{:S(2)}, u32[]{:S(2)}) %collective-permute-start.14) | collective-permute-done | bytes 491552 | tf_op jit(solution)/shard_map/ppermute | solution.py:587
  139.6 2.8 %collective-permute-start.15 = (bf16[1,160,768]{2,1,0:T(8,128)(2,1)S(1)}, bf16[1,160,768]{2,1,0:T(8,128)(2,1)S(1)}, u32[]{:S(2)}, u32[]{:S(2)}) collective-permute-start(bf16[1,160,768]{2,1,0:T(8,128)(2,1)S(1)} %pad_maximum_fusion.9), channel_id=1, source_target_pairs={{0,16},{1,17},{2,18},{3,19},{4,20},{5,21},{6,22},{7,23},{8,24},{9,... | collective-permute-start | bytes 737288 | tf_op jit(solution)/shard_map/ppermute | solution.py:587
  142.6 1.6 collective-permute-start.28
  144.2 9.4 %collective-permute-done.19 = bf16[8,96,768]{2,1,0:T(8,128)(2,1)S(1)} collective-permute-done((bf16[8,96,768]{2,1,0:T(8,128)(2,1)S(1)}, bf16[8,96,768]{2,1,0:T(8,128)(2,1)S(1)}, u32[]{:S(2)}, u32[]{:S(2)}) %collective-permute-start.19) | collective-permute-done | bytes 1179680 | tf_op jit(solution)/shard_map/ppermute | solution.py:587
  155.0 1.6 collective-permute-start.16
  157.3 4.1 %collective-permute-done.16 = bf16[160,768]{1,0:T(8,128)(2,1)S(1)} collective-permute-done((bf16[160,768]{1,0:T(8,128)(2,1)S(1)}, bf16[160,768]{1,0:T(8,128)(2,1)S(1)}, u32[]{:S(2)}, u32[]{:S(2)}) %collective-permute-start.16) | collective-permute-done | bytes 245792 | tf_op jit(solution)/shard_map/ppermute | solution.py:587
  161.7 2.6 %collective-permute-start.29 = (bf16[1,192,768]{2,1,0:T(8,128)(2,1)S(1)}, bf16[1,192,768]{2,1,0:T(8,128)(2,1)S(1)}, u32[]{:S(2)}, u32[]{:S(2)}) collective-permute-start(bf16[1,192,768]{2,1,0:T(8,128)(2,1)S(1)} %fusion.7), channel_id=1, source_target_pairs={{0,16},{1,17},{2,18},{3,19},{4,20},{5,21},{6,22},{7,23},{8,24},{9,... | collective-permute-start | bytes 884744 | tf_op jit(solution)/shard_map/ppermute | solution.py:587
  165.2 4.5 %collective-permute-done.21 = bf16[4,144,768]{2,1,0:T(8,128)(2,1)S(1)} collective-permute-done((bf16[4,144,768]{2,1,0:T(8,128)(2,1)S(1)}, bf16[4,144,768]{2,1,0:T(8,128)(2,1)S(1)}, u32[]{:S(2)}, u32[]{:S(2)}) %collective-permute-start.21) | collective-permute-done | bytes 884768 | tf_op jit(solution)/shard_map/ppermute | solution.py:587
  170.0 1.6 collective-permute-start.22
  173.1 7.4 %collective-permute-done.22 = bf16[2,144,768]{2,1,0:T(8,128)(2,1)S(1)} collective-permute-done((bf16[2,144,768]{2,1,0:T(8,128)(2,1)S(1)}, bf16[2,144,768]{2,1,0:T(8,128)(2,1)S(1)}, u32[]{:S(2)}, u32[]{:S(2)}) %collective-permute-start.22) | collective-permute-done | bytes 442400 | tf_op jit(solution)/shard_map/ppermute | solution.py:587
  180.7 5.0 %collective-permute-start.23 = (bf16[1,144,768]{2,1,0:T(8,128)(2,1)S(1)}, bf16[1,144,768]{2,1,0:T(8,128)(2,1)S(1)}, u32[]{:S(2)}, u32[]{:S(2)}) collective-permute-start(bf16[1,144,768]{2,1,0:T(8,128)(2,1)S(1)} %pad_maximum_fusion.12), channel_id=1, source_target_pairs={{0,16},{1,17},{2,18},{3,19},{4,20},{5,21},{6,22},{7,23},{8,24},{9,... | collective-permute-start | bytes 663560 | tf_op jit(solution)/shard_map/ppermute | solution.py:587
  185.9 3.3 %collective-permute-start.30 = (bf16[192,768]{1,0:T(8,128)(2,1)S(1)}, bf16[192,768]{1,0:T(8,128)(2,1)S(1)}, u32[]{:S(2)}, u32[]{:S(2)}) collective-permute-start(bf16[192,768]{1,0:T(8,128)(2,1)S(1)} %fusion.4), channel_id=1, source_target_pairs={{0,2},{1,3},{2,0},{3,1},{4,6},{5,7},{6,4},{7,5},{8,10},{9,11},{10,... | collective-permute-start | bytes 884744 | tf_op jit(solution)/shard_map/ppermute | solution.py:587
  189.2 2.9 %collective-permute-done.23 = bf16[1,144,768]{2,1,0:T(8,128)(2,1)S(1)} collective-permute-done((bf16[1,144,768]{2,1,0:T(8,128)(2,1)S(1)}, bf16[1,144,768]{2,1,0:T(8,128)(2,1)S(1)}, u32[]{:S(2)}, u32[]{:S(2)}) %collective-permute-start.23) | collective-permute-done | bytes 221216 | tf_op jit(solution)/shard_map/ppermute | solution.py:587
  192.4 3.2 %collective-permute-start.24 = (bf16[144,768]{1,0:T(8,128)(2,1)S(1)}, bf16[144,768]{1,0:T(8,128)(2,1)S(1)}, u32[]{:S(2)}, u32[]{:S(2)}) collective-permute-start(bf16[144,768]{1,0:T(8,128)(2,1)S(1)} %pad_maximum_fusion.13), channel_id=1, source_target_pairs={{0,2},{1,3},{2,0},{3,1},{4,6},{5,7},{6,4},{7,5},{8,10},{9,11},{10,... | collective-permute-start | bytes 663560 | tf_op jit(solution)/shard_map/ppermute | solution.py:587
  196.2 3.2 %collective-permute-done.24 = bf16[144,768]{1,0:T(8,128)(2,1)S(1)} collective-permute-done((bf16[144,768]{1,0:T(8,128)(2,1)S(1)}, bf16[144,768]{1,0:T(8,128)(2,1)S(1)}, u32[]{:S(2)}, u32[]{:S(2)}) %collective-permute-start.24) | collective-permute-done | bytes 221216 | tf_op jit(solution)/shard_map/ppermute | solution.py:587
  202.4 1.1 pad_maximum_fusion
  (210 shorter events, 23.4 us)
Async XLA Ops:
  0.7 7.9 %copy-start.36 = (f32[768]{0:T(1024)S(1)}, f32[768]{0:T(1024)}, u32[]{:S(2)}) copy-start(f32[768]{0:T(1024)} %param.27) | copy-start | bytes 9220
  0.7 7.9 %copy-start.37 = (f32[768]{0:T(1024)S(1)}, f32[768]{0:T(1024)}, u32[]{:S(2)}) copy-start(f32[768]{0:T(1024)} %param.28) | copy-start | bytes 9220
  0.7 7.9 %copy-start.38 = (f32[768]{0:T(1024)S(1)}, f32[768]{0:T(1024)}, u32[]{:S(2)}) copy-start(f32[768]{0:T(1024)} %param.32) | copy-start | bytes 9220
  0.7 7.9 %copy-start.39 = (f32[768]{0:T(1024)S(1)}, f32[768]{0:T(1024)}, u32[]{:S(2)}) copy-start(f32[768]{0:T(1024)} %param.33) | copy-start | bytes 9220
  0.7 7.9 %copy-start.40 = (f32[768]{0:T(1024)S(1)}, f32[768]{0:T(1024)}, u32[]{:S(2)}) copy-start(f32[768]{0:T(1024)} %param.34) | copy-start | bytes 9220
  0.7 8.1 %copy-start.35 = (bf16[4,128,768]{2,1,0:T(8,128)(2,1)S(1)}, bf16[4,128,768]{2,1,0:T(8,128)(2,1)}, u32[]{:S(2)}) copy-start(bf16[4,128,768]{2,1,0:T(8,128)(2,1)} %param.35) | copy-start | bytes 2359300
  2.1 6.9 %collective-permute-start = (bf16[128,768]{1,0:T(8,128)(2,1)S(1)}, bf16[128,768]{1,0:T(8,128)(2,1)S(1)}, u32[]{:S(2)}, u32[]{:S(2)}) collective-permute-start(bf16[128,768]{1,0:T(8,128)(2,1)S(1)} %get-tuple-element.55), channel_id=1, source_target_pairs={{0,1},{1,0},{2,3},{3,2},{4,5},{5,4},{6,7},{7,6},{8,9},{9,8},{10,11... | collective-permute-start | bytes 589832 | tf_op jit(solution)/shard_map/ppermute | solution.py:526
  2.6 8.3 %collective-permute-start.1 = (bf16[128,768]{1,0:T(8,128)(2,1)S(1)}, bf16[128,768]{1,0:T(8,128)(2,1)S(1)}, u32[]{:S(2)}, u32[]{:S(2)}) collective-permute-start(bf16[128,768]{1,0:T(8,128)(2,1)S(1)} %get-tuple-element.56), channel_id=1, source_target_pairs={{0,2},{1,3},{2,0},{3,1},{4,6},{5,7},{6,4},{7,5},{8,10},{9,11},{10,... | collective-permute-start | bytes 589832 | tf_op jit(solution)/shard_map/ppermute | solution.py:526
  5.2 9.4 %collective-permute-start.2 = (bf16[128,768]{1,0:T(8,128)(2,1)S(1)}, bf16[128,768]{1,0:T(8,128)(2,1)S(1)}, u32[]{:S(2)}, u32[]{:S(2)}) collective-permute-start(bf16[128,768]{1,0:T(8,128)(2,1)S(1)} %get-tuple-element.57), channel_id=1, source_target_pairs={{0,3},{1,2},{2,1},{3,0},{4,7},{5,6},{6,5},{7,4},{8,11},{9,10},{10,... | collective-permute-start | bytes 589832 | tf_op jit(solution)/shard_map/ppermute | solution.py:526
  8.5 8.9 %copy-start.2 = (bf16[768,768]{1,0:T(8,128)(2,1)S(1)}, bf16[768,768]{1,0:T(8,128)(2,1)}, u32[]{:S(2)}) copy-start(bf16[768,768]{1,0:T(8,128)(2,1)} %wa.1) | copy-start | bytes 3538948
  8.8 21.1 %copy-start.1 = (bf16[768,3072]{1,0:T(8,128)(2,1)S(1)}, bf16[768,3072]{1,0:T(8,128)(2,1)}, u32[]{:S(2)}) copy-start(bf16[768,3072]{1,0:T(8,128)(2,1)} %wi.1) | copy-start | bytes 14155780
  14.7 15.1 %collective-permute-start.3 = (bf16[128,768]{1,0:T(8,128)(2,1)S(1)}, bf16[128,768]{1,0:T(8,128)(2,1)S(1)}, u32[]{:S(2)}, u32[]{:S(2)}) collective-permute-start(bf16[128,768]{1,0:T(8,128)(2,1)S(1)} %get-tuple-element.60), channel_id=1, source_target_pairs={{0,1},{1,0},{2,3},{3,2},{4,5},{5,4},{6,7},{7,6},{8,9},{9,8},{10,11... | collective-permute-start | bytes 589832 | tf_op jit(solution)/shard_map/ppermute | solution.py:526
  14.9 14.9 %collective-permute-start.4 = (bf16[128,768]{1,0:T(8,128)(2,1)S(1)}, bf16[128,768]{1,0:T(8,128)(2,1)S(1)}, u32[]{:S(2)}, u32[]{:S(2)}) collective-permute-start(bf16[128,768]{1,0:T(8,128)(2,1)S(1)} %get-tuple-element.61), channel_id=1, source_target_pairs={{0,2},{1,3},{2,0},{3,1},{4,6},{5,7},{6,4},{7,5},{8,10},{9,11},{10,... | collective-permute-start | bytes 589832 | tf_op jit(solution)/shard_map/ppermute | solution.py:526
  16.6 13.2 %collective-permute-start.5 = (bf16[128,768]{1,0:T(8,128)(2,1)S(1)}, bf16[128,768]{1,0:T(8,128)(2,1)S(1)}, u32[]{:S(2)}, u32[]{:S(2)}) collective-permute-start(bf16[128,768]{1,0:T(8,128)(2,1)S(1)} %get-tuple-element.62), channel_id=1, source_target_pairs={{0,3},{1,2},{2,1},{3,0},{4,7},{5,6},{6,5},{7,4},{8,11},{9,10},{10,... | collective-permute-start | bytes 589832 | tf_op jit(solution)/shard_map/ppermute | solution.py:526
  17.4 12.5 %copy-start = (bf16[3072,768]{1,0:T(8,128)(2,1)S(1)}, bf16[3072,768]{1,0:T(8,128)(2,1)}, u32[]{:S(2)}) copy-start(bf16[3072,768]{1,0:T(8,128)(2,1)} %refs_6_.3) | copy-start | bytes 14155780
  17.4 12.5 %copy-start.28 = (f32[3072]{0:T(1024)S(1)}, f32[3072]{0:T(1024)}, u32[]{:S(2)}) copy-start(f32[3072]{0:T(1024)} %param.30) | copy-start | bytes 36868
  63.8 7.5 %copy-start.19 = (f32[512,768]{1,0:T(8,128)}, f32[512,768]{1,0:T(8,128)S(1)}, u32[]{:S(2)}) copy-start(f32[512,768]{1,0:T(8,128)S(1)} %get-tuple-element.69.gmid) | copy-start | bytes 4718596
  63.9 13.2 %copy-start.5 = (bf16[768,768]{1,0:T(8,128)(2,1)S(1)}, bf16[768,768]{1,0:T(8,128)(2,1)}, u32[]{:S(2)}) copy-start(bf16[768,768]{1,0:T(8,128)(2,1)} %wv.3) | copy-start | bytes 3538948
  76.8 29.7 %collective-permute-start.12 = (bf16[8,160,768]{2,1,0:T(8,128)(2,1)}, bf16[8,160,768]{2,1,0:T(8,128)(2,1)}, u32[]{:S(2)}, u32[]{:S(2)}) collective-permute-start(bf16[8,160,768]{2,1,0:T(8,128)(2,1)} %get-tuple-element.84), channel_id=1, source_target_pairs={{0,1},{1,0},{2,3},{3,2},{4,5},{5,4},{6,7},{7,6},{8,9},{9,8},{10,11... | collective-permute-start | bytes 5898248 | tf_op jit(solution)/shard_map/ppermute | solution.py:587
  82.0 14.0 %copy-start.32 = (bf16[8,1,192,768]{3,2,1,0:T(8,128)(2,1)S(1)}, bf16[8,1,192,768]{3,2,1,0:T(8,128)(2,1)}, u32[]{:S(2)}) copy-start(bf16[8,1,192,768]{3,2,1,0:T(8,128)(2,1)} %copy-done.31) | copy-start | bytes 7077892
  82.0 18.2 %copy-start.30 = (bf16[8,4,48,768]{3,2,1,0:T(8,128)(2,1)S(1)}, bf16[8,4,48,768]{3,2,1,0:T(8,128)(2,1)}, u32[]{:S(2)}) copy-start(bf16[8,4,48,768]{3,2,1,0:T(8,128)(2,1)} %copy-done.29) | copy-start | bytes 7077892
  84.6 19.7 %copy-start.34 = (bf16[8,1,48,768]{3,2,1,0:T(8,128)(2,1)S(1)}, bf16[8,1,48,768]{3,2,1,0:T(8,128)(2,1)}, u32[]{:S(2)}) copy-start(bf16[8,1,48,768]{3,2,1,0:T(8,128)(2,1)} %copy-done.33) | copy-start | bytes 1769476
  84.7 7.8 %collective-permute-start.10 = (bf16[128,768]{1,0:T(8,128)(2,1)S(1)}, bf16[128,768]{1,0:T(8,128)(2,1)S(1)}, u32[]{:S(2)}, u32[]{:S(2)}) collective-permute-start(bf16[128,768]{1,0:T(8,128)(2,1)S(1)} %get-tuple-element.123), channel_id=1, source_target_pairs={{0,2},{1,3},{2,0},{3,1},{4,6},{5,7},{6,4},{7,5},{8,10},{9,11},{10,... | collective-permute-start | bytes 589832 | tf_op jit(solution)/shard_map/ppermute | solution.py:526
  86.5 7.8 %collective-permute-start.11 = (bf16[128,768]{1,0:T(8,128)(2,1)S(1)}, bf16[128,768]{1,0:T(8,128)(2,1)S(1)}, u32[]{:S(2)}, u32[]{:S(2)}) collective-permute-start(bf16[128,768]{1,0:T(8,128)(2,1)S(1)} %get-tuple-element.122), channel_id=1, source_target_pairs={{0,1},{1,0},{2,3},{3,2},{4,5},{5,4},{6,7},{7,6},{8,9},{9,8},{10,11... | collective-permute-start | bytes 589832 | tf_op jit(solution)/shard_map/ppermute | solution.py:526
  86.5 9.5 %collective-permute-start.9 = (bf16[128,768]{1,0:T(8,128)(2,1)S(1)}, bf16[128,768]{1,0:T(8,128)(2,1)S(1)}, u32[]{:S(2)}, u32[]{:S(2)}) collective-permute-start(bf16[128,768]{1,0:T(8,128)(2,1)S(1)} %get-tuple-element.124), channel_id=1, source_target_pairs={{0,3},{1,2},{2,1},{3,0},{4,7},{5,6},{6,5},{7,4},{8,11},{9,10},{10,... | collective-permute-start | bytes 589832 | tf_op jit(solution)/shard_map/ppermute | solution.py:526
  86.9 13.2 %collective-permute-start.6 = (bf16[128,768]{1,0:T(8,128)(2,1)S(1)}, bf16[128,768]{1,0:T(8,128)(2,1)S(1)}, u32[]{:S(2)}, u32[]{:S(2)}) collective-permute-start(bf16[128,768]{1,0:T(8,128)(2,1)S(1)} %get-tuple-element.127), channel_id=1, source_target_pairs={{0,3},{1,2},{2,1},{3,0},{4,7},{5,6},{6,5},{7,4},{8,11},{9,10},{10,... | collective-permute-start | bytes 589832 | tf_op jit(solution)/shard_map/ppermute | solution.py:526
  92.5 11.8 %collective-permute-start.7 = (bf16[128,768]{1,0:T(8,128)(2,1)S(1)}, bf16[128,768]{1,0:T(8,128)(2,1)S(1)}, u32[]{:S(2)}, u32[]{:S(2)}) collective-permute-start(bf16[128,768]{1,0:T(8,128)(2,1)S(1)} %get-tuple-element.126), channel_id=1, source_target_pairs={{0,2},{1,3},{2,0},{3,1},{4,6},{5,7},{6,4},{7,5},{8,10},{9,11},{10,... | collective-permute-start | bytes 589832 | tf_op jit(solution)/shard_map/ppermute | solution.py:526
  94.2 10.1 %collective-permute-start.8 = (bf16[128,768]{1,0:T(8,128)(2,1)S(1)}, bf16[128,768]{1,0:T(8,128)(2,1)S(1)}, u32[]{:S(2)}, u32[]{:S(2)}) collective-permute-start(bf16[128,768]{1,0:T(8,128)(2,1)S(1)} %get-tuple-element.125), channel_id=1, source_target_pairs={{0,1},{1,0},{2,3},{3,2},{4,5},{5,4},{6,7},{7,6},{8,9},{9,8},{10,11... | collective-permute-start | bytes 589832 | tf_op jit(solution)/shard_map/ppermute | solution.py:526
  96.0 16.2 %collective-permute-start.26 = (bf16[8,192,768]{2,1,0:T(8,128)(2,1)S(1)}, bf16[8,192,768]{2,1,0:T(8,128)(2,1)S(1)}, u32[]{:S(2)}, u32[]{:S(2)}) collective-permute-start(bf16[8,192,768]{2,1,0:T(8,128)(2,1)S(1)} %bitcast.200), channel_id=1, source_target_pairs={{0,1},{1,0},{2,3},{3,2},{4,5},{5,4},{6,7},{7,6},{8,9},{9,8},{10,11... | collective-permute-start | bytes 7077896 | tf_op jit(solution)/shard_map/ppermute | solution.py:587
  100.2 25.9 %collective-permute-start.18 = (bf16[8,192,768]{2,1,0:T(8,128)(2,1)S(1)}, bf16[8,192,768]{2,1,0:T(8,128)(2,1)S(1)}, u32[]{:S(2)}, u32[]{:S(2)}) collective-permute-start(bf16[8,192,768]{2,1,0:T(8,128)(2,1)S(1)} %bitcast.199), channel_id=1, source_target_pairs={{0,1},{1,0},{2,3},{3,2},{4,5},{5,4},{6,7},{7,6},{8,9},{9,8},{10,11... | collective-permute-start | bytes 7077896 | tf_op jit(solution)/shard_map/ppermute | solution.py:587
  104.3 6.2 %collective-permute-start.20 = (bf16[8,48,768]{2,1,0:T(8,128)(2,1)S(1)}, bf16[8,48,768]{2,1,0:T(8,128)(2,1)S(1)}, u32[]{:S(2)}, u32[]{:S(2)}) collective-permute-start(bf16[8,48,768]{2,1,0:T(8,128)(2,1)S(1)} %bitcast.201), channel_id=1, source_target_pairs={{0,1},{1,0},{2,3},{3,2},{4,5},{5,4},{6,7},{7,6},{8,9},{9,8},{10,11... | collective-permute-start | bytes 1769480 | tf_op jit(solution)/shard_map/ppermute | solution.py:587
  108.9 14.2 %collective-permute-start.13 = (bf16[4,160,768]{2,1,0:T(8,128)(2,1)S(1)}, bf16[4,160,768]{2,1,0:T(8,128)(2,1)S(1)}, u32[]{:S(2)}, u32[]{:S(2)}) collective-permute-start(bf16[4,160,768]{2,1,0:T(8,128)(2,1)S(1)} %pad_maximum_fusion.1), channel_id=1, source_target_pairs={{0,4},{1,9},{2,6},{3,11},{4,0},{5,13},{6,2},{7,15},{8,12},{9,1},{1... | collective-permute-start | bytes 2949128 | tf_op jit(solution)/shard_map/ppermute | solution.py:587
  112.5 13.6 %copy-start.15 = (bf16[8,4,48,768]{3,2,1,0:T(8,128)(2,1)S(1)}, bf16[8,4,48,768]{3,2,1,0:T(8,128)(2,1)}, u32[]{:S(2)}) copy-start(bf16[8,4,48,768]{3,2,1,0:T(8,128)(2,1)} %copy-done.14) | copy-start | bytes 7077892
  112.5 29.9 %collective-permute-start.27 = (bf16[4,192,768]{2,1,0:T(8,128)(2,1)S(1)}, bf16[4,192,768]{2,1,0:T(8,128)(2,1)S(1)}, u32[]{:S(2)}, u32[]{:S(2)}) collective-permute-start(bf16[4,192,768]{2,1,0:T(8,128)(2,1)S(1)} %fusion), channel_id=1, source_target_pairs={{0,4},{1,9},{2,6},{3,11},{4,0},{5,13},{6,2},{7,15},{8,12},{9,1},{1... | collective-permute-start | bytes 3538952 | tf_op jit(solution)/shard_map/ppermute | solution.py:587
  124.3 14.2 %collective-permute-start.14 = (bf16[2,160,768]{2,1,0:T(8,128)(2,1)S(1)}, bf16[2,160,768]{2,1,0:T(8,128)(2,1)S(1)}, u32[]{:S(2)}, u32[]{:S(2)}) collective-permute-start(bf16[2,160,768]{2,1,0:T(8,128)(2,1)S(1)} %pad_maximum_fusion.6), channel_id=1, source_target_pairs={{0,8},{1,5},{2,10},{3,7},{4,12},{5,1},{6,14},{7,3},{8,0},{9,13},{1... | collective-permute-start | bytes 1474568 | tf_op jit(solution)/shard_map/ppermute | solution.py:587
  126.4 27.2 %collective-permute-start.19 = (bf16[8,96,768]{2,1,0:T(8,128)(2,1)S(1)}, bf16[8,96,768]{2,1,0:T(8,128)(2,1)S(1)}, u32[]{:S(2)}, u32[]{:S(2)}) collective-permute-start(bf16[8,96,768]{2,1,0:T(8,128)(2,1)S(1)} %add_convert_fusion), channel_id=1, source_target_pairs={{0,2},{1,3},{2,0},{3,1},{4,6},{5,7},{6,4},{7,5},{8,10},{9,11},{10,... | collective-permute-start | bytes 3538952 | tf_op jit(solution)/shard_map/ppermute | solution.py:587
  139.6 14.2 %collective-permute-start.15 = (bf16[1,160,768]{2,1,0:T(8,128)(2,1)S(1)}, bf16[1,160,768]{2,1,0:T(8,128)(2,1)S(1)}, u32[]{:S(2)}, u32[]{:S(2)}) collective-permute-start(bf16[1,160,768]{2,1,0:T(8,128)(2,1)S(1)} %pad_maximum_fusion.9), channel_id=1, source_target_pairs={{0,16},{1,17},{2,18},{3,19},{4,20},{5,21},{6,22},{7,23},{8,24},{9,... | collective-permute-start | bytes 737288 | tf_op jit(solution)/shard_map/ppermute | solution.py:587
  142.6 19.0 %collective-permute-start.28 = (bf16[2,192,768]{2,1,0:T(8,128)(2,1)S(1)}, bf16[2,192,768]{2,1,0:T(8,128)(2,1)S(1)}, u32[]{:S(2)}, u32[]{:S(2)}) collective-permute-start(bf16[2,192,768]{2,1,0:T(8,128)(2,1)S(1)} %fusion.2), channel_id=1, source_target_pairs={{0,8},{1,5},{2,10},{3,7},{4,12},{5,1},{6,14},{7,3},{8,0},{9,13},{1... | collective-permute-start | bytes 1769480 | tf_op jit(solution)/shard_map/ppermute | solution.py:587
  155.0 6.4 %collective-permute-start.16 = (bf16[160,768]{1,0:T(8,128)(2,1)S(1)}, bf16[160,768]{1,0:T(8,128)(2,1)S(1)}, u32[]{:S(2)}, u32[]{:S(2)}) collective-permute-start(bf16[160,768]{1,0:T(8,128)(2,1)S(1)} %pad_maximum_fusion.10), channel_id=1, source_target_pairs={{0,2},{1,3},{2,0},{3,1},{4,6},{5,7},{6,4},{7,5},{8,10},{9,11},{10,... | collective-permute-start | bytes 737288 | tf_op jit(solution)/shard_map/ppermute | solution.py:587
  156.6 13.1 %collective-permute-start.21 = (bf16[4,144,768]{2,1,0:T(8,128)(2,1)S(1)}, bf16[4,144,768]{2,1,0:T(8,128)(2,1)S(1)}, u32[]{:S(2)}, u32[]{:S(2)}) collective-permute-start(bf16[4,144,768]{2,1,0:T(8,128)(2,1)S(1)} %pad_maximum_fusion.2), channel_id=1, source_target_pairs={{0,4},{1,9},{2,6},{3,11},{4,0},{5,13},{6,2},{7,15},{8,12},{9,1},{1... | collective-permute-start | bytes 2654216 | tf_op jit(solution)/shard_map/ppermute | solution.py:587
  161.5 2.9 %collective-permute-start.17 = (bf16[160,768]{1,0:T(8,128)(2,1)S(1)}, bf16[160,768]{1,0:T(8,128)(2,1)S(1)}, u32[]{:S(2)}, u32[]{:S(2)}) collective-permute-start(bf16[160,768]{1,0:T(8,128)(2,1)S(1)} %pad_maximum_fusion.11), channel_id=1, source_target_pairs={{0,1},{1,0},{2,3},{3,2},{4,5},{5,4},{6,7},{7,6},{8,9},{9,8},{10,11... | collective-permute-start | bytes 737288 | tf_op jit(solution)/shard_map/ppermute | solution.py:587
  161.7 24.0 %collective-permute-start.29 = (bf16[1,192,768]{2,1,0:T(8,128)(2,1)S(1)}, bf16[1,192,768]{2,1,0:T(8,128)(2,1)S(1)}, u32[]{:S(2)}, u32[]{:S(2)}) collective-permute-start(bf16[1,192,768]{2,1,0:T(8,128)(2,1)S(1)} %fusion.7), channel_id=1, source_target_pairs={{0,16},{1,17},{2,18},{3,19},{4,20},{5,21},{6,22},{7,23},{8,24},{9,... | collective-permute-start | bytes 884744 | tf_op jit(solution)/shard_map/ppermute | solution.py:587
  170.0 10.5 %collective-permute-start.22 = (bf16[2,144,768]{2,1,0:T(8,128)(2,1)S(1)}, bf16[2,144,768]{2,1,0:T(8,128)(2,1)S(1)}, u32[]{:S(2)}, u32[]{:S(2)}) collective-permute-start(bf16[2,144,768]{2,1,0:T(8,128)(2,1)S(1)} %pad_maximum_fusion.7), channel_id=1, source_target_pairs={{0,8},{1,5},{2,10},{3,7},{4,12},{5,1},{6,14},{7,3},{8,0},{9,13},{1... | collective-permute-start | bytes 1327112 | tf_op jit(solution)/shard_map/ppermute | solution.py:587
  180.7 11.5 %collective-permute-start.23 = (bf16[1,144,768]{2,1,0:T(8,128)(2,1)S(1)}, bf16[1,144,768]{2,1,0:T(8,128)(2,1)S(1)}, u32[]{:S(2)}, u32[]{:S(2)}) collective-permute-start(bf16[1,144,768]{2,1,0:T(8,128)(2,1)S(1)} %pad_maximum_fusion.12), channel_id=1, source_target_pairs={{0,16},{1,17},{2,18},{3,19},{4,20},{5,21},{6,22},{7,23},{8,24},{9,... | collective-permute-start | bytes 663560 | tf_op jit(solution)/shard_map/ppermute | solution.py:587
  185.9 10.2 %collective-permute-start.30 = (bf16[192,768]{1,0:T(8,128)(2,1)S(1)}, bf16[192,768]{1,0:T(8,128)(2,1)S(1)}, u32[]{:S(2)}, u32[]{:S(2)}) collective-permute-start(bf16[192,768]{1,0:T(8,128)(2,1)S(1)} %fusion.4), channel_id=1, source_target_pairs={{0,2},{1,3},{2,0},{3,1},{4,6},{5,7},{6,4},{7,5},{8,10},{9,11},{10,... | collective-permute-start | bytes 884744 | tf_op jit(solution)/shard_map/ppermute | solution.py:587
  192.4 7.1 %collective-permute-start.24 = (bf16[144,768]{1,0:T(8,128)(2,1)S(1)}, bf16[144,768]{1,0:T(8,128)(2,1)S(1)}, u32[]{:S(2)}, u32[]{:S(2)}) collective-permute-start(bf16[144,768]{1,0:T(8,128)(2,1)S(1)} %pad_maximum_fusion.13), channel_id=1, source_target_pairs={{0,2},{1,3},{2,0},{3,1},{4,6},{5,7},{6,4},{7,5},{8,10},{9,11},{10,... | collective-permute-start | bytes 663560 | tf_op jit(solution)/shard_map/ppermute | solution.py:587
  196.2 3.4 %collective-permute-start.31 = (bf16[192,768]{1,0:T(8,128)(2,1)S(1)}, bf16[192,768]{1,0:T(8,128)(2,1)S(1)}, u32[]{:S(2)}, u32[]{:S(2)}) collective-permute-start(bf16[192,768]{1,0:T(8,128)(2,1)S(1)} %add_convert_fusion.4), channel_id=1, source_target_pairs={{0,1},{1,0},{2,3},{3,2},{4,5},{5,4},{6,7},{7,6},{8,9},{9,8},{10,11... | collective-permute-start | bytes 884744 | tf_op jit(solution)/shard_map/ppermute | solution.py:587
  199.5 1.8 collective-permute-start.25
  (27 other events, 137.0 us)
